TPU v7x, 256 devices: a whole 4x4x8 slice. The times are simulated.
256 devices in a mesh: dp: 4 (over z_lo), expert: 64 (over x, y, z_hi, core).
Axes of the slice: x: 4, y: 4, z: 8 (z_hi: 2, z_lo: 4; z = z_hi * 4 + z_lo), core: 2. Of those that a mesh axis runs over, the one named last changes fastest.
Arguments:
- tokens: bfloat16 [2, 4096, 4096], P(None, ('dp', 'expert')), may hold values from -6 to 6
- expert_ids: int32 [2, 4096, 8], P(None, ('dp', 'expert')), may hold values from 0 to 63, all different within a row; in each aligned block of 16 rows (0 to 15, 16 to 31, ..., all dimensions but the last counted through in order) at most 3 rows name the same one
- gate_probs: float32 [2, 4096, 8], P(None, ('dp', 'expert')), may hold values from 0.1 to 1
- gate_up: bfloat16 [64, 2, 768, 4096], P('expert', None, 'dp'), may hold values from -0.09375 to 0.09375
- down_proj: bfloat16 [64, 768, 4096], P('expert', 'dp'), may hold values from -0.21875 to 0.21875
- pairs: int32 [8, 2], replicated, may hold values from 0 to 63, as said below
Outputs:
- moe_out: bfloat16 [2, 4096, 4096], P(None, ('dp', 'expert'))
- placed_gate_up: bfloat16 [64, 2, 768, 4096], P('expert', None, 'dp')
- placed_down: bfloat16 [64, 768, 4096], P('expert', 'dp')
Inputs may be any that keep to these rules, and one draw needn't show every extreme that they name: `expert_ids`: in each step, the 16 rows of one device name one expert at most 3 times. `pairs`: each row is (j, j + 32) with j below 32; no slot stands in two rows.
All inputs are finite; a program needn't handle non-finite values.
Results may differ from a plain program's by a relative error of at most 0.012.
Values may be sent and summed in bfloat16 or wider, within the bound.
No kernel may reach another device: no remote copies, remote signals or barrier semaphores. Data moves between devices by JAX's collectives and lax.ppermute only.
A program may use at most 128 MiB of HBM per device.

v0:
```python
import jax
import jax.numpy as jnp
from jax import lax
from jax.experimental import pallas as pl
from jax.experimental.pallas import tpu as pltpu
from jax.sharding import Mesh, PartitionSpec as P


F32 = jnp.float32
BF16 = jnp.bfloat16
CAP = 3
CHUNK = 1024
META = 128
TILE = 256
PLANE = ("x", "y", "c")


def over_tiles(rows, body):
    def wrapped(m, carry):
        body(pl.ds(pl.multiple_of(m * TILE, TILE), TILE))
        return carry

    lax.fori_loop(0, rows // TILE, wrapped, 0)


def up_first_kernel(x_ref, gu_a, gu_b, acc):
    step = pl.program_id(0)
    weights = jnp.concatenate([gu_a[0, 0], gu_b[0, 0], gu_a[0, 1], gu_b[0, 1]], axis=0)

    def body(at):
        part = lax.dot_general(
            x_ref[at, :], weights, (((1,), (1,)), ((), ())), preferred_element_type=F32
        )

        @pl.when(step == 0)
        def _():
            acc[at, :] = part

        @pl.when(step > 0)
        def _():
            acc[at, :] += part

    over_tiles(x_ref.shape[0], body)


def up_last_kernel(n_in, x_ref, gu_a, gu_b, start, hid, acc):
    step = pl.program_id(0)
    units = hid.shape[1]
    weights = jnp.concatenate([gu_a[0, 0], gu_b[0, 0], gu_a[0, 1], gu_b[0, 1]], axis=0)

    def body(at):
        part = lax.dot_general(
            x_ref[at, :], weights, (((1,), (1,)), ((), ())), preferred_element_type=F32
        )

        @pl.when(step == 0)
        def _():
            acc[at, :] = start[at, :] + part

        @pl.when(step > 0)
        def _():
            acc[at, :] += part

        @pl.when(step == n_in - 1)
        def _():
            gate = acc[at, :units]
            hid[at, :] = (gate / (1.0 + jnp.exp(-gate)) * acc[at, units:]).astype(BF16)

    over_tiles(x_ref.shape[0], body)


def up(x, gu_a, gu_b, at_col, start=None):
    rows, depth = x.shape
    units = gu_a.shape[2]
    n_in = depth // CHUNK
    base = at_col // CHUNK
    gu_spec = pl.BlockSpec((1, 2, units, CHUNK), lambda i: (0, 0, 0, base + i))
    specs = [pl.BlockSpec((rows, CHUNK), lambda i: (0, i)), gu_spec, gu_spec]
    cost = pl.CostEstimate(
        flops=2 * rows * depth * units * 4,
        bytes_accessed=2 * rows * depth + 8 * units * depth + 16 * rows * units,
        transcendentals=0,
    )
    wide = pl.BlockSpec((rows, 4 * units), lambda i: (0, 0))
    if start is None:
        return pl.pallas_call(
            up_first_kernel,
            grid=(n_in,),
            in_specs=specs,
            out_specs=wide,
            out_shape=jax.ShapeDtypeStruct((rows, 4 * units), F32),
            cost_estimate=cost,
            name="up_first",
        )(x, gu_a, gu_b)
    return pl.pallas_call(
        lambda *refs: up_last_kernel(n_in, *refs),
        grid=(n_in,),
        in_specs=specs + [wide],
        out_specs=pl.BlockSpec((rows, 2 * units), lambda i: (0, 0)),
        out_shape=jax.ShapeDtypeStruct((rows, 2 * units), BF16),
        scratch_shapes=[pltpu.VMEM((rows, 4 * units), F32)],
        cost_estimate=cost,
        name="up_last",
    )(x, gu_a, gu_b, start)


def down_kernel(hid_a, hid_b, w0, w1, w2, w3, out_ref):
    weights = jnp.concatenate([w0[...], w1[...], w2[...], w3[...]], axis=0)

    def body(at):
        hidden = jnp.concatenate([hid_a[at, :], hid_b[at, :]], axis=1)
        out_ref[at, :] = jnp.dot(hidden, weights, preferred_element_type=F32).astype(BF16)

    over_tiles(hid_a.shape[0], body)


def down(hid_a, hid_b, pieces):
    rows, units = hid_a.shape
    shard, depth = pieces[0].shape
    hid_spec = pl.BlockSpec((rows, units), lambda i: (0, 0))
    w_spec = pl.BlockSpec((shard, CHUNK), lambda i: (0, i))
    return pl.pallas_call(
        down_kernel,
        grid=(depth // CHUNK,),
        in_specs=[hid_spec, hid_spec] + [w_spec] * 4,
        out_specs=pl.BlockSpec((rows, CHUNK), lambda i: (0, i)),
        out_shape=jax.ShapeDtypeStruct((rows, depth), BF16),
        cost_estimate=pl.CostEstimate(
            flops=2 * rows * depth * units * 2,
            bytes_accessed=2 * rows * depth + 8 * shard * depth + 4 * rows * units,
            transcendentals=0,
        ),
        name="down",
    )(hid_a, hid_b, *pieces)


def swap(value, axes):
    count = 2 ** len(axes)
    return lax.ppermute(value, axes, [(i, i ^ (count - 1)) for i in range(count)])


def column(own):
    return jnp.concatenate(
        [own, swap(own, ("h",)), swap(own, ("qh",)), swap(own, ("qh", "h"))], axis=0
    )


def tables(meta, rows, tops, plane, q_high, experts, slots):
    total = meta.shape[0]
    per = slots // experts
    ids = meta[:, :tops]
    e_pos = lax.iota(jnp.int32, experts)
    e_num = (((e_pos >> 1) * 2 + plane) * 2 + (e_pos & 1)).astype(F32)
    hit = ids[:, :, None] == e_num
    named = jnp.any(hit, axis=1)
    g_high = jnp.sum(jnp.where(hit, meta[:, tops : 2 * tops, None], 0.0), axis=1).astype(BF16)
    g_low = jnp.sum(jnp.where(hit, meta[:, 2 * tops : 3 * tops, None], 0.0), axis=1).astype(BF16)
    t_row = lax.broadcasted_iota(jnp.int32, (total, total), 0)
    t_col = lax.broadcasted_iota(jnp.int32, (total, total), 1)
    earlier = ((t_row // rows == t_col // rows) & (t_col < t_row)).astype(BF16)
    rank = jnp.dot(earlier, named.astype(BF16), preferred_element_type=F32)
    place = jnp.where(named, rank, -1.0).astype(BF16)
    spread = (
        lax.broadcasted_iota(jnp.int32, (experts, slots), 0)
        == lax.broadcasted_iota(jnp.int32, (experts, slots), 1) // per
    ).astype(BF16)
    wide = jnp.dot(
        jnp.concatenate([place, g_high, g_low], axis=0), spread, preferred_element_type=F32
    )
    n_col = lax.broadcasted_iota(jnp.int32, (total, slots), 1) % per
    t_blk = lax.broadcasted_iota(jnp.int32, (total, slots), 0) // rows
    t_blk = t_blk ^ (q_high * (total // rows // 2))
    chosen = (n_col // CAP == t_blk) & (wide[:total] == (n_col % CAP).astype(F32))
    mix = jnp.concatenate(
        [
            jnp.where(chosen, wide[total : 2 * total], 0.0),
            jnp.where(chosen, wide[2 * total :], 0.0),
        ],
        axis=0,
    )
    return chosen.astype(BF16), mix.astype(BF16)


def pack(pick, held):
    return lax.dot_general(
        pick, held, (((0,), (0,)), ((), ())), preferred_element_type=F32
    ).astype(BF16)


def across(value, experts):
    slots, depth = value.shape
    return lax.all_to_all(
        value.reshape(experts, slots // experts, depth), PLANE, 0, 0, tiled=True
    ).reshape(slots, depth)


def local(tokens, expert_ids, gate_probs, gate_up, down_proj, pairs):
    steps, rows, depth = tokens.shape
    tops = expert_ids.shape[2]
    half = depth // 2
    plane = lax.axis_index("h")
    q_high = lax.axis_index("qh")
    slot = (
        (lax.axis_index("x") * 4 + lax.axis_index("y")) * 2 + plane
    ) * 2 + lax.axis_index("c")
    own = steps * rows
    experts = 32
    slots = experts * 4 * steps * CAP

    flat = tokens.reshape(own, depth)
    gates = gate_probs.reshape(own, tops)
    high = lax.reduce_precision(gates, 8, 7)
    low = gates - high
    first = jnp.concatenate(
        [
            flat[:, :half],
            expert_ids.reshape(own, tops).astype(BF16),
            high.astype(BF16),
            low.astype(BF16),
            jnp.zeros((own, META - 3 * tops), BF16),
        ],
        axis=1,
    )
    across_x = [(i, i ^ 2) for i in range(4)]
    got_dn = lax.ppermute(down_proj, ("x",), across_x)
    held0 = column(first)
    held1 = column(flat[:, half:])
    gu_b = swap(gate_up, ("ql",))
    mine = lax.dynamic_slice_in_dim(down_proj[0], q_high * half, half, axis=1)
    theirs = lax.dynamic_slice_in_dim(down_proj[0], (1 - q_high) * half, half, axis=1)
    pieces = [
        mine,
        swap(mine, ("ql",)),
        swap(theirs, ("qh",)),
        swap(theirs, ("qh", "ql")),
    ]

    pick, mix = tables(
        held0[:, half:].astype(F32), rows, tops, plane, q_high, experts, slots
    )
    packed0 = pack(pick, held0[:, :half])
    x0 = across(packed0, experts)
    packed1 = pack(pick, held1)
    x1 = across(packed1, experts)
    start = up(x0, gate_up, gu_b, 0)
    hidden = up(x1, gate_up, gu_b, half, start)
    hidden_b = swap(hidden, ("qh",))
    got_gu = lax.ppermute(gate_up, ("x",), across_x)
    made = down(hidden, hidden_b, pieces)
    back = across(made, experts)
    both = jnp.dot(mix, back, preferred_element_type=F32)
    mixed = both[: 4 * own] + both[4 * own :]
    parts = mixed.reshape(4, own, half)
    sent = parts[1:].astype(BF16)
    near = parts[0] + swap(sent[0], ("h",)).astype(F32)
    far = swap(sent[1], ("qh",)).astype(F32) + swap(sent[2], ("qh", "h")).astype(F32)
    low_half = q_high == 0
    out = jnp.concatenate(
        [jnp.where(low_half, near, far), jnp.where(low_half, far, near)], axis=1
    )
    moving = jnp.any(pairs == slot)
    return (
        out.astype(BF16).reshape(steps, rows, depth),
        jnp.where(moving, got_gu, gate_up),
        jnp.where(moving, got_dn, down_proj),
    )


def solution(mesh):
    fine = Mesh(mesh.devices.reshape(2, 2, 4, 4, 2, 2), ("qh", "ql", "x", "y", "h", "c"))
    dp = ("qh", "ql")
    ex = ("x", "y", "h", "c")
    return jax.shard_map(
        local,
        mesh=fine,
        in_specs=(
            P(None, dp + ex, None),
            P(None, dp + ex, None),
            P(None, dp + ex, None),
            P(ex, None, dp, None),
            P(ex, dp, None),
            P(),
        ),
        out_specs=(
            P(None, dp + ex, None),
            P(ex, None, dp, None),
            P(ex, dp, None),
        ),
        check_vma=False,
    )
```

profile of v0, /device:TPU:65, one launch (start us, length us, event | category | flops | bytes accessed | tf_op | source)
XLA Modules:
  0.0 384.8 jit_solution(15502066479939294330)
XLA Ops:
  0.6 1.6 fusion.59
  4.1 5.2 %collective-permute-start = (bf16[32,2176]{1,0:T(8,128)(2,1)S(1)}, bf16[32,2176]{1,0:T(8,128)(2,1)S(1)}, u32[]{:S(2)}, u32[]{:S(2)}) collective-permute-start(bf16[32,2176]{1,0:T(8,128)(2,1)S(1)} %concatenate.25), channel_id=1, source_target_pairs={{0,2},{2,0},{1,3},{3,1},{4,6},{6,4},{5,7},{7,5},{8,10},{10,8},{9,1... | collective-permute-start | bytes 417800 | tf_op jit(solution)/shard_map/ppermute | solution.py:139
  10.6 5.5 %collective-permute-done = bf16[32,2176]{1,0:T(8,128)(2,1)S(1)} collective-permute-done((bf16[32,2176]{1,0:T(8,128)(2,1)S(1)}, bf16[32,2176]{1,0:T(8,128)(2,1)S(1)}, u32[]{:S(2)}, u32[]{:S(2)}) %collective-permute-start) | collective-permute-done | bytes 139296 | tf_op jit(solution)/shard_map/ppermute | solution.py:139
  16.1 4.9 %collective-permute-done.1 = bf16[32,2176]{1,0:T(8,128)(2,1)S(1)} collective-permute-done((bf16[32,2176]{1,0:T(8,128)(2,1)S(1)}, bf16[32,2176]{1,0:T(8,128)(2,1)S(1)}, u32[]{:S(2)}, u32[]{:S(2)}) %collective-permute-start.1) | collective-permute-done | bytes 139296 | tf_op jit(solution)/shard_map/ppermute | solution.py:139
  24.7 2.7 convolution_convert_fusion
  27.5 8.4 %all-to-all-start.1 = ((bf16[32,24,2048]{2,1,0:T(8,128)(2,1)}), bf16[32,24,2048]{2,1,0:T(8,128)(2,1)}, u32[]{:S(2)}, u32[]{:S(2)}) async-start(bf16[32,24,2048]{2,1,0:T(8,128)(2,1)} %bitcast.21), calls=%async_computation.1 | async-start | bytes 6291456 | tf_op jit(solution)/shard_map/all_to_all | solution.py:192
  37.0 3.7 collective-permute-start.3
  40.7 1.6 collective-permute-start.4
  42.6 73.7 %collective-permute-done.3 = bf16[32,2048]{1,0:T(8,128)(2,1)S(1)} collective-permute-done((bf16[32,2048]{1,0:T(8,128)(2,1)}, bf16[32,2048]{1,0:T(8,128)(2,1)S(1)}, u32[]{:S(2)}, u32[]{:S(2)}) %collective-permute-start.3) | collective-permute-done | bytes 131104 | tf_op jit(solution)/shard_map/ppermute | solution.py:139
  116.3 3.6 convolution_convert_fusion.1
  119.9 9.3 %all-to-all-start = ((bf16[32,24,2048]{2,1,0:T(8,128)(2,1)}), bf16[32,24,2048]{2,1,0:T(8,128)(2,1)}, u32[]{:S(2)}, u32[]{:S(2)}) async-start(bf16[32,24,2048]{2,1,0:T(8,128)(2,1)} %bitcast.20), calls=%async_computation | async-start | bytes 6291456 | tf_op jit(solution)/shard_map/all_to_all | solution.py:192
  129.2 2.8 dynamic-slice_bitcast_fusion
  132.4 3.6 collective-permute-start.9
  136.0 7.5 %up_first.1.refs_3_ = f32[768,768]{1,0:T(8,128)} custom-call(bf16[768,2048]{1,0:T(8,128)(2,1)} %bitcast.5.x_ref, bf16[1,2,192,4096]{3,2,1,0:T(8,128)(2,1)} %refs_1_.1, bf16[1,2,192,4096]{3,2,1,0:T(8,128)(2,1)} %collective-permute-done.6.gu_b.refs_2_), custom_call_target="tpu_custom_call" | custom-call | flops 2415919104 | bytes 8650752 | tf_op jit(solution)/shard_map/up_first/pallas_call | solution.py:86
  143.5 25.5 %all-to-all-done = bf16[32,24,2048]{2,1,0:T(8,128)(2,1)} async-done(((bf16[32,24,2048]{2,1,0:T(8,128)(2,1)}), bf16[32,24,2048]{2,1,0:T(8,128)(2,1)}, u32[]{:S(2)}, u32[]{:S(2)}) %all-to-all-start) | async-done | bytes 3145760 | tf_op jit(solution)/shard_map/all_to_all | solution.py:192
  169.0 8.5 %up_last.1.hid_a = bf16[768,384]{1,0:T(8,128)(2,1)} custom-call(bf16[768,2048]{1,0:T(8,128)(2,1)} %bitcast.3.refs_0_, bf16[1,2,192,4096]{3,2,1,0:T(8,128)(2,1)} %refs_1_.1, bf16[1,2,192,4096]{3,2,1,0:T(8,128)(2,1)} %collective-permute-done.6.gu_b.refs_2_, f32[768,768]{1,0:T(8,128)} %up_first.1.refs_3_), custom_call_target="tpu_custom_call" | custom-call | flops 2415919104 | bytes 8650752 | tf_op jit(solution)/shard_map/up_last/pallas_call | solution.py:95
  177.5 2.6 collective-permute-start.7
  180.2 4.6 %collective-permute-done.10.w3 = bf16[192,2048]{1,0:T(8,128)(2,1)} collective-permute-done((bf16[192,2048]{1,0:T(8,128)(2,1)}, bf16[192,2048]{1,0:T(8,128)(2,1)}, u32[]{:S(2)}, u32[]{:S(2)}) %collective-permute-start.10) | collective-permute-done | bytes 786464 | tf_op jit(solution)/shard_map/ppermute | solution.py:139
  184.8 2.4 collective-permute-done.8.w1
  187.3 25.2 %collective-permute-done.9.w2 = bf16[192,2048]{1,0:T(8,128)(2,1)} collective-permute-done((bf16[192,2048]{1,0:T(8,128)(2,1)}, bf16[192,2048]{1,0:T(8,128)(2,1)}, u32[]{:S(2)}, u32[]{:S(2)}) %collective-permute-start.9) | collective-permute-done | bytes 786464 | tf_op jit(solution)/shard_map/ppermute | solution.py:139
  212.5 12.6 %collective-permute-done.7.hid_b = bf16[768,384]{1,0:T(8,128)(2,1)S(1)} collective-permute-done((bf16[768,384]{1,0:T(8,128)(2,1)}, bf16[768,384]{1,0:T(8,128)(2,1)S(1)}, u32[]{:S(2)}, u32[]{:S(2)}) %collective-permute-start.7) | collective-permute-done | bytes 589856 | tf_op jit(solution)/shard_map/ppermute | solution.py:139
  225.9 6.7 %down.1 = bf16[768,2048]{1,0:T(8,128)(2,1)} custom-call(bf16[768,384]{1,0:T(8,128)(2,1)} %up_last.1.hid_a, bf16[768,384]{1,0:T(8,128)(2,1)} %copy-done.4, bf16[192,2048]{1,0:T(8,128)(2,1)} %get-tuple-element.10.w0, bf16[192,2048]{1,0:T(8,128)(2,1)} %collective-permute-done.8.w1, bf16[192,2048]{1,0:T(8,128)(2,1)} %collective-permute-done.9.w2, ...), custom_call_target="tpu_custom_call" | custom-call | flops 2415919104 | bytes 7471104 | tf_op jit(solution)/shard_map/down/pallas_call | solution.py:122
  232.7 8.5 %all-to-all-start.2 = ((bf16[32,24,2048]{2,1,0:T(8,128)(2,1)}), bf16[32,24,2048]{2,1,0:T(8,128)(2,1)}, u32[]{:S(2)}, u32[]{:S(2)}) async-start(bf16[32,24,2048]{2,1,0:T(8,128)(2,1)} %bitcast.22), calls=%async_computation.2 | async-start | bytes 6291456 | tf_op jit(solution)/shard_map/all_to_all | solution.py:192
  241.2 3.0 collective-permute-start.15
  244.9 1.7 fusion.17
  246.6 67.4 %collective-permute-done.15 = bf16[1,192,4096]{2,1,0:T(8,128)(2,1)} collective-permute-done((bf16[1,192,4096]{2,1,0:T(8,128)(2,1)}, bf16[1,192,4096]{2,1,0:T(8,128)(2,1)}, u32[]{:S(2)}, u32[]{:S(2)}) %collective-permute-start.15) | collective-permute-done | bytes 1572896 | tf_op jit(solution)/shard_map/ppermute | solution.py:225
  314.0 3.3 broadcast_select_fusion.1
  317.3 3.0 fusion.19
  320.5 4.3 %collective-permute-start.11 = (bf16[32,2048]{1,0:T(8,128)(2,1)S(1)}, bf16[32,2048]{1,0:T(8,128)(2,1)S(1)}, u32[]{:S(2)}, u32[]{:S(2)}) collective-permute-start(bf16[32,2048]{1,0:T(8,128)(2,1)S(1)} %get-tuple-element.13), channel_id=1, source_target_pairs={{0,2},{2,0},{1,3},{3,1},{4,6},{6,4},{5,7},{7,5},{8,10},{10,8},{9,1... | collective-permute-start | bytes 393224 | tf_op jit(solution)/shard_map/ppermute | solution.py:139
  324.8 3.0 collective-permute-start.12
  327.8 53.6 %collective-permute-done.14 = bf16[1,2,192,4096]{3,2,1,0:T(8,128)(2,1)} collective-permute-done((bf16[1,2,192,4096]{3,2,1,0:T(8,128)(2,1)S(1)}, bf16[1,2,192,4096]{3,2,1,0:T(8,128)(2,1)}, u32[]{:S(2)}, u32[]{:S(2)}) %collective-permute-start.14) | collective-permute-done | bytes 3145760 | tf_op jit(solution)/shard_map/ppermute | solution.py:248
  381.5 2.6 broadcast_select_fusion
  (58 shorter events, 11.1 us)
Async XLA Ops:
  4.1 12.0 %collective-permute-start = (bf16[32,2176]{1,0:T(8,128)(2,1)S(1)}, bf16[32,2176]{1,0:T(8,128)(2,1)S(1)}, u32[]{:S(2)}, u32[]{:S(2)}) collective-permute-start(bf16[32,2176]{1,0:T(8,128)(2,1)S(1)} %concatenate.25), channel_id=1, source_target_pairs={{0,2},{2,0},{1,3},{3,1},{4,6},{6,4},{5,7},{7,5},{8,10},{10,8},{9,1... | collective-permute-start | bytes 417800 | tf_op jit(solution)/shard_map/ppermute | solution.py:139
  9.3 11.7 %collective-permute-start.1 = (bf16[32,2176]{1,0:T(8,128)(2,1)S(1)}, bf16[32,2176]{1,0:T(8,128)(2,1)S(1)}, u32[]{:S(2)}, u32[]{:S(2)}) collective-permute-start(bf16[32,2176]{1,0:T(8,128)(2,1)S(1)} %concatenate.25), channel_id=1, source_target_pairs={{0,128},{128,0},{1,129},{129,1},{2,130},{130,2},{3,131},{131,3},{4... | collective-permute-start | bytes 417800 | tf_op jit(solution)/shard_map/ppermute | solution.py:139
  10.5 11.9 %collective-permute-start.2 = (bf16[32,2176]{1,0:T(8,128)(2,1)S(1)}, bf16[32,2176]{1,0:T(8,128)(2,1)S(1)}, u32[]{:S(2)}, u32[]{:S(2)}) collective-permute-start(bf16[32,2176]{1,0:T(8,128)(2,1)S(1)} %concatenate.25), channel_id=1, source_target_pairs={{0,130},{2,128},{128,2},{130,0},{1,131},{3,129},{129,3},{131,1},{4... | collective-permute-start | bytes 417800 | tf_op jit(solution)/shard_map/ppermute | solution.py:139
  23.5 1.0 copy-start.2
  27.5 8.4 %copy-start = (bf16[1,2,192,4096]{3,2,1,0:T(8,128)(2,1)S(1)}, bf16[1,2,192,4096]{3,2,1,0:T(8,128)(2,1)}, u32[]{:S(2)}) copy-start(bf16[1,2,192,4096]{3,2,1,0:T(8,128)(2,1)} %refs_1_.1) | copy-start | bytes 9437188
  27.5 92.4 %all-to-all-start.1 = ((bf16[32,24,2048]{2,1,0:T(8,128)(2,1)}), bf16[32,24,2048]{2,1,0:T(8,128)(2,1)}, u32[]{:S(2)}, u32[]{:S(2)}) async-start(bf16[32,24,2048]{2,1,0:T(8,128)(2,1)} %bitcast.21), calls=%async_computation.1 | async-start | bytes 6291456 | tf_op jit(solution)/shard_map/all_to_all | solution.py:192
  35.9 100.1 %collective-permute-start.6 = (bf16[1,2,192,4096]{3,2,1,0:T(8,128)(2,1)S(1)}, bf16[1,2,192,4096]{3,2,1,0:T(8,128)(2,1)}, u32[]{:S(2)}, u32[]{:S(2)}) collective-permute-start(bf16[1,2,192,4096]{3,2,1,0:T(8,128)(2,1)S(1)} %copy-done), channel_id=1, source_target_pairs={{0,64},{64,0},{1,65},{65,1},{2,66},{66,2},{3,67},{67,3},{4,68},{68... | collective-permute-start | bytes 9437192 | tf_op jit(solution)/shard_map/ppermute | solution.py:139
  37.0 79.3 %collective-permute-start.3 = (bf16[32,2048]{1,0:T(8,128)(2,1)}, bf16[32,2048]{1,0:T(8,128)(2,1)S(1)}, u32[]{:S(2)}, u32[]{:S(2)}) collective-permute-start(bf16[32,2048]{1,0:T(8,128)(2,1)} %get-tuple-element.16), channel_id=1, source_target_pairs={{0,2},{2,0},{1,3},{3,1},{4,6},{6,4},{5,7},{7,5},{8,10},{10,8},{9,1... | collective-permute-start | bytes 393224 | tf_op jit(solution)/shard_map/ppermute | solution.py:139
  40.7 75.6 %collective-permute-start.4 = (bf16[32,2048]{1,0:T(8,128)(2,1)}, bf16[32,2048]{1,0:T(8,128)(2,1)S(1)}, u32[]{:S(2)}, u32[]{:S(2)}) collective-permute-start(bf16[32,2048]{1,0:T(8,128)(2,1)} %get-tuple-element.16), channel_id=1, source_target_pairs={{0,128},{128,0},{1,129},{129,1},{2,130},{130,2},{3,131},{131,3},{4... | collective-permute-start | bytes 393224 | tf_op jit(solution)/shard_map/ppermute | solution.py:139
  42.3 74.0 %collective-permute-start.5 = (bf16[32,2048]{1,0:T(8,128)(2,1)}, bf16[32,2048]{1,0:T(8,128)(2,1)S(1)}, u32[]{:S(2)}, u32[]{:S(2)}) collective-permute-start(bf16[32,2048]{1,0:T(8,128)(2,1)} %get-tuple-element.16), channel_id=1, source_target_pairs={{0,130},{2,128},{128,2},{130,0},{1,131},{3,129},{129,3},{131,1},{4... | collective-permute-start | bytes 393224 | tf_op jit(solution)/shard_map/ppermute | solution.py:139
  119.9 49.1 %all-to-all-start = ((bf16[32,24,2048]{2,1,0:T(8,128)(2,1)}), bf16[32,24,2048]{2,1,0:T(8,128)(2,1)}, u32[]{:S(2)}, u32[]{:S(2)}) async-start(bf16[32,24,2048]{2,1,0:T(8,128)(2,1)} %bitcast.20), calls=%async_computation | async-start | bytes 6291456 | tf_op jit(solution)/shard_map/all_to_all | solution.py:192
  132.0 52.8 %collective-permute-start.10 = (bf16[192,2048]{1,0:T(8,128)(2,1)}, bf16[192,2048]{1,0:T(8,128)(2,1)}, u32[]{:S(2)}, u32[]{:S(2)}) collective-permute-start(bf16[192,2048]{1,0:T(8,128)(2,1)} %get-tuple-element.9), channel_id=1, source_target_pairs={{0,192},{64,128},{128,64},{192,0},{1,193},{65,129},{129,65},{193,1... | collective-permute-start | bytes 2359304 | tf_op jit(solution)/shard_map/ppermute | solution.py:139
  132.4 80.1 %collective-permute-start.9 = (bf16[192,2048]{1,0:T(8,128)(2,1)}, bf16[192,2048]{1,0:T(8,128)(2,1)}, u32[]{:S(2)}, u32[]{:S(2)}) collective-permute-start(bf16[192,2048]{1,0:T(8,128)(2,1)} %get-tuple-element.9), channel_id=1, source_target_pairs={{0,128},{128,0},{1,129},{129,1},{2,130},{130,2},{3,131},{131,3},{4... | collective-permute-start | bytes 2359304 | tf_op jit(solution)/shard_map/ppermute | solution.py:139
  136.0 51.3 %collective-permute-start.8 = (bf16[192,2048]{1,0:T(8,128)(2,1)}, bf16[192,2048]{1,0:T(8,128)(2,1)}, u32[]{:S(2)}, u32[]{:S(2)}) collective-permute-start(bf16[192,2048]{1,0:T(8,128)(2,1)} %get-tuple-element.10.w0), channel_id=1, source_target_pairs={{0,64},{64,0},{1,65},{65,1},{2,66},{66,2},{3,67},{67,3},{4,68},{68... | collective-permute-start | bytes 2359304 | tf_op jit(solution)/shard_map/ppermute | solution.py:139
  177.5 47.6 %collective-permute-start.7 = (bf16[768,384]{1,0:T(8,128)(2,1)}, bf16[768,384]{1,0:T(8,128)(2,1)S(1)}, u32[]{:S(2)}, u32[]{:S(2)}) collective-permute-start(bf16[768,384]{1,0:T(8,128)(2,1)} %up_last.1.hid_a), channel_id=1, source_target_pairs={{0,128},{128,0},{1,129},{129,1},{2,130},{130,2},{3,131},{131,3},{4... | collective-permute-start | bytes 1769480 | tf_op jit(solution)/shard_map/ppermute | solution.py:139
  225.1 0.8 copy-start.4
  232.7 11.5 %copy-start.1 = (bf16[1,2,192,4096]{3,2,1,0:T(8,128)(2,1)S(1)}, bf16[1,2,192,4096]{3,2,1,0:T(8,128)(2,1)}, u32[]{:S(2)}) copy-start(bf16[1,2,192,4096]{3,2,1,0:T(8,128)(2,1)} %refs_1_.1) | copy-start | bytes 9437188
  232.7 11.6 %copy-start.3 = (s32[8,2]{0,1:T(2,128)S(1)}, s32[8,2]{0,1:T(2,128)}, u32[]{:S(2)}) copy-start(s32[8,2]{0,1:T(2,128)} %param.11) | copy-start | bytes 196
  232.7 84.7 %all-to-all-start.2 = ((bf16[32,24,2048]{2,1,0:T(8,128)(2,1)}), bf16[32,24,2048]{2,1,0:T(8,128)(2,1)}, u32[]{:S(2)}, u32[]{:S(2)}) async-start(bf16[32,24,2048]{2,1,0:T(8,128)(2,1)} %bitcast.22), calls=%async_computation.2 | async-start | bytes 6291456 | tf_op jit(solution)/shard_map/all_to_all | solution.py:192
  241.2 72.9 %collective-permute-start.15 = (bf16[1,192,4096]{2,1,0:T(8,128)(2,1)}, bf16[1,192,4096]{2,1,0:T(8,128)(2,1)}, u32[]{:S(2)}, u32[]{:S(2)}) collective-permute-start(bf16[1,192,4096]{2,1,0:T(8,128)(2,1)} %param.10), channel_id=1, source_target_pairs={{0,32},{16,48},{32,0},{48,16},{1,33},{17,49},{33,1},{49,17},{2,34}... | collective-permute-start | bytes 4718600 | tf_op jit(solution)/shard_map/ppermute | solution.py:225
  244.1 137.3 %collective-permute-start.14 = (bf16[1,2,192,4096]{3,2,1,0:T(8,128)(2,1)S(1)}, bf16[1,2,192,4096]{3,2,1,0:T(8,128)(2,1)}, u32[]{:S(2)}, u32[]{:S(2)}) collective-permute-start(bf16[1,2,192,4096]{3,2,1,0:T(8,128)(2,1)S(1)} %copy-done.1), channel_id=1, source_target_pairs={{0,32},{16,48},{32,0},{48,16},{1,33},{17,49},{33,1},{49,17},{2,34}... | collective-permute-start | bytes 9437192 | tf_op jit(solution)/shard_map/ppermute | solution.py:248
  320.5 63.5 %collective-permute-start.11 = (bf16[32,2048]{1,0:T(8,128)(2,1)S(1)}, bf16[32,2048]{1,0:T(8,128)(2,1)S(1)}, u32[]{:S(2)}, u32[]{:S(2)}) collective-permute-start(bf16[32,2048]{1,0:T(8,128)(2,1)S(1)} %get-tuple-element.13), channel_id=1, source_target_pairs={{0,2},{2,0},{1,3},{3,1},{4,6},{6,4},{5,7},{7,5},{8,10},{10,8},{9,1... | collective-permute-start | bytes 393224 | tf_op jit(solution)/shard_map/ppermute | solution.py:139
  324.8 59.2 %collective-permute-start.12 = (bf16[32,2048]{1,0:T(8,128)(2,1)S(1)}, bf16[32,2048]{1,0:T(8,128)(2,1)S(1)}, u32[]{:S(2)}, u32[]{:S(2)}) collective-permute-start(bf16[32,2048]{1,0:T(8,128)(2,1)S(1)} %get-tuple-element.15), channel_id=1, source_target_pairs={{0,128},{128,0},{1,129},{129,1},{2,130},{130,2},{3,131},{131,3},{4... | collective-permute-start | bytes 393224 | tf_op jit(solution)/shard_map/ppermute | solution.py:139
  327.8 56.2 %collective-permute-start.13 = (bf16[32,2048]{1,0:T(8,128)(2,1)S(1)}, bf16[32,2048]{1,0:T(8,128)(2,1)S(1)}, u32[]{:S(2)}, u32[]{:S(2)}) collective-permute-start(bf16[32,2048]{1,0:T(8,128)(2,1)S(1)} %get-tuple-element.14), channel_id=1, source_target_pairs={{0,130},{2,128},{128,2},{130,0},{1,131},{3,129},{129,3},{131,1},{4... | collective-permute-start | bytes 393224 | tf_op jit(solution)/shard_map/ppermute | solution.py:139
where the time goes:
time: 390 us; the launch traced here: 385 us
  waiting for transfers between devices  277 us (71%)
  starting transfers between devices  56.4 us (14%)
  Pallas kernels  22.8 us (6%)
  other arithmetic  10.4 us (3%)
  matrix products  9.88 us (3%)
  local copies, waits for them, and re-layouts  7.67 us (2%)
    ppermute x14, waiting for transfers between devices, swap(): return lax.ppermute(value, axes, [(i, i ^ count - 1) for i in range(count)])  130 us
    ppermute x1, waiting for transfers between devices, local(): got_dn = lax.ppermute(down_proj, ('x',), across_x)  67.4 us
    ppermute x1, waiting for transfers between devices, local(): got_gu = lax.ppermute(gate_up, ('x',), across_x)  53.6 us
    ppermute x14, starting transfers between devices, swap(): return lax.ppermute(value, axes, [(i, i ^ count - 1) for i in range(count)])  27 us
    all_to_all x3, starting transfers between devices, across(): lax.all_to_all(value.reshape(experts, slots // experts, depth), PLANE, 0,...  26.3 us
    all_to_all x3, waiting for transfers between devices, across(): lax.all_to_all(value.reshape(experts, slots // experts, depth), PLANE, 0,...  25.5 us
    pallas_call x1, Pallas kernels, up(): pl.pallas_call(lambda *refs: up_last_kernel(n_in, *refs), grid=(n_in,), i...  8.51 us
  transfers between devices with their start and end apart: 19, of which 11 were waited for; matrix products, arithmetic and copies ran while one was open for 5% of the time, Pallas kernels for 4%

commit v1 on v0

--- a/solution.py
+++ b/solution.py
@@ -224,16 +224,13 @@
     across_x = [(i, i ^ 2) for i in range(4)]
     got_dn = lax.ppermute(down_proj, ("x",), across_x)
     held0 = column(first)
-    held1 = column(flat[:, half:])
+    later, _ = lax.optimization_barrier((flat, held0[:8, :META]))
+    held1 = column(later[:, half:])
     gu_b = swap(gate_up, ("ql",))
     mine = lax.dynamic_slice_in_dim(down_proj[0], q_high * half, half, axis=1)
     theirs = lax.dynamic_slice_in_dim(down_proj[0], (1 - q_high) * half, half, axis=1)
-    pieces = [
-        mine,
-        swap(mine, ("ql",)),
-        swap(theirs, ("qh",)),
-        swap(theirs, ("qh", "ql")),
-    ]
+    near_piece = swap(mine, ("ql",))
+    pieces = [mine, near_piece, swap(theirs, ("qh",)), swap(theirs, ("qh", "ql"))]
 
     pick, mix = tables(
         held0[:, half:].astype(F32), rows, tops, plane, q_high, experts, slots

time: 390 us -> 388 us (level)
  no operation moved by 1% of the time
where the time goes in v1:
time: 388 us; the launch traced here: 383 us
  waiting for transfers between devices  276 us (71%)
  starting transfers between devices  56.6 us (15%)
  Pallas kernels  22.7 us (6%)
  other arithmetic  10.5 us (3%)
  matrix products  8.98 us (2%)
  local copies, waits for them, and re-layouts  7.87 us (2%)
    ppermute x14, waiting for transfers between devices, swap(): return lax.ppermute(value, axes, [(i, i ^ count - 1) for i in range(count)])  129 us
    ppermute x1, waiting for transfers between devices, local(): got_dn = lax.ppermute(down_proj, ('x',), across_x)  67.4 us
    ppermute x1, waiting for transfers between devices, local(): got_gu = lax.ppermute(gate_up, ('x',), across_x)  53.6 us
    ppermute x14, starting transfers between devices, swap(): return lax.ppermute(value, axes, [(i, i ^ count - 1) for i in range(count)])  27.1 us
    all_to_all x3, starting transfers between devices, across(): lax.all_to_all(value.reshape(experts, slots // experts, depth), PLANE, 0,...  26.4 us
    all_to_all x3, waiting for transfers between devices, across(): lax.all_to_all(value.reshape(experts, slots // experts, depth), PLANE, 0,...  25.5 us
    pallas_call x1, Pallas kernels, up(): pl.pallas_call(lambda *refs: up_last_kernel(n_in, *refs), grid=(n_in,), i...  8.51 us
  transfers between devices with their start and end apart: 19, of which 11 were waited for; matrix products, arithmetic and copies ran while one was open for 5% of the time, Pallas kernels for 4%

profile of v1, /device:TPU:65, one launch (start us, length us, event | category | flops | bytes accessed | tf_op | source)
XLA Modules:
  0.0 383.4 jit_solution(9102489707388398526)
XLA Ops:
  3.4 5.2 %collective-permute-start = (bf16[32,2176]{1,0:T(8,128)(2,1)S(1)}, bf16[32,2176]{1,0:T(8,128)(2,1)S(1)}, u32[]{:S(2)}, u32[]{:S(2)}) collective-permute-start(bf16[32,2176]{1,0:T(8,128)(2,1)S(1)} %concatenate.25), channel_id=1, source_target_pairs={{0,2},{2,0},{1,3},{3,1},{4,6},{6,4},{5,7},{7,5},{8,10},{10,8},{9,1... | collective-permute-start | bytes 417800 | tf_op jit(solution)/shard_map/ppermute | solution.py:139
  9.9 5.5 %collective-permute-done = bf16[32,2176]{1,0:T(8,128)(2,1)S(1)} collective-permute-done((bf16[32,2176]{1,0:T(8,128)(2,1)S(1)}, bf16[32,2176]{1,0:T(8,128)(2,1)S(1)}, u32[]{:S(2)}, u32[]{:S(2)}) %collective-permute-start) | collective-permute-done | bytes 139296 | tf_op jit(solution)/shard_map/ppermute | solution.py:139
  15.4 4.9 %collective-permute-done.1 = bf16[32,2176]{1,0:T(8,128)(2,1)S(1)} collective-permute-done((bf16[32,2176]{1,0:T(8,128)(2,1)S(1)}, bf16[32,2176]{1,0:T(8,128)(2,1)S(1)}, u32[]{:S(2)}, u32[]{:S(2)}) %collective-permute-start.1) | collective-permute-done | bytes 139296 | tf_op jit(solution)/shard_map/ppermute | solution.py:139
  20.3 1.4 collective-permute-done.2
  24.0 2.7 convolution_convert_fusion
  26.7 8.4 %all-to-all-start.1 = ((bf16[32,24,2048]{2,1,0:T(8,128)(2,1)}), bf16[32,24,2048]{2,1,0:T(8,128)(2,1)}, u32[]{:S(2)}, u32[]{:S(2)}) async-start(bf16[32,24,2048]{2,1,0:T(8,128)(2,1)} %bitcast.21), calls=%async_computation.1 | async-start | bytes 6291456 | tf_op jit(solution)/shard_map/all_to_all | solution.py:192
  37.2 3.8 collective-permute-start.3
  40.9 1.6 collective-permute-start.4
  42.9 72.7 %collective-permute-done.3 = bf16[32,2048]{1,0:T(8,128)(2,1)S(1)} collective-permute-done((bf16[32,2048]{1,0:T(8,128)(2,1)S(1)}, bf16[32,2048]{1,0:T(8,128)(2,1)S(1)}, u32[]{:S(2)}, u32[]{:S(2)}) %collective-permute-start.3) | collective-permute-done | bytes 131104 | tf_op jit(solution)/shard_map/ppermute | solution.py:139
  115.6 2.7 convolution_convert_fusion.1
  118.3 9.3 %all-to-all-start = ((bf16[32,24,2048]{2,1,0:T(8,128)(2,1)}), bf16[32,24,2048]{2,1,0:T(8,128)(2,1)}, u32[]{:S(2)}, u32[]{:S(2)}) async-start(bf16[32,24,2048]{2,1,0:T(8,128)(2,1)} %bitcast.20), calls=%async_computation | async-start | bytes 6291456 | tf_op jit(solution)/shard_map/all_to_all | solution.py:192
  127.6 2.8 dynamic-slice_bitcast_fusion
  130.8 3.6 collective-permute-start.9
  134.4 7.5 %up_first.1.refs_3_ = f32[768,768]{1,0:T(8,128)} custom-call(bf16[768,2048]{1,0:T(8,128)(2,1)} %bitcast.5.x_ref, bf16[1,2,192,4096]{3,2,1,0:T(8,128)(2,1)} %refs_1_.1, bf16[1,2,192,4096]{3,2,1,0:T(8,128)(2,1)} %collective-permute-done.6.gu_b.refs_2_), custom_call_target="tpu_custom_call" | custom-call | flops 2415919104 | bytes 8650752 | tf_op jit(solution)/shard_map/up_first/pallas_call | solution.py:86
  141.9 25.5 %all-to-all-done = bf16[32,24,2048]{2,1,0:T(8,128)(2,1)} async-done(((bf16[32,24,2048]{2,1,0:T(8,128)(2,1)}), bf16[32,24,2048]{2,1,0:T(8,128)(2,1)}, u32[]{:S(2)}, u32[]{:S(2)}) %all-to-all-start) | async-done | bytes 3145760 | tf_op jit(solution)/shard_map/all_to_all | solution.py:192
  167.4 8.5 %up_last.1.hid_a = bf16[768,384]{1,0:T(8,128)(2,1)} custom-call(bf16[768,2048]{1,0:T(8,128)(2,1)} %bitcast.3.refs_0_, bf16[1,2,192,4096]{3,2,1,0:T(8,128)(2,1)} %refs_1_.1, bf16[1,2,192,4096]{3,2,1,0:T(8,128)(2,1)} %collective-permute-done.6.gu_b.refs_2_, f32[768,768]{1,0:T(8,128)} %up_first.1.refs_3_), custom_call_target="tpu_custom_call" | custom-call | flops 2415919104 | bytes 8650752 | tf_op jit(solution)/shard_map/up_last/pallas_call | solution.py:95
  175.9 2.6 collective-permute-start.7
  178.6 4.6 %collective-permute-done.10.w3 = bf16[192,2048]{1,0:T(8,128)(2,1)} collective-permute-done((bf16[192,2048]{1,0:T(8,128)(2,1)}, bf16[192,2048]{1,0:T(8,128)(2,1)}, u32[]{:S(2)}, u32[]{:S(2)}) %collective-permute-start.10) | collective-permute-done | bytes 786464 | tf_op jit(solution)/shard_map/ppermute | solution.py:139
  183.2 2.4 collective-permute-done.8.w1
  185.6 25.2 %collective-permute-done.9.w2 = bf16[192,2048]{1,0:T(8,128)(2,1)} collective-permute-done((bf16[192,2048]{1,0:T(8,128)(2,1)}, bf16[192,2048]{1,0:T(8,128)(2,1)}, u32[]{:S(2)}, u32[]{:S(2)}) %collective-permute-start.9) | collective-permute-done | bytes 786464 | tf_op jit(solution)/shard_map/ppermute | solution.py:139
  210.9 12.6 %collective-permute-done.7.hid_b = bf16[768,384]{1,0:T(8,128)(2,1)S(1)} collective-permute-done((bf16[768,384]{1,0:T(8,128)(2,1)}, bf16[768,384]{1,0:T(8,128)(2,1)S(1)}, u32[]{:S(2)}, u32[]{:S(2)}) %collective-permute-start.7) | collective-permute-done | bytes 589856 | tf_op jit(solution)/shard_map/ppermute | solution.py:139
  224.3 6.7 %down.1 = bf16[768,2048]{1,0:T(8,128)(2,1)} custom-call(bf16[768,384]{1,0:T(8,128)(2,1)} %up_last.1.hid_a, bf16[768,384]{1,0:T(8,128)(2,1)} %copy-done.4, bf16[192,2048]{1,0:T(8,128)(2,1)} %get-tuple-element.10.w0, bf16[192,2048]{1,0:T(8,128)(2,1)} %collective-permute-done.8.w1, bf16[192,2048]{1,0:T(8,128)(2,1)} %collective-permute-done.9.w2, ...), custom_call_target="tpu_custom_call" | custom-call | flops 2415919104 | bytes 7471104 | tf_op jit(solution)/shard_map/down/pallas_call | solution.py:122
  231.1 8.7 %all-to-all-start.2 = ((bf16[32,24,2048]{2,1,0:T(8,128)(2,1)}), bf16[32,24,2048]{2,1,0:T(8,128)(2,1)}, u32[]{:S(2)}, u32[]{:S(2)}) async-start(bf16[32,24,2048]{2,1,0:T(8,128)(2,1)} %bitcast.22), calls=%async_computation.2 | async-start | bytes 6291456 | tf_op jit(solution)/shard_map/all_to_all | solution.py:192
  239.7 3.0 collective-permute-start.15
  243.4 1.7 fusion.17
  245.2 67.4 %collective-permute-done.15 = bf16[1,192,4096]{2,1,0:T(8,128)(2,1)} collective-permute-done((bf16[1,192,4096]{2,1,0:T(8,128)(2,1)}, bf16[1,192,4096]{2,1,0:T(8,128)(2,1)}, u32[]{:S(2)}, u32[]{:S(2)}) %collective-permute-start.15) | collective-permute-done | bytes 1572896 | tf_op jit(solution)/shard_map/ppermute | solution.py:225
  312.6 3.4 broadcast_select_fusion.1
  315.9 3.0 fusion.19
  319.1 4.3 %collective-permute-start.11 = (bf16[32,2048]{1,0:T(8,128)(2,1)S(1)}, bf16[32,2048]{1,0:T(8,128)(2,1)S(1)}, u32[]{:S(2)}, u32[]{:S(2)}) collective-permute-start(bf16[32,2048]{1,0:T(8,128)(2,1)S(1)} %get-tuple-element.13), channel_id=1, source_target_pairs={{0,2},{2,0},{1,3},{3,1},{4,6},{6,4},{5,7},{7,5},{8,10},{10,8},{9,1... | collective-permute-start | bytes 393224 | tf_op jit(solution)/shard_map/ppermute | solution.py:139
  323.4 3.0 collective-permute-start.12
  326.4 53.6 %collective-permute-done.14 = bf16[1,2,192,4096]{3,2,1,0:T(8,128)(2,1)} collective-permute-done((bf16[1,2,192,4096]{3,2,1,0:T(8,128)(2,1)S(1)}, bf16[1,2,192,4096]{3,2,1,0:T(8,128)(2,1)}, u32[]{:S(2)}, u32[]{:S(2)}) %collective-permute-start.14) | collective-permute-done | bytes 3145760 | tf_op jit(solution)/shard_map/ppermute | solution.py:245
  380.0 2.6 broadcast_select_fusion
  (59 shorter events, 11.6 us)
Async XLA Ops:
  3.4 12.0 %collective-permute-start = (bf16[32,2176]{1,0:T(8,128)(2,1)S(1)}, bf16[32,2176]{1,0:T(8,128)(2,1)S(1)}, u32[]{:S(2)}, u32[]{:S(2)}) collective-permute-start(bf16[32,2176]{1,0:T(8,128)(2,1)S(1)} %concatenate.25), channel_id=1, source_target_pairs={{0,2},{2,0},{1,3},{3,1},{4,6},{6,4},{5,7},{7,5},{8,10},{10,8},{9,1... | collective-permute-start | bytes 417800 | tf_op jit(solution)/shard_map/ppermute | solution.py:139
  8.6 11.7 %collective-permute-start.1 = (bf16[32,2176]{1,0:T(8,128)(2,1)S(1)}, bf16[32,2176]{1,0:T(8,128)(2,1)S(1)}, u32[]{:S(2)}, u32[]{:S(2)}) collective-permute-start(bf16[32,2176]{1,0:T(8,128)(2,1)S(1)} %concatenate.25), channel_id=1, source_target_pairs={{0,128},{128,0},{1,129},{129,1},{2,130},{130,2},{3,131},{131,3},{4... | collective-permute-start | bytes 417800 | tf_op jit(solution)/shard_map/ppermute | solution.py:139
  9.8 11.9 %collective-permute-start.2 = (bf16[32,2176]{1,0:T(8,128)(2,1)S(1)}, bf16[32,2176]{1,0:T(8,128)(2,1)S(1)}, u32[]{:S(2)}, u32[]{:S(2)}) collective-permute-start(bf16[32,2176]{1,0:T(8,128)(2,1)S(1)} %concatenate.25), channel_id=1, source_target_pairs={{0,130},{2,128},{128,2},{130,0},{1,131},{3,129},{129,3},{131,1},{4... | collective-permute-start | bytes 417800 | tf_op jit(solution)/shard_map/ppermute | solution.py:139
  22.8 1.0 copy-start.2
  26.7 8.4 %copy-start = (bf16[1,2,192,4096]{3,2,1,0:T(8,128)(2,1)S(1)}, bf16[1,2,192,4096]{3,2,1,0:T(8,128)(2,1)}, u32[]{:S(2)}) copy-start(bf16[1,2,192,4096]{3,2,1,0:T(8,128)(2,1)} %refs_1_.1) | copy-start | bytes 9437188
  26.7 91.5 %all-to-all-start.1 = ((bf16[32,24,2048]{2,1,0:T(8,128)(2,1)}), bf16[32,24,2048]{2,1,0:T(8,128)(2,1)}, u32[]{:S(2)}, u32[]{:S(2)}) async-start(bf16[32,24,2048]{2,1,0:T(8,128)(2,1)} %bitcast.21), calls=%async_computation.1 | async-start | bytes 6291456 | tf_op jit(solution)/shard_map/all_to_all | solution.py:192
  35.2 99.2 %collective-permute-start.6 = (bf16[1,2,192,4096]{3,2,1,0:T(8,128)(2,1)S(1)}, bf16[1,2,192,4096]{3,2,1,0:T(8,128)(2,1)}, u32[]{:S(2)}, u32[]{:S(2)}) collective-permute-start(bf16[1,2,192,4096]{3,2,1,0:T(8,128)(2,1)S(1)} %copy-done), channel_id=1, source_target_pairs={{0,64},{64,0},{1,65},{65,1},{2,66},{66,2},{3,67},{67,3},{4,68},{68... | collective-permute-start | bytes 9437192 | tf_op jit(solution)/shard_map/ppermute | solution.py:139
  37.2 78.4 %collective-permute-start.3 = (bf16[32,2048]{1,0:T(8,128)(2,1)S(1)}, bf16[32,2048]{1,0:T(8,128)(2,1)S(1)}, u32[]{:S(2)}, u32[]{:S(2)}) collective-permute-start(bf16[32,2048]{1,0:T(8,128)(2,1)S(1)} %slice.83), channel_id=1, source_target_pairs={{0,2},{2,0},{1,3},{3,1},{4,6},{6,4},{5,7},{7,5},{8,10},{10,8},{9,1... | collective-permute-start | bytes 393224 | tf_op jit(solution)/shard_map/ppermute | solution.py:139
  40.9 74.6 %collective-permute-start.4 = (bf16[32,2048]{1,0:T(8,128)(2,1)S(1)}, bf16[32,2048]{1,0:T(8,128)(2,1)S(1)}, u32[]{:S(2)}, u32[]{:S(2)}) collective-permute-start(bf16[32,2048]{1,0:T(8,128)(2,1)S(1)} %slice.83), channel_id=1, source_target_pairs={{0,128},{128,0},{1,129},{129,1},{2,130},{130,2},{3,131},{131,3},{4... | collective-permute-start | bytes 393224 | tf_op jit(solution)/shard_map/ppermute | solution.py:139
  42.6 73.0 %collective-permute-start.5 = (bf16[32,2048]{1,0:T(8,128)(2,1)S(1)}, bf16[32,2048]{1,0:T(8,128)(2,1)S(1)}, u32[]{:S(2)}, u32[]{:S(2)}) collective-permute-start(bf16[32,2048]{1,0:T(8,128)(2,1)S(1)} %slice.83), channel_id=1, source_target_pairs={{0,130},{2,128},{128,2},{130,0},{1,131},{3,129},{129,3},{131,1},{4... | collective-permute-start | bytes 393224 | tf_op jit(solution)/shard_map/ppermute | solution.py:139
  118.3 49.1 %all-to-all-start = ((bf16[32,24,2048]{2,1,0:T(8,128)(2,1)}), bf16[32,24,2048]{2,1,0:T(8,128)(2,1)}, u32[]{:S(2)}, u32[]{:S(2)}) async-start(bf16[32,24,2048]{2,1,0:T(8,128)(2,1)} %bitcast.20), calls=%async_computation | async-start | bytes 6291456 | tf_op jit(solution)/shard_map/all_to_all | solution.py:192
  130.4 52.8 %collective-permute-start.10 = (bf16[192,2048]{1,0:T(8,128)(2,1)}, bf16[192,2048]{1,0:T(8,128)(2,1)}, u32[]{:S(2)}, u32[]{:S(2)}) collective-permute-start(bf16[192,2048]{1,0:T(8,128)(2,1)} %get-tuple-element.9), channel_id=1, source_target_pairs={{0,192},{64,128},{128,64},{192,0},{1,193},{65,129},{129,65},{193,1... | collective-permute-start | bytes 2359304 | tf_op jit(solution)/shard_map/ppermute | solution.py:139
  130.8 80.1 %collective-permute-start.9 = (bf16[192,2048]{1,0:T(8,128)(2,1)}, bf16[192,2048]{1,0:T(8,128)(2,1)}, u32[]{:S(2)}, u32[]{:S(2)}) collective-permute-start(bf16[192,2048]{1,0:T(8,128)(2,1)} %get-tuple-element.9), channel_id=1, source_target_pairs={{0,128},{128,0},{1,129},{129,1},{2,130},{130,2},{3,131},{131,3},{4... | collective-permute-start | bytes 2359304 | tf_op jit(solution)/shard_map/ppermute | solution.py:139
  134.4 51.3 %collective-permute-start.8 = (bf16[192,2048]{1,0:T(8,128)(2,1)}, bf16[192,2048]{1,0:T(8,128)(2,1)}, u32[]{:S(2)}, u32[]{:S(2)}) collective-permute-start(bf16[192,2048]{1,0:T(8,128)(2,1)} %get-tuple-element.10.w0), channel_id=1, source_target_pairs={{0,64},{64,0},{1,65},{65,1},{2,66},{66,2},{3,67},{67,3},{4,68},{68... | collective-permute-start | bytes 2359304 | tf_op jit(solution)/shard_map/ppermute | solution.py:139
  175.9 47.6 %collective-permute-start.7 = (bf16[768,384]{1,0:T(8,128)(2,1)}, bf16[768,384]{1,0:T(8,128)(2,1)S(1)}, u32[]{:S(2)}, u32[]{:S(2)}) collective-permute-start(bf16[768,384]{1,0:T(8,128)(2,1)} %up_last.1.hid_a), channel_id=1, source_target_pairs={{0,128},{128,0},{1,129},{129,1},{2,130},{130,2},{3,131},{131,3},{4... | collective-permute-start | bytes 1769480 | tf_op jit(solution)/shard_map/ppermute | solution.py:139
  223.5 0.8 copy-start.4
  231.0 11.6 %copy-start.1 = (bf16[1,2,192,4096]{3,2,1,0:T(8,128)(2,1)S(1)}, bf16[1,2,192,4096]{3,2,1,0:T(8,128)(2,1)}, u32[]{:S(2)}) copy-start(bf16[1,2,192,4096]{3,2,1,0:T(8,128)(2,1)} %refs_1_.1) | copy-start | bytes 9437188
  231.1 11.7 %copy-start.3 = (s32[8,2]{0,1:T(2,128)S(1)}, s32[8,2]{0,1:T(2,128)}, u32[]{:S(2)}) copy-start(s32[8,2]{0,1:T(2,128)} %param.11) | copy-start | bytes 196
  231.1 84.9 %all-to-all-start.2 = ((bf16[32,24,2048]{2,1,0:T(8,128)(2,1)}), bf16[32,24,2048]{2,1,0:T(8,128)(2,1)}, u32[]{:S(2)}, u32[]{:S(2)}) async-start(bf16[32,24,2048]{2,1,0:T(8,128)(2,1)} %bitcast.22), calls=%async_computation.2 | async-start | bytes 6291456 | tf_op jit(solution)/shard_map/all_to_all | solution.py:192
  239.7 72.9 %collective-permute-start.15 = (bf16[1,192,4096]{2,1,0:T(8,128)(2,1)}, bf16[1,192,4096]{2,1,0:T(8,128)(2,1)}, u32[]{:S(2)}, u32[]{:S(2)}) collective-permute-start(bf16[1,192,4096]{2,1,0:T(8,128)(2,1)} %param.10), channel_id=1, source_target_pairs={{0,32},{16,48},{32,0},{48,16},{1,33},{17,49},{33,1},{49,17},{2,34}... | collective-permute-start | bytes 4718600 | tf_op jit(solution)/shard_map/ppermute | solution.py:225
  242.7 137.3 %collective-permute-start.14 = (bf16[1,2,192,4096]{3,2,1,0:T(8,128)(2,1)S(1)}, bf16[1,2,192,4096]{3,2,1,0:T(8,128)(2,1)}, u32[]{:S(2)}, u32[]{:S(2)}) collective-permute-start(bf16[1,2,192,4096]{3,2,1,0:T(8,128)(2,1)S(1)} %copy-done.1), channel_id=1, source_target_pairs={{0,32},{16,48},{32,0},{48,16},{1,33},{17,49},{33,1},{49,17},{2,34}... | collective-permute-start | bytes 9437192 | tf_op jit(solution)/shard_map/ppermute | solution.py:245
  319.1 63.5 %collective-permute-start.11 = (bf16[32,2048]{1,0:T(8,128)(2,1)S(1)}, bf16[32,2048]{1,0:T(8,128)(2,1)S(1)}, u32[]{:S(2)}, u32[]{:S(2)}) collective-permute-start(bf16[32,2048]{1,0:T(8,128)(2,1)S(1)} %get-tuple-element.13), channel_id=1, source_target_pairs={{0,2},{2,0},{1,3},{3,1},{4,6},{6,4},{5,7},{7,5},{8,10},{10,8},{9,1... | collective-permute-start | bytes 393224 | tf_op jit(solution)/shard_map/ppermute | solution.py:139
  323.4 59.2 %collective-permute-start.12 = (bf16[32,2048]{1,0:T(8,128)(2,1)S(1)}, bf16[32,2048]{1,0:T(8,128)(2,1)S(1)}, u32[]{:S(2)}, u32[]{:S(2)}) collective-permute-start(bf16[32,2048]{1,0:T(8,128)(2,1)S(1)} %get-tuple-element.15), channel_id=1, source_target_pairs={{0,128},{128,0},{1,129},{129,1},{2,130},{130,2},{3,131},{131,3},{4... | collective-permute-start | bytes 393224 | tf_op jit(solution)/shard_map/ppermute | solution.py:139
  326.4 56.2 %collective-permute-start.13 = (bf16[32,2048]{1,0:T(8,128)(2,1)S(1)}, bf16[32,2048]{1,0:T(8,128)(2,1)S(1)}, u32[]{:S(2)}, u32[]{:S(2)}) collective-permute-start(bf16[32,2048]{1,0:T(8,128)(2,1)S(1)} %get-tuple-element.14), channel_id=1, source_target_pairs={{0,130},{2,128},{128,2},{130,0},{1,131},{3,129},{129,3},{131,1},{4... | collective-permute-start | bytes 393224 | tf_op jit(solution)/shard_map/ppermute | solution.py:139

commit v2 on v1

--- a/solution.py
+++ b/solution.py
@@ -11,6 +11,7 @@
 CAP = 3
 CHUNK = 1024
 META = 128
+HEAD = 256
 TILE = 256
 PLANE = ("x", "y", "c")
 
@@ -134,6 +135,47 @@
     )(hid_a, hid_b, *pieces)
 
 
+def put_kernel(moving, got, own, *refs):
+    out = refs[-1]
+
+    @pl.when(moving[0] != 0)
+    def _():
+        out[...] = got[...]
+
+    @pl.when(moving[0] == 0)
+    def _():
+        out[...] = own[...]
+
+
+def put(moving, got, own, first, base=None):
+    block = 64
+    depth = own.shape[1]
+    start = first // block
+    here = pl.BlockSpec((block, depth), lambda i, m: (start + i, 0))
+    specs = [pl.BlockSpec((block, depth), lambda i, m: (i, 0)), here]
+    args = [moving, got, own]
+    aliases = {}
+    if base is not None:
+        specs.append(pl.BlockSpec(memory_space=pl.ANY))
+        args.append(base)
+        aliases = {3: 0}
+    return pl.pallas_call(
+        put_kernel,
+        grid_spec=pltpu.PrefetchScalarGridSpec(
+            num_scalar_prefetch=1,
+            grid=(got.shape[0] // block,),
+            in_specs=specs,
+            out_specs=here,
+        ),
+        out_shape=jax.ShapeDtypeStruct(own.shape, own.dtype),
+        input_output_aliases=aliases,
+        cost_estimate=pl.CostEstimate(
+            flops=0, bytes_accessed=6 * got.shape[0] * depth, transcendentals=0
+        ),
+        name="put",
+    )(*args)
+
+
 def swap(value, axes):
     count = 2 ** len(axes)
     return lax.ppermute(value, axes, [(i, i ^ (count - 1)) for i in range(count)])
@@ -224,8 +266,7 @@
     across_x = [(i, i ^ 2) for i in range(4)]
     got_dn = lax.ppermute(down_proj, ("x",), across_x)
     held0 = column(first)
-    later, _ = lax.optimization_barrier((flat, held0[:8, :META]))
-    held1 = column(later[:, half:])
+    held1 = column(flat[:, half:])
     gu_b = swap(gate_up, ("ql",))
     mine = lax.dynamic_slice_in_dim(down_proj[0], q_high * half, half, axis=1)
     theirs = lax.dynamic_slice_in_dim(down_proj[0], (1 - q_high) * half, half, axis=1)
@@ -242,7 +283,9 @@
     start = up(x0, gate_up, gu_b, 0)
     hidden = up(x1, gate_up, gu_b, half, start)
     hidden_b = swap(hidden, ("qh",))
-    got_gu = lax.ppermute(gate_up, ("x",), across_x)
+    table = gate_up.reshape(-1, depth)
+    got_gu0 = lax.ppermute(table[:HEAD], ("x",), across_x)
+    got_gu1 = lax.ppermute(table[HEAD:], ("x",), across_x)
     made = down(hidden, hidden_b, pieces)
     back = across(made, experts)
     both = jnp.dot(mix, back, preferred_element_type=F32)
@@ -256,10 +299,14 @@
         [jnp.where(low_half, near, far), jnp.where(low_half, far, near)], axis=1
     )
     moving = jnp.any(pairs == slot)
+    flag = moving.astype(jnp.int32).reshape(1)
+    new_gu = put(flag, got_gu0, table, 0)
+    new_gu = put(flag, got_gu1, table, HEAD, new_gu)
+    new_dn = jnp.where(moving, got_dn, down_proj)
     return (
         out.astype(BF16).reshape(steps, rows, depth),
-        jnp.where(moving, got_gu, gate_up),
-        jnp.where(moving, got_dn, down_proj),
+        new_gu.reshape(gate_up.shape),
+        new_dn,
     )
 
 

time: 388 us -> 391 us (level)
  waiting for transfers between devices: 276 us -> 264 us
  starting transfers between devices: 56.6 us -> 64.3 us
  Pallas kernels: 22.7 us -> 29.2 us
  other arithmetic: 10.5 us -> 5.81 us
    ppermute x1, waiting for transfers between devices: 67.4 us -> 22.7 us  [local(): got_dn = lax.ppermute(down_proj, ('x',), across_x)]
    all_to_all x3, waiting for transfers between devices: 25.5 us -> 54.5 us  [across(): lax.all_to_all(value.reshape(experts, slots // experts, depth), PLANE, 0,...]
    pallas_call x0 -> x2, Pallas kernels: none -> 6.48 us  [put(): pl.pallas_call(put_kernel, grid_spec=pltpu.PrefetchScalarGridSpec(num_sca...]
    ppermute x14, starting transfers between devices: 27.1 us -> 32.2 us  [swap(): return lax.ppermute(value, axes, [(i, i ^ count - 1) for i in range(count)])]
    select_n x2 -> x1, other arithmetic: 5.99 us -> 2 us  [local(): new_dn = jnp.where(moving, got_dn, down_proj)]
    ppermute x1 -> x2, waiting for transfers between devices: 53.6 us -> 56 us  [the longest x1 37.8 us: local(): got_gu0 = lax.ppermute(table[:HEAD], ('x',), across_x)]
  transfers between devices with their start and end apart: 19 -> 20, of which waited for: 11 -> 13; matrix products, arithmetic and copies ran while one was open for 5% -> 4% of each run, Pallas kernels for 4% -> 6%
where the time goes in v2:
time: 391 us; the launch traced here: 386 us
  waiting for transfers between devices  264 us (68%)
  starting transfers between devices  64.3 us (16%)
  Pallas kernels  29.2 us (7%)
  local copies, waits for them, and re-layouts  11.2 us (3%)
  matrix products  9.76 us (2%)
  other arithmetic  5.81 us (1%)
    ppermute x14, waiting for transfers between devices, swap(): return lax.ppermute(value, axes, [(i, i ^ count - 1) for i in range(count)])  130 us
    all_to_all x3, waiting for transfers between devices, across(): lax.all_to_all(value.reshape(experts, slots // experts, depth), PLANE, 0,...  54.5 us
    ppermute x1, waiting for transfers between devices, local(): got_gu0 = lax.ppermute(table[:HEAD], ('x',), across_x)  37.8 us
    ppermute x14, starting transfers between devices, swap(): return lax.ppermute(value, axes, [(i, i ^ count - 1) for i in range(count)])  32.2 us
    all_to_all x3, starting transfers between devices, across(): lax.all_to_all(value.reshape(experts, slots // experts, depth), PLANE, 0,...  26.3 us
    ppermute x1, waiting for transfers between devices, local(): got_dn = lax.ppermute(down_proj, ('x',), across_x)  22.7 us
    ppermute x1, waiting for transfers between devices, local(): got_gu1 = lax.ppermute(table[HEAD:], ('x',), across_x)  18.2 us
    pallas_call x1, Pallas kernels, up(): pl.pallas_call(lambda *refs: up_last_kernel(n_in, *refs), grid=(n_in,), i...  8.5 us
  transfers between devices with their start and end apart: 20, of which 13 were waited for; matrix products, arithmetic and copies ran while one was open for 4% of the time, Pallas kernels for 6%

profile of v2, /device:TPU:65, one launch (start us, length us, event | category | flops | bytes accessed | tf_op | source)
XLA Modules:
  0.0 385.5 jit_solution(10921962024868926272)
XLA Ops:
  4.1 5.2 %collective-permute-start = (bf16[32,2176]{1,0:T(8,128)(2,1)S(1)}, bf16[32,2176]{1,0:T(8,128)(2,1)S(1)}, u32[]{:S(2)}, u32[]{:S(2)}) collective-permute-start(bf16[32,2176]{1,0:T(8,128)(2,1)S(1)} %concatenate.25), channel_id=1, source_target_pairs={{0,2},{2,0},{1,3},{3,1},{4,6},{6,4},{5,7},{7,5},{8,10},{10,8},{9,1... | collective-permute-start | bytes 417800 | tf_op jit(solution)/shard_map/ppermute | solution.py:181
  10.6 5.5 %collective-permute-done = bf16[32,2176]{1,0:T(8,128)(2,1)S(1)} collective-permute-done((bf16[32,2176]{1,0:T(8,128)(2,1)S(1)}, bf16[32,2176]{1,0:T(8,128)(2,1)S(1)}, u32[]{:S(2)}, u32[]{:S(2)}) %collective-permute-start) | collective-permute-done | bytes 139296 | tf_op jit(solution)/shard_map/ppermute | solution.py:181
  16.1 4.9 %collective-permute-done.1 = bf16[32,2176]{1,0:T(8,128)(2,1)S(1)} collective-permute-done((bf16[32,2176]{1,0:T(8,128)(2,1)S(1)}, bf16[32,2176]{1,0:T(8,128)(2,1)S(1)}, u32[]{:S(2)}, u32[]{:S(2)}) %collective-permute-start.1) | collective-permute-done | bytes 139296 | tf_op jit(solution)/shard_map/ppermute | solution.py:181
  24.7 2.7 convolution_convert_fusion
  27.5 8.4 %all-to-all-start.1 = ((bf16[32,24,2048]{2,1,0:T(8,128)(2,1)}), bf16[32,24,2048]{2,1,0:T(8,128)(2,1)}, u32[]{:S(2)}, u32[]{:S(2)}) async-start(bf16[32,24,2048]{2,1,0:T(8,128)(2,1)} %bitcast.28), calls=%async_computation.1 | async-start | bytes 6291456 | tf_op jit(solution)/shard_map/all_to_all | solution.py:234
  37.0 3.7 collective-permute-start.3
  42.6 73.7 %collective-permute-done.3 = bf16[32,2048]{1,0:T(8,128)(2,1)S(1)} collective-permute-done((bf16[32,2048]{1,0:T(8,128)(2,1)}, bf16[32,2048]{1,0:T(8,128)(2,1)S(1)}, u32[]{:S(2)}, u32[]{:S(2)}) %collective-permute-start.3) | collective-permute-done | bytes 131104 | tf_op jit(solution)/shard_map/ppermute | solution.py:181
  116.3 3.6 convolution_convert_fusion.1
  119.9 9.3 %all-to-all-start = ((bf16[32,24,2048]{2,1,0:T(8,128)(2,1)}), bf16[32,24,2048]{2,1,0:T(8,128)(2,1)}, u32[]{:S(2)}, u32[]{:S(2)}) async-start(bf16[32,24,2048]{2,1,0:T(8,128)(2,1)} %bitcast.27), calls=%async_computation | async-start | bytes 6291456 | tf_op jit(solution)/shard_map/all_to_all | solution.py:234
  129.2 2.7 dynamic-slice_bitcast_fusion
  132.4 3.6 collective-permute-start.9
  136.0 7.5 %up_first.1.refs_3_ = f32[768,768]{1,0:T(8,128)} custom-call(bf16[768,2048]{1,0:T(8,128)(2,1)} %bitcast.5.x_ref, bf16[1,2,192,4096]{3,2,1,0:T(8,128)(2,1)} %refs_1_.1, bf16[1,2,192,4096]{3,2,1,0:T(8,128)(2,1)} %collective-permute-done.6.gu_b.refs_2_), custom_call_target="tpu_custom_call" | custom-call | flops 2415919104 | bytes 8650752 | tf_op jit(solution)/shard_map/up_first/pallas_call | solution.py:87
  143.5 25.5 %all-to-all-done = bf16[32,24,2048]{2,1,0:T(8,128)(2,1)} async-done(((bf16[32,24,2048]{2,1,0:T(8,128)(2,1)}), bf16[32,24,2048]{2,1,0:T(8,128)(2,1)}, u32[]{:S(2)}, u32[]{:S(2)}) %all-to-all-start) | async-done | bytes 3145760 | tf_op jit(solution)/shard_map/all_to_all | solution.py:234
  169.0 8.5 %up_last.1.hid_a = bf16[768,384]{1,0:T(8,128)(2,1)} custom-call(bf16[768,2048]{1,0:T(8,128)(2,1)} %bitcast.3.refs_0_, bf16[1,2,192,4096]{3,2,1,0:T(8,128)(2,1)} %refs_1_.1, bf16[1,2,192,4096]{3,2,1,0:T(8,128)(2,1)} %collective-permute-done.6.gu_b.refs_2_, f32[768,768]{1,0:T(8,128)} %up_first.1.refs_3_), custom_call_target="tpu_custom_call" | custom-call | flops 2415919104 | bytes 8650752 | tf_op jit(solution)/shard_map/up_last/pallas_call | solution.py:96
  177.5 2.6 collective-permute-start.7
  180.2 4.6 %collective-permute-done.10.w3 = bf16[192,2048]{1,0:T(8,128)(2,1)} collective-permute-done((bf16[192,2048]{1,0:T(8,128)(2,1)}, bf16[192,2048]{1,0:T(8,128)(2,1)}, u32[]{:S(2)}, u32[]{:S(2)}) %collective-permute-start.10) | collective-permute-done | bytes 786464 | tf_op jit(solution)/shard_map/ppermute | solution.py:181
  184.8 2.4 collective-permute-done.8.w1
  187.3 25.2 %collective-permute-done.9.w2 = bf16[192,2048]{1,0:T(8,128)(2,1)} collective-permute-done((bf16[192,2048]{1,0:T(8,128)(2,1)}, bf16[192,2048]{1,0:T(8,128)(2,1)}, u32[]{:S(2)}, u32[]{:S(2)}) %collective-permute-start.9) | collective-permute-done | bytes 786464 | tf_op jit(solution)/shard_map/ppermute | solution.py:181
  212.5 12.6 %collective-permute-done.7.hid_b = bf16[768,384]{1,0:T(8,128)(2,1)S(1)} collective-permute-done((bf16[768,384]{1,0:T(8,128)(2,1)}, bf16[768,384]{1,0:T(8,128)(2,1)S(1)}, u32[]{:S(2)}, u32[]{:S(2)}) %collective-permute-start.7) | collective-permute-done | bytes 589856 | tf_op jit(solution)/shard_map/ppermute | solution.py:181
  225.9 6.7 %down.1 = bf16[768,2048]{1,0:T(8,128)(2,1)} custom-call(bf16[768,384]{1,0:T(8,128)(2,1)} %up_last.1.hid_a, bf16[768,384]{1,0:T(8,128)(2,1)} %copy-done.6, bf16[192,2048]{1,0:T(8,128)(2,1)} %get-tuple-element.10.w0, bf16[192,2048]{1,0:T(8,128)(2,1)} %collective-permute-done.8.w1, bf16[192,2048]{1,0:T(8,128)(2,1)} %collective-permute-done.9.w2, ...), custom_call_target="tpu_custom_call" | custom-call | flops 2415919104 | bytes 7471104 | tf_op jit(solution)/shard_map/down/pallas_call | solution.py:123
  232.7 8.5 %all-to-all-start.2 = ((bf16[32,24,2048]{2,1,0:T(8,128)(2,1)}), bf16[32,24,2048]{2,1,0:T(8,128)(2,1)}, u32[]{:S(2)}, u32[]{:S(2)}) async-start(bf16[32,24,2048]{2,1,0:T(8,128)(2,1)} %bitcast.30), calls=%async_computation.2 | async-start | bytes 6291456 | tf_op jit(solution)/shard_map/all_to_all | solution.py:234
  241.2 3.0 collective-permute-start.16
  246.8 2.9 collective-permute-start.14
  252.0 29.0 %all-to-all-done.2 = bf16[32,24,2048]{2,1,0:T(8,128)(2,1)} async-done(((bf16[32,24,2048]{2,1,0:T(8,128)(2,1)}), bf16[32,24,2048]{2,1,0:T(8,128)(2,1)}, u32[]{:S(2)}, u32[]{:S(2)}) %all-to-all-start.2) | async-done | bytes 3145760 | tf_op jit(solution)/shard_map/all_to_all | solution.py:234
  281.0 2.9 fusion.19
  284.0 4.3 %collective-permute-start.11 = (bf16[32,2048]{1,0:T(8,128)(2,1)S(1)}, bf16[32,2048]{1,0:T(8,128)(2,1)S(1)}, u32[]{:S(2)}, u32[]{:S(2)}) collective-permute-start(bf16[32,2048]{1,0:T(8,128)(2,1)S(1)} %get-tuple-element.13), channel_id=1, source_target_pairs={{0,2},{2,0},{1,3},{3,1},{4,6},{6,4},{5,7},{7,5},{8,10},{10,8},{9,1... | collective-permute-start | bytes 393224 | tf_op jit(solution)/shard_map/ppermute | solution.py:181
  288.3 3.0 collective-permute-start.12
  291.3 22.7 %collective-permute-done.16 = bf16[1,192,4096]{2,1,0:T(8,128)(2,1)} collective-permute-done((bf16[1,192,4096]{2,1,0:T(8,128)(2,1)}, bf16[1,192,4096]{2,1,0:T(8,128)(2,1)}, u32[]{:S(2)}, u32[]{:S(2)}) %collective-permute-start.16) | collective-permute-done | bytes 1572896 | tf_op jit(solution)/shard_map/ppermute | solution.py:267
  314.0 5.1 %collective-permute-start.13 = (bf16[32,2048]{1,0:T(8,128)(2,1)S(1)}, bf16[32,2048]{1,0:T(8,128)(2,1)S(1)}, u32[]{:S(2)}, u32[]{:S(2)}) collective-permute-start(bf16[32,2048]{1,0:T(8,128)(2,1)S(1)} %get-tuple-element.14), channel_id=1, source_target_pairs={{0,130},{2,128},{128,2},{130,0},{1,131},{3,129},{129,3},{131,1},{4... | collective-permute-start | bytes 393224 | tf_op jit(solution)/shard_map/ppermute | solution.py:181
  321.2 37.8 %collective-permute-done.15.got = bf16[256,4096]{1,0:T(8,128)(2,1)} collective-permute-done((bf16[256,4096]{1,0:T(8,128)(2,1)}, bf16[256,4096]{1,0:T(8,128)(2,1)}, u32[]{:S(2)}, u32[]{:S(2)}) %collective-permute-start.15) | collective-permute-done | bytes 2097184 | tf_op jit(solution)/shard_map/ppermute | solution.py:287
  359.0 4.1 %put.2.refs_0_ = bf16[384,4096]{1,0:T(8,128)(2,1)} custom-call(s32[1]{0:T(128)} %bitcast.12.moving, bf16[256,4096]{1,0:T(8,128)(2,1)} %collective-permute-done.15.got, bf16[384,4096]{1,0:T(8,128)(2,1)} %bitcast.23), custom_call_target="tpu_custom_call" | custom-call | bytes 6291456 | tf_op jit(solution)/shard_map/put/pallas_call | solution.py:162
  363.1 18.2 %collective-permute-done.14.got = bf16[128,4096]{1,0:T(8,128)(2,1)S(1)} collective-permute-done((bf16[128,4096]{1,0:T(8,128)(2,1)}, bf16[128,4096]{1,0:T(8,128)(2,1)S(1)}, u32[]{:S(2)}, u32[]{:S(2)}) %collective-permute-start.14) | collective-permute-done | bytes 1048608 | tf_op jit(solution)/shard_map/ppermute | solution.py:288
  (67 shorter events, 23.3 us)
Async XLA Ops:
  4.1 12.0 %collective-permute-start = (bf16[32,2176]{1,0:T(8,128)(2,1)S(1)}, bf16[32,2176]{1,0:T(8,128)(2,1)S(1)}, u32[]{:S(2)}, u32[]{:S(2)}) collective-permute-start(bf16[32,2176]{1,0:T(8,128)(2,1)S(1)} %concatenate.25), channel_id=1, source_target_pairs={{0,2},{2,0},{1,3},{3,1},{4,6},{6,4},{5,7},{7,5},{8,10},{10,8},{9,1... | collective-permute-start | bytes 417800 | tf_op jit(solution)/shard_map/ppermute | solution.py:181
  9.3 11.7 %collective-permute-start.1 = (bf16[32,2176]{1,0:T(8,128)(2,1)S(1)}, bf16[32,2176]{1,0:T(8,128)(2,1)S(1)}, u32[]{:S(2)}, u32[]{:S(2)}) collective-permute-start(bf16[32,2176]{1,0:T(8,128)(2,1)S(1)} %concatenate.25), channel_id=1, source_target_pairs={{0,128},{128,0},{1,129},{129,1},{2,130},{130,2},{3,131},{131,3},{4... | collective-permute-start | bytes 417800 | tf_op jit(solution)/shard_map/ppermute | solution.py:181
  10.5 11.9 %collective-permute-start.2 = (bf16[32,2176]{1,0:T(8,128)(2,1)S(1)}, bf16[32,2176]{1,0:T(8,128)(2,1)S(1)}, u32[]{:S(2)}, u32[]{:S(2)}) collective-permute-start(bf16[32,2176]{1,0:T(8,128)(2,1)S(1)} %concatenate.25), channel_id=1, source_target_pairs={{0,130},{2,128},{128,2},{130,0},{1,131},{3,129},{129,3},{131,1},{4... | collective-permute-start | bytes 417800 | tf_op jit(solution)/shard_map/ppermute | solution.py:181
  23.5 1.0 copy-start.3
  27.5 8.4 %copy-start = (bf16[1,2,192,4096]{3,2,1,0:T(8,128)(2,1)S(1)}, bf16[1,2,192,4096]{3,2,1,0:T(8,128)(2,1)}, u32[]{:S(2)}) copy-start(bf16[1,2,192,4096]{3,2,1,0:T(8,128)(2,1)} %refs_1_.1) | copy-start | bytes 9437188
  27.5 92.4 %all-to-all-start.1 = ((bf16[32,24,2048]{2,1,0:T(8,128)(2,1)}), bf16[32,24,2048]{2,1,0:T(8,128)(2,1)}, u32[]{:S(2)}, u32[]{:S(2)}) async-start(bf16[32,24,2048]{2,1,0:T(8,128)(2,1)} %bitcast.28), calls=%async_computation.1 | async-start | bytes 6291456 | tf_op jit(solution)/shard_map/all_to_all | solution.py:234
  35.9 100.1 %collective-permute-start.6 = (bf16[1,2,192,4096]{3,2,1,0:T(8,128)(2,1)S(1)}, bf16[1,2,192,4096]{3,2,1,0:T(8,128)(2,1)}, u32[]{:S(2)}, u32[]{:S(2)}) collective-permute-start(bf16[1,2,192,4096]{3,2,1,0:T(8,128)(2,1)S(1)} %copy-done), channel_id=1, source_target_pairs={{0,64},{64,0},{1,65},{65,1},{2,66},{66,2},{3,67},{67,3},{4,68},{68... | collective-permute-start | bytes 9437192 | tf_op jit(solution)/shard_map/ppermute | solution.py:181
  37.0 79.3 %collective-permute-start.3 = (bf16[32,2048]{1,0:T(8,128)(2,1)}, bf16[32,2048]{1,0:T(8,128)(2,1)S(1)}, u32[]{:S(2)}, u32[]{:S(2)}) collective-permute-start(bf16[32,2048]{1,0:T(8,128)(2,1)} %get-tuple-element.16), channel_id=1, source_target_pairs={{0,2},{2,0},{1,3},{3,1},{4,6},{6,4},{5,7},{7,5},{8,10},{10,8},{9,1... | collective-permute-start | bytes 393224 | tf_op jit(solution)/shard_map/ppermute | solution.py:181
  40.7 75.6 %collective-permute-start.4 = (bf16[32,2048]{1,0:T(8,128)(2,1)}, bf16[32,2048]{1,0:T(8,128)(2,1)S(1)}, u32[]{:S(2)}, u32[]{:S(2)}) collective-permute-start(bf16[32,2048]{1,0:T(8,128)(2,1)} %get-tuple-element.16), channel_id=1, source_target_pairs={{0,128},{128,0},{1,129},{129,1},{2,130},{130,2},{3,131},{131,3},{4... | collective-permute-start | bytes 393224 | tf_op jit(solution)/shard_map/ppermute | solution.py:181
  42.3 74.0 %collective-permute-start.5 = (bf16[32,2048]{1,0:T(8,128)(2,1)}, bf16[32,2048]{1,0:T(8,128)(2,1)S(1)}, u32[]{:S(2)}, u32[]{:S(2)}) collective-permute-start(bf16[32,2048]{1,0:T(8,128)(2,1)} %get-tuple-element.16), channel_id=1, source_target_pairs={{0,130},{2,128},{128,2},{130,0},{1,131},{3,129},{129,3},{131,1},{4... | collective-permute-start | bytes 393224 | tf_op jit(solution)/shard_map/ppermute | solution.py:181
  119.9 49.1 %all-to-all-start = ((bf16[32,24,2048]{2,1,0:T(8,128)(2,1)}), bf16[32,24,2048]{2,1,0:T(8,128)(2,1)}, u32[]{:S(2)}, u32[]{:S(2)}) async-start(bf16[32,24,2048]{2,1,0:T(8,128)(2,1)} %bitcast.27), calls=%async_computation | async-start | bytes 6291456 | tf_op jit(solution)/shard_map/all_to_all | solution.py:234
  132.0 52.8 %collective-permute-start.10 = (bf16[192,2048]{1,0:T(8,128)(2,1)}, bf16[192,2048]{1,0:T(8,128)(2,1)}, u32[]{:S(2)}, u32[]{:S(2)}) collective-permute-start(bf16[192,2048]{1,0:T(8,128)(2,1)} %get-tuple-element.9), channel_id=1, source_target_pairs={{0,192},{64,128},{128,64},{192,0},{1,193},{65,129},{129,65},{193,1... | collective-permute-start | bytes 2359304 | tf_op jit(solution)/shard_map/ppermute | solution.py:181
  132.4 80.1 %collective-permute-start.9 = (bf16[192,2048]{1,0:T(8,128)(2,1)}, bf16[192,2048]{1,0:T(8,128)(2,1)}, u32[]{:S(2)}, u32[]{:S(2)}) collective-permute-start(bf16[192,2048]{1,0:T(8,128)(2,1)} %get-tuple-element.9), channel_id=1, source_target_pairs={{0,128},{128,0},{1,129},{129,1},{2,130},{130,2},{3,131},{131,3},{4... | collective-permute-start | bytes 2359304 | tf_op jit(solution)/shard_map/ppermute | solution.py:181
  136.0 51.3 %collective-permute-start.8 = (bf16[192,2048]{1,0:T(8,128)(2,1)}, bf16[192,2048]{1,0:T(8,128)(2,1)}, u32[]{:S(2)}, u32[]{:S(2)}) collective-permute-start(bf16[192,2048]{1,0:T(8,128)(2,1)} %get-tuple-element.10.w0), channel_id=1, source_target_pairs={{0,64},{64,0},{1,65},{65,1},{2,66},{66,2},{3,67},{67,3},{4,68},{68... | collective-permute-start | bytes 2359304 | tf_op jit(solution)/shard_map/ppermute | solution.py:181
  177.5 47.6 %collective-permute-start.7 = (bf16[768,384]{1,0:T(8,128)(2,1)}, bf16[768,384]{1,0:T(8,128)(2,1)S(1)}, u32[]{:S(2)}, u32[]{:S(2)}) collective-permute-start(bf16[768,384]{1,0:T(8,128)(2,1)} %up_last.1.hid_a), channel_id=1, source_target_pairs={{0,128},{128,0},{1,129},{129,1},{2,130},{130,2},{3,131},{131,3},{4... | collective-permute-start | bytes 1769480 | tf_op jit(solution)/shard_map/ppermute | solution.py:181
  225.1 0.8 copy-start.6
  232.7 11.5 %copy-start.1 = (bf16[1,2,192,4096]{3,2,1,0:T(8,128)(2,1)S(1)}, bf16[1,2,192,4096]{3,2,1,0:T(8,128)(2,1)}, u32[]{:S(2)}) copy-start(bf16[1,2,192,4096]{3,2,1,0:T(8,128)(2,1)} %refs_1_.1) | copy-start | bytes 9437188
  232.7 48.3 %all-to-all-start.2 = ((bf16[32,24,2048]{2,1,0:T(8,128)(2,1)}), bf16[32,24,2048]{2,1,0:T(8,128)(2,1)}, u32[]{:S(2)}, u32[]{:S(2)}) async-start(bf16[32,24,2048]{2,1,0:T(8,128)(2,1)} %bitcast.30), calls=%async_computation.2 | async-start | bytes 6291456 | tf_op jit(solution)/shard_map/all_to_all | solution.py:234
  241.2 72.9 %collective-permute-start.16 = (bf16[1,192,4096]{2,1,0:T(8,128)(2,1)}, bf16[1,192,4096]{2,1,0:T(8,128)(2,1)}, u32[]{:S(2)}, u32[]{:S(2)}) collective-permute-start(bf16[1,192,4096]{2,1,0:T(8,128)(2,1)} %param.10), channel_id=1, source_target_pairs={{0,32},{16,48},{32,0},{48,16},{1,33},{17,49},{33,1},{49,17},{2,34}... | collective-permute-start | bytes 4718600 | tf_op jit(solution)/shard_map/ppermute | solution.py:267
  244.1 5.5 %copy-start.5 = (s32[8,2]{0,1:T(2,128)S(1)}, s32[8,2]{0,1:T(2,128)}, u32[]{:S(2)}) copy-start(s32[8,2]{0,1:T(2,128)} %param.11) | copy-start | bytes 196
  245.6 113.4 %collective-permute-start.15 = (bf16[256,4096]{1,0:T(8,128)(2,1)}, bf16[256,4096]{1,0:T(8,128)(2,1)}, u32[]{:S(2)}, u32[]{:S(2)}) collective-permute-start(bf16[256,4096]{1,0:T(8,128)(2,1)} %slice.97), channel_id=1, source_target_pairs={{0,32},{16,48},{32,0},{48,16},{1,33},{17,49},{33,1},{49,17},{2,34}... | collective-permute-start | bytes 6291464 | tf_op jit(solution)/shard_map/ppermute | solution.py:287
  246.8 134.6 %collective-permute-start.14 = (bf16[128,4096]{1,0:T(8,128)(2,1)}, bf16[128,4096]{1,0:T(8,128)(2,1)S(1)}, u32[]{:S(2)}, u32[]{:S(2)}) collective-permute-start(bf16[128,4096]{1,0:T(8,128)(2,1)} %slice.96), channel_id=1, source_target_pairs={{0,32},{16,48},{32,0},{48,16},{1,33},{17,49},{33,1},{49,17},{2,34}... | collective-permute-start | bytes 3145736 | tf_op jit(solution)/shard_map/ppermute | solution.py:288
  283.8 35.3 %copy-start.2 = (bf16[1,192,4096]{2,1,0:T(8,128)(2,1)S(1)}, bf16[1,192,4096]{2,1,0:T(8,128)(2,1)}, u32[]{:S(2)}) copy-start(bf16[1,192,4096]{2,1,0:T(8,128)(2,1)} %param.10) | copy-start | bytes 4718596
  284.0 100.6 %collective-permute-start.11 = (bf16[32,2048]{1,0:T(8,128)(2,1)S(1)}, bf16[32,2048]{1,0:T(8,128)(2,1)S(1)}, u32[]{:S(2)}, u32[]{:S(2)}) collective-permute-start(bf16[32,2048]{1,0:T(8,128)(2,1)S(1)} %get-tuple-element.13), channel_id=1, source_target_pairs={{0,2},{2,0},{1,3},{3,1},{4,6},{6,4},{5,7},{7,5},{8,10},{10,8},{9,1... | collective-permute-start | bytes 393224 | tf_op jit(solution)/shard_map/ppermute | solution.py:181
  288.3 96.3 %collective-permute-start.12 = (bf16[32,2048]{1,0:T(8,128)(2,1)S(1)}, bf16[32,2048]{1,0:T(8,128)(2,1)S(1)}, u32[]{:S(2)}, u32[]{:S(2)}) collective-permute-start(bf16[32,2048]{1,0:T(8,128)(2,1)S(1)} %get-tuple-element.15), channel_id=1, source_target_pairs={{0,128},{128,0},{1,129},{129,1},{2,130},{130,2},{3,131},{131,3},{4... | collective-permute-start | bytes 393224 | tf_op jit(solution)/shard_map/ppermute | solution.py:181
  314.0 70.7 %collective-permute-start.13 = (bf16[32,2048]{1,0:T(8,128)(2,1)S(1)}, bf16[32,2048]{1,0:T(8,128)(2,1)S(1)}, u32[]{:S(2)}, u32[]{:S(2)}) collective-permute-start(bf16[32,2048]{1,0:T(8,128)(2,1)S(1)} %get-tuple-element.14), channel_id=1, source_target_pairs={{0,130},{2,128},{128,2},{130,0},{1,131},{3,129},{129,3},{131,1},{4... | collective-permute-start | bytes 393224 | tf_op jit(solution)/shard_map/ppermute | solution.py:181
  381.3 1.0 copy-start.4

commit v3 on v2

--- a/solution.py
+++ b/solution.py
@@ -11,82 +11,42 @@
 CAP = 3
 CHUNK = 1024
 META = 128
-HEAD = 256
-TILE = 256
+HEAD = 288
 PLANE = ("x", "y", "c")
 
 
-def over_tiles(rows, body):
-    def wrapped(m, carry):
-        body(pl.ds(pl.multiple_of(m * TILE, TILE), TILE))
-        return carry
-
-    lax.fori_loop(0, rows // TILE, wrapped, 0)
-
-
-def up_first_kernel(x_ref, gu_a, gu_b, acc):
-    step = pl.program_id(0)
+def project(x, gu_a, gu_b):
     weights = jnp.concatenate([gu_a[0, 0], gu_b[0, 0], gu_a[0, 1], gu_b[0, 1]], axis=0)
-
-    def body(at):
-        part = lax.dot_general(
-            x_ref[at, :], weights, (((1,), (1,)), ((), ())), preferred_element_type=F32
-        )
-
-        @pl.when(step == 0)
-        def _():
-            acc[at, :] = part
-
-        @pl.when(step > 0)
-        def _():
-            acc[at, :] += part
-
-    over_tiles(x_ref.shape[0], body)
-
-
-def up_last_kernel(n_in, x_ref, gu_a, gu_b, start, hid, acc):
-    step = pl.program_id(0)
+    return lax.dot_general(x[...], weights, (((1,), (1,)), ((), ())), preferred_element_type=F32)
+
+
+def up_first_kernel(x_ref, gu_a, gu_b, out):
+    out[...] = project(x_ref, gu_a, gu_b)
+
+
+def up_last_kernel(x_ref, gu_a, gu_b, start, hid):
     units = hid.shape[1]
-    weights = jnp.concatenate([gu_a[0, 0], gu_b[0, 0], gu_a[0, 1], gu_b[0, 1]], axis=0)
-
-    def body(at):
-        part = lax.dot_general(
-            x_ref[at, :], weights, (((1,), (1,)), ((), ())), preferred_element_type=F32
-        )
-
-        @pl.when(step == 0)
-        def _():
-            acc[at, :] = start[at, :] + part
-
-        @pl.when(step > 0)
-        def _():
-            acc[at, :] += part
-
-        @pl.when(step == n_in - 1)
-        def _():
-            gate = acc[at, :units]
-            hid[at, :] = (gate / (1.0 + jnp.exp(-gate)) * acc[at, units:]).astype(BF16)
-
-    over_tiles(x_ref.shape[0], body)
-
-
-def up(x, gu_a, gu_b, at_col, start=None):
+    value = start[...] + project(x_ref, gu_a, gu_b)
+    gate = value[:, :units]
+    hid[...] = (gate / (1.0 + jnp.exp(-gate)) * value[:, units:]).astype(BF16)
+
+
+def up(x, gu_a, gu_b, at, start=None):
     rows, depth = x.shape
     units = gu_a.shape[2]
-    n_in = depth // CHUNK
-    base = at_col // CHUNK
-    gu_spec = pl.BlockSpec((1, 2, units, CHUNK), lambda i: (0, 0, 0, base + i))
-    specs = [pl.BlockSpec((rows, CHUNK), lambda i: (0, i)), gu_spec, gu_spec]
+    tile = rows // 2
+    gu_spec = pl.BlockSpec((1, 2, units, depth), lambda i: (0, 0, 0, at // depth))
+    wide = pl.BlockSpec((tile, 4 * units), lambda i: (i, 0))
+    specs = [pl.BlockSpec((tile, depth), lambda i: (i, 0)), gu_spec, gu_spec]
     cost = pl.CostEstimate(
         flops=2 * rows * depth * units * 4,
         bytes_accessed=2 * rows * depth + 8 * units * depth + 16 * rows * units,
         transcendentals=0,
     )
-    wide = pl.BlockSpec((rows, 4 * units), lambda i: (0, 0))
     if start is None:
         return pl.pallas_call(
             up_first_kernel,
-            grid=(n_in,),
+            grid=(2,),
             in_specs=specs,
             out_specs=wide,
             out_shape=jax.ShapeDtypeStruct((rows, 4 * units), F32),
@@ -94,25 +54,20 @@
             name="up_first",
         )(x, gu_a, gu_b)
     return pl.pallas_call(
-        lambda *refs: up_last_kernel(n_in, *refs),
-        grid=(n_in,),
+        up_last_kernel,
+        grid=(2,),
         in_specs=specs + [wide],
-        out_specs=pl.BlockSpec((rows, 2 * units), lambda i: (0, 0)),
+        out_specs=pl.BlockSpec((tile, 2 * units), lambda i: (i, 0)),
         out_shape=jax.ShapeDtypeStruct((rows, 2 * units), BF16),
-        scratch_shapes=[pltpu.VMEM((rows, 4 * units), F32)],
         cost_estimate=cost,
         name="up_last",
     )(x, gu_a, gu_b, start)
 
 
 def down_kernel(hid_a, hid_b, w0, w1, w2, w3, out_ref):
+    hidden = jnp.concatenate([hid_a[...], hid_b[...]], axis=1)
     weights = jnp.concatenate([w0[...], w1[...], w2[...], w3[...]], axis=0)
-
-    def body(at):
-        hidden = jnp.concatenate([hid_a[at, :], hid_b[at, :]], axis=1)
-        out_ref[at, :] = jnp.dot(hidden, weights, preferred_element_type=F32).astype(BF16)
-
-    over_tiles(hid_a.shape[0], body)
+    out_ref[...] = jnp.dot(hidden, weights, preferred_element_type=F32).astype(BF16)
 
 
 def down(hid_a, hid_b, pieces):
@@ -148,7 +103,7 @@
 
 
 def put(moving, got, own, first, base=None):
-    block = 64
+    block = 96
     depth = own.shape[1]
     start = first // block
     here = pl.BlockSpec((block, depth), lambda i, m: (start + i, 0))
@@ -240,6 +195,7 @@
     steps, rows, depth = tokens.shape
     tops = expert_ids.shape[2]
     half = depth // 2
+    late = depth - CHUNK
     plane = lax.axis_index("h")
     q_high = lax.axis_index("qh")
     slot = (
@@ -255,7 +211,7 @@
     low = gates - high
     first = jnp.concatenate(
         [
-            flat[:, :half],
+            flat[:, late:],
             expert_ids.reshape(own, tops).astype(BF16),
             high.astype(BF16),
             low.astype(BF16),
@@ -266,22 +222,24 @@
     across_x = [(i, i ^ 2) for i in range(4)]
     got_dn = lax.ppermute(down_proj, ("x",), across_x)
     held0 = column(first)
-    held1 = column(flat[:, half:])
+    held1 = column(flat[:, :late])
     gu_b = swap(gate_up, ("ql",))
     mine = lax.dynamic_slice_in_dim(down_proj[0], q_high * half, half, axis=1)
     theirs = lax.dynamic_slice_in_dim(down_proj[0], (1 - q_high) * half, half, axis=1)
+    across_piece = swap(theirs, ("qh", "ql"))
+    far_piece = swap(theirs, ("qh",))
     near_piece = swap(mine, ("ql",))
-    pieces = [mine, near_piece, swap(theirs, ("qh",)), swap(theirs, ("qh", "ql"))]
+    pieces = [mine, near_piece, far_piece, across_piece]
 
     pick, mix = tables(
-        held0[:, half:].astype(F32), rows, tops, plane, q_high, experts, slots
-    )
-    packed0 = pack(pick, held0[:, :half])
+        held0[:, CHUNK:].astype(F32), rows, tops, plane, q_high, experts, slots
+    )
+    packed0 = pack(pick, held0[:, :CHUNK])
     x0 = across(packed0, experts)
     packed1 = pack(pick, held1)
     x1 = across(packed1, experts)
-    start = up(x0, gate_up, gu_b, 0)
-    hidden = up(x1, gate_up, gu_b, half, start)
+    start = up(x0, gate_up, gu_b, late)
+    hidden = up(x1, gate_up, gu_b, 0, start)
     hidden_b = swap(hidden, ("qh",))
     table = gate_up.reshape(-1, depth)
     got_gu0 = lax.ppermute(table[:HEAD], ("x",), across_x)

time: 391 us -> 374 us (0.957)
  waiting for transfers between devices: 264 us -> 243 us
  starting transfers between devices: 64.3 us -> 71.6 us
  Pallas kernels: 29.2 us -> 25.1 us
    ppermute x1, waiting for transfers between devices: 37.8 us -> 64.2 us  [local(): got_gu0 = lax.ppermute(table[:HEAD], ('x',), across_x)]
    all_to_all x3, waiting for transfers between devices: 54.5 us -> 30.3 us  [across(): lax.all_to_all(value.reshape(experts, slots // experts, depth), PLANE, 0,...]
    ppermute x1, waiting for transfers between devices: 18.2 us -> 0.01 us  [local(): got_gu1 = lax.ppermute(table[HEAD:], ('x',), across_x)]
    all_to_all x3, starting transfers between devices: 26.3 us -> 37.2 us  [across(): lax.all_to_all(value.reshape(experts, slots // experts, depth), PLANE, 0,...]
    ppermute x14, waiting for transfers between devices: 130 us -> 122 us  [swap(): return lax.ppermute(value, axes, [(i, i ^ count - 1) for i in range(count)])]
  transfers between devices with their start and end apart: 20 -> 20, of which waited for: 13 -> 11; matrix products, arithmetic and copies ran while one was open for 4% -> 4% of each run, Pallas kernels for 6% -> 5%
where the time goes in v3:
time: 374 us; the launch traced here: 369 us
  waiting for transfers between devices  243 us (65%)
  starting transfers between devices  71.6 us (19%)
  Pallas kernels  25.1 us (7%)
  local copies, waits for them, and re-layouts  12.7 us (3%)
  matrix products  8.83 us (2%)
  other arithmetic  6.77 us (2%)
    ppermute x14, waiting for transfers between devices, swap(): return lax.ppermute(value, axes, [(i, i ^ count - 1) for i in range(count)])  122 us
    ppermute x1, waiting for transfers between devices, local(): got_gu0 = lax.ppermute(table[:HEAD], ('x',), across_x)  64.2 us
    all_to_all x3, starting transfers between devices, across(): lax.all_to_all(value.reshape(experts, slots // experts, depth), PLANE, 0,...  37.2 us
    all_to_all x3, waiting for transfers between devices, across(): lax.all_to_all(value.reshape(experts, slots // experts, depth), PLANE, 0,...  30.3 us
    ppermute x14, starting transfers between devices, swap(): return lax.ppermute(value, axes, [(i, i ^ count - 1) for i in range(count)])  28.4 us
    ppermute x1, waiting for transfers between devices, local(): got_dn = lax.ppermute(down_proj, ('x',), across_x)  26.3 us
    pallas_call x1, Pallas kernels, up(): pl.pallas_call(up_last_kernel, grid=(2,), in_specs=specs + [wide], out_sp...  8.29 us
  transfers between devices with their start and end apart: 20, of which 11 were waited for; matrix products, arithmetic and copies ran while one was open for 4% of the time, Pallas kernels for 5%

profile of v3, /device:TPU:65, one launch (start us, length us, event | category | flops | bytes accessed | tf_op | source)
XLA Modules:
  0.0 369.3 jit_solution(7631761498178692504)
XLA Ops:
  3.3 4.3 %collective-permute-start.2 = (bf16[32,1152]{1,0:T(8,128)(2,1)S(1)}, bf16[32,1152]{1,0:T(8,128)(2,1)S(1)}, u32[]{:S(2)}, u32[]{:S(2)}) collective-permute-start(bf16[32,1152]{1,0:T(8,128)(2,1)S(1)} %concatenate.25), channel_id=1, source_target_pairs={{0,130},{2,128},{128,2},{130,0},{1,131},{3,129},{129,3},{131,1},{4... | collective-permute-start | bytes 221192 | tf_op jit(solution)/shard_map/ppermute | solution.py:136
  9.9 3.6 collective-permute-done.1
  13.5 2.6 collective-permute-done
  18.4 1.8 convolution_convert_fusion.1
  20.2 9.9 %all-to-all-start.1 = ((bf16[32,24,1024]{2,1,0:T(8,128)(2,1)}), bf16[32,24,1024]{2,1,0:T(8,128)(2,1)S(1)}, u32[]{:S(2)}, u32[]{:S(2)}) async-start(bf16[32,24,1024]{2,1,0:T(8,128)(2,1)} %bitcast.4), calls=%async_computation.1 | async-start | bytes 3145728 | tf_op jit(solution)/shard_map/all_to_all | solution.py:189
  31.9 3.9 %collective-permute-start.3 = (bf16[32,3072]{1,0:T(8,128)(2,1)S(1)}, bf16[32,3072]{1,0:T(8,128)(2,1)S(1)}, u32[]{:S(2)}, u32[]{:S(2)}) collective-permute-start(bf16[32,3072]{1,0:T(8,128)(2,1)S(1)} %slice.89), channel_id=1, source_target_pairs={{0,2},{2,0},{1,3},{3,1},{4,6},{6,4},{5,7},{7,5},{8,10},{10,8},{9,1... | collective-permute-start | bytes 589832 | tf_op jit(solution)/shard_map/ppermute | solution.py:136
  35.8 7.1 %collective-permute-done.5 = bf16[32,3072]{1,0:T(8,128)(2,1)S(1)} collective-permute-done((bf16[32,3072]{1,0:T(8,128)(2,1)S(1)}, bf16[32,3072]{1,0:T(8,128)(2,1)S(1)}, u32[]{:S(2)}, u32[]{:S(2)}) %collective-permute-start.5) | collective-permute-done | bytes 196640 | tf_op jit(solution)/shard_map/ppermute | solution.py:136
  42.9 4.9 %collective-permute-done.3 = bf16[32,3072]{1,0:T(8,128)(2,1)S(1)} collective-permute-done((bf16[32,3072]{1,0:T(8,128)(2,1)S(1)}, bf16[32,3072]{1,0:T(8,128)(2,1)S(1)}, u32[]{:S(2)}, u32[]{:S(2)}) %collective-permute-start.3) | collective-permute-done | bytes 196640 | tf_op jit(solution)/shard_map/ppermute | solution.py:136
  47.8 3.6 convolution_convert_fusion
  53.9 8.0 %all-to-all-start = ((bf16[32,24,3072]{2,1,0:T(8,128)(2,1)}), bf16[32,24,3072]{2,1,0:T(8,128)(2,1)}, u32[]{:S(2)}, u32[]{:S(2)}) async-start(bf16[32,24,3072]{2,1,0:T(8,128)(2,1)} %bitcast.27), calls=%async_computation | async-start | bytes 9437184 | tf_op jit(solution)/shard_map/all_to_all | solution.py:189
  61.9 5.4 %collective-permute-start.6 = (bf16[1,2,192,4096]{3,2,1,0:T(8,128)(2,1)S(1)}, bf16[1,2,192,4096]{3,2,1,0:T(8,128)(2,1)}, u32[]{:S(2)}, u32[]{:S(2)}) collective-permute-start(bf16[1,2,192,4096]{3,2,1,0:T(8,128)(2,1)S(1)} %copy-done), channel_id=1, source_target_pairs={{0,64},{64,0},{1,65},{65,1},{2,66},{66,2},{3,67},{67,3},{4,68},{68... | collective-permute-start | bytes 9437192 | tf_op jit(solution)/shard_map/ppermute | solution.py:136
  67.3 2.7 dynamic-slice_bitcast_fusion
  71.2 2.3 collective-permute-start.8
  73.5 77.7 %collective-permute-done.6.gu_b = bf16[1,2,192,4096]{3,2,1,0:T(8,128)(2,1)} collective-permute-done((bf16[1,2,192,4096]{3,2,1,0:T(8,128)(2,1)S(1)}, bf16[1,2,192,4096]{3,2,1,0:T(8,128)(2,1)}, u32[]{:S(2)}, u32[]{:S(2)}) %collective-permute-start.6) | collective-permute-done | bytes 3145760 | tf_op jit(solution)/shard_map/ppermute | solution.py:136
  151.3 4.3 %up_first.1.start = f32[768,768]{1,0:T(8,128)} custom-call(bf16[768,1024]{1,0:T(8,128)(2,1)} %bitcast.29, bf16[1,2,192,4096]{3,2,1,0:T(8,128)(2,1)} %gu_a.3, bf16[1,2,192,4096]{3,2,1,0:T(8,128)(2,1)} %collective-permute-done.6.gu_b), custom_call_target="tpu_custom_call" | custom-call | flops 1207959552 | bytes 5505024 | tf_op jit(solution)/shard_map/up_first/pallas_call | solution.py:47
  155.6 8.3 %up_last.1.hid_a = bf16[768,384]{1,0:T(8,128)(2,1)} custom-call(bf16[768,3072]{1,0:T(8,128)(2,1)} %bitcast.3.x_ref, bf16[1,2,192,4096]{3,2,1,0:T(8,128)(2,1)} %gu_a.3, bf16[1,2,192,4096]{3,2,1,0:T(8,128)(2,1)} %collective-permute-done.6.gu_b, f32[768,768]{1,0:T(8,128)} %up_first.1.start), custom_call_target="tpu_custom_call" | custom-call | flops 3623878656 | bytes 11796480 | tf_op jit(solution)/shard_map/up_last/pallas_call | solution.py:56
  163.8 3.1 collective-permute-start.7
  167.0 24.4 %collective-permute-done.8.w1 = bf16[192,2048]{1,0:T(8,128)(2,1)} collective-permute-done((bf16[192,2048]{1,0:T(8,128)(2,1)}, bf16[192,2048]{1,0:T(8,128)(2,1)}, u32[]{:S(2)}, u32[]{:S(2)}) %collective-permute-start.8) | collective-permute-done | bytes 786464 | tf_op jit(solution)/shard_map/ppermute | solution.py:136
  191.4 1.9 collective-permute-done.7.hid_b
  194.2 5.8 %down.1 = bf16[768,2048]{1,0:T(8,128)(2,1)} custom-call(bf16[768,384]{1,0:T(8,128)(2,1)} %up_last.1.hid_a, bf16[768,384]{1,0:T(8,128)(2,1)} %copy-done.8, bf16[192,2048]{1,0:T(8,128)(2,1)} %get-tuple-element.10.w0, bf16[192,2048]{1,0:T(8,128)(2,1)} %collective-permute-done.8.w1, bf16[192,2048]{1,0:T(8,128)(2,1)} %collective-permute-done.9.w2, ...), custom_call_target="tpu_custom_call" | custom-call | flops 2415919104 | bytes 7471104 | tf_op jit(solution)/shard_map/down/pallas_call | solution.py:78
  200.0 19.3 %all-to-all-start.2 = ((bf16[32,24,2048]{2,1,0:T(8,128)(2,1)}), bf16[32,24,2048]{2,1,0:T(8,128)(2,1)}, u32[]{:S(2)}, u32[]{:S(2)}) async-start(bf16[32,24,2048]{2,1,0:T(8,128)(2,1)} %bitcast.30), calls=%async_computation.2 | async-start | bytes 6291456 | tf_op jit(solution)/shard_map/all_to_all | solution.py:189
  219.3 3.0 collective-permute-start.16
  223.3 1.6 slice.97
  224.8 2.9 collective-permute-start.15
  230.0 29.0 %all-to-all-done.2 = bf16[32,24,2048]{2,1,0:T(8,128)(2,1)} async-done(((bf16[32,24,2048]{2,1,0:T(8,128)(2,1)}), bf16[32,24,2048]{2,1,0:T(8,128)(2,1)}, u32[]{:S(2)}, u32[]{:S(2)}) %all-to-all-start.2) | async-done | bytes 3145760 | tf_op jit(solution)/shard_map/all_to_all | solution.py:189
  259.1 2.9 fusion.18
  262.8 2.1 collective-permute-start.13
  265.8 26.3 %collective-permute-done.16 = bf16[1,192,4096]{2,1,0:T(8,128)(2,1)} collective-permute-done((bf16[1,192,4096]{2,1,0:T(8,128)(2,1)}, bf16[1,192,4096]{2,1,0:T(8,128)(2,1)}, u32[]{:S(2)}, u32[]{:S(2)}) %collective-permute-start.16) | collective-permute-done | bytes 1572896 | tf_op jit(solution)/shard_map/ppermute | solution.py:223
  293.3 2.0 broadcast_select_fusion
  295.3 64.2 %collective-permute-done.15.got = bf16[288,4096]{1,0:T(8,128)(2,1)S(1)} collective-permute-done((bf16[288,4096]{1,0:T(8,128)(2,1)}, bf16[288,4096]{1,0:T(8,128)(2,1)S(1)}, u32[]{:S(2)}, u32[]{:S(2)}) %collective-permute-start.15) | collective-permute-done | bytes 2359328 | tf_op jit(solution)/shard_map/ppermute | solution.py:245
  360.8 4.4 %put.2.refs_0_ = bf16[384,4096]{1,0:T(8,128)(2,1)} custom-call(s32[1]{0:T(128)} %bitcast.12.moving, bf16[288,4096]{1,0:T(8,128)(2,1)} %copy-done.5, bf16[384,4096]{1,0:T(8,128)(2,1)} %bitcast.23), custom_call_target="tpu_custom_call" | custom-call | bytes 7077888 | tf_op jit(solution)/shard_map/put/pallas_call | solution.py:117
  365.3 2.3 put.3
  (72 shorter events, 22.5 us)
Async XLA Ops:
  3.3 6.6 %collective-permute-start.2 = (bf16[32,1152]{1,0:T(8,128)(2,1)S(1)}, bf16[32,1152]{1,0:T(8,128)(2,1)S(1)}, u32[]{:S(2)}, u32[]{:S(2)}) collective-permute-start(bf16[32,1152]{1,0:T(8,128)(2,1)S(1)} %concatenate.25), channel_id=1, source_target_pairs={{0,130},{2,128},{128,2},{130,0},{1,131},{3,129},{129,3},{131,1},{4... | collective-permute-start | bytes 221192 | tf_op jit(solution)/shard_map/ppermute | solution.py:136
  7.6 5.8 %collective-permute-start.1 = (bf16[32,1152]{1,0:T(8,128)(2,1)S(1)}, bf16[32,1152]{1,0:T(8,128)(2,1)S(1)}, u32[]{:S(2)}, u32[]{:S(2)}) collective-permute-start(bf16[32,1152]{1,0:T(8,128)(2,1)S(1)} %concatenate.25), channel_id=1, source_target_pairs={{0,128},{128,0},{1,129},{129,1},{2,130},{130,2},{3,131},{131,3},{4... | collective-permute-start | bytes 221192 | tf_op jit(solution)/shard_map/ppermute | solution.py:136
  8.8 7.2 %collective-permute-start = (bf16[32,1152]{1,0:T(8,128)(2,1)S(1)}, bf16[32,1152]{1,0:T(8,128)(2,1)S(1)}, u32[]{:S(2)}, u32[]{:S(2)}) collective-permute-start(bf16[32,1152]{1,0:T(8,128)(2,1)S(1)} %concatenate.25), channel_id=1, source_target_pairs={{0,2},{2,0},{1,3},{3,1},{4,6},{6,4},{5,7},{7,5},{8,10},{10,8},{9,1... | collective-permute-start | bytes 221192 | tf_op jit(solution)/shard_map/ppermute | solution.py:136
  17.1 1.0 copy-start.4
  20.2 9.9 %copy-start.6 = (bf16[2,16,4096]{2,1,0:T(8,128)(2,1)S(1)}, bf16[2,16,4096]{2,1,0:T(8,128)(2,1)}, u32[]{:S(2)}) copy-start(bf16[2,16,4096]{2,1,0:T(8,128)(2,1)} %param.6) | copy-start | bytes 786436
  20.2 32.6 %all-to-all-start.1 = ((bf16[32,24,1024]{2,1,0:T(8,128)(2,1)}), bf16[32,24,1024]{2,1,0:T(8,128)(2,1)S(1)}, u32[]{:S(2)}, u32[]{:S(2)}) async-start(bf16[32,24,1024]{2,1,0:T(8,128)(2,1)} %bitcast.4), calls=%async_computation.1 | async-start | bytes 3145728 | tf_op jit(solution)/shard_map/all_to_all | solution.py:189
  30.1 12.8 %collective-permute-start.5 = (bf16[32,3072]{1,0:T(8,128)(2,1)S(1)}, bf16[32,3072]{1,0:T(8,128)(2,1)S(1)}, u32[]{:S(2)}, u32[]{:S(2)}) collective-permute-start(bf16[32,3072]{1,0:T(8,128)(2,1)S(1)} %slice.89), channel_id=1, source_target_pairs={{0,130},{2,128},{128,2},{130,0},{1,131},{3,129},{129,3},{131,1},{4... | collective-permute-start | bytes 589832 | tf_op jit(solution)/shard_map/ppermute | solution.py:136
  30.7 12.2 %collective-permute-start.4 = (bf16[32,3072]{1,0:T(8,128)(2,1)S(1)}, bf16[32,3072]{1,0:T(8,128)(2,1)S(1)}, u32[]{:S(2)}, u32[]{:S(2)}) collective-permute-start(bf16[32,3072]{1,0:T(8,128)(2,1)S(1)} %slice.89), channel_id=1, source_target_pairs={{0,128},{128,0},{1,129},{129,1},{2,130},{130,2},{3,131},{131,3},{4... | collective-permute-start | bytes 589832 | tf_op jit(solution)/shard_map/ppermute | solution.py:136
  31.9 15.9 %collective-permute-start.3 = (bf16[32,3072]{1,0:T(8,128)(2,1)S(1)}, bf16[32,3072]{1,0:T(8,128)(2,1)S(1)}, u32[]{:S(2)}, u32[]{:S(2)}) collective-permute-start(bf16[32,3072]{1,0:T(8,128)(2,1)S(1)} %slice.89), channel_id=1, source_target_pairs={{0,2},{2,0},{1,3},{3,1},{4,6},{6,4},{5,7},{7,5},{8,10},{10,8},{9,1... | collective-permute-start | bytes 589832 | tf_op jit(solution)/shard_map/ppermute | solution.py:136
  52.7 1.1 copy-start.3
  53.9 8.0 %copy-start = (bf16[1,2,192,4096]{3,2,1,0:T(8,128)(2,1)S(1)}, bf16[1,2,192,4096]{3,2,1,0:T(8,128)(2,1)}, u32[]{:S(2)}) copy-start(bf16[1,2,192,4096]{3,2,1,0:T(8,128)(2,1)} %gu_a.3) | copy-start | bytes 9437188
  53.9 101.7 %all-to-all-start = ((bf16[32,24,3072]{2,1,0:T(8,128)(2,1)}), bf16[32,24,3072]{2,1,0:T(8,128)(2,1)}, u32[]{:S(2)}, u32[]{:S(2)}) async-start(bf16[32,24,3072]{2,1,0:T(8,128)(2,1)} %bitcast.27), calls=%async_computation | async-start | bytes 9437184 | tf_op jit(solution)/shard_map/all_to_all | solution.py:189
  61.9 89.4 %collective-permute-start.6 = (bf16[1,2,192,4096]{3,2,1,0:T(8,128)(2,1)S(1)}, bf16[1,2,192,4096]{3,2,1,0:T(8,128)(2,1)}, u32[]{:S(2)}, u32[]{:S(2)}) collective-permute-start(bf16[1,2,192,4096]{3,2,1,0:T(8,128)(2,1)S(1)} %copy-done), channel_id=1, source_target_pairs={{0,64},{64,0},{1,65},{65,1},{2,66},{66,2},{3,67},{67,3},{4,68},{68... | collective-permute-start | bytes 9437192 | tf_op jit(solution)/shard_map/ppermute | solution.py:136
  70.0 121.4 %collective-permute-start.9 = (bf16[192,2048]{1,0:T(8,128)(2,1)}, bf16[192,2048]{1,0:T(8,128)(2,1)}, u32[]{:S(2)}, u32[]{:S(2)}) collective-permute-start(bf16[192,2048]{1,0:T(8,128)(2,1)} %get-tuple-element.9), channel_id=1, source_target_pairs={{0,128},{128,0},{1,129},{129,1},{2,130},{130,2},{3,131},{131,3},{4... | collective-permute-start | bytes 2359304 | tf_op jit(solution)/shard_map/ppermute | solution.py:136
  70.8 120.6 %collective-permute-start.10 = (bf16[192,2048]{1,0:T(8,128)(2,1)}, bf16[192,2048]{1,0:T(8,128)(2,1)}, u32[]{:S(2)}, u32[]{:S(2)}) collective-permute-start(bf16[192,2048]{1,0:T(8,128)(2,1)} %get-tuple-element.9), channel_id=1, source_target_pairs={{0,192},{64,128},{128,64},{192,0},{1,193},{65,129},{129,65},{193,1... | collective-permute-start | bytes 2359304 | tf_op jit(solution)/shard_map/ppermute | solution.py:136
  71.2 120.2 %collective-permute-start.8 = (bf16[192,2048]{1,0:T(8,128)(2,1)}, bf16[192,2048]{1,0:T(8,128)(2,1)}, u32[]{:S(2)}, u32[]{:S(2)}) collective-permute-start(bf16[192,2048]{1,0:T(8,128)(2,1)} %get-tuple-element.10.w0), channel_id=1, source_target_pairs={{0,64},{64,0},{1,65},{65,1},{2,66},{66,2},{3,67},{67,3},{4,68},{68... | collective-permute-start | bytes 2359304 | tf_op jit(solution)/shard_map/ppermute | solution.py:136
  163.8 29.5 %collective-permute-start.7 = (bf16[768,384]{1,0:T(8,128)(2,1)}, bf16[768,384]{1,0:T(8,128)(2,1)S(1)}, u32[]{:S(2)}, u32[]{:S(2)}) collective-permute-start(bf16[768,384]{1,0:T(8,128)(2,1)} %up_last.1.hid_a), channel_id=1, source_target_pairs={{0,128},{128,0},{1,129},{129,1},{2,130},{130,2},{3,131},{131,3},{4... | collective-permute-start | bytes 1769480 | tf_op jit(solution)/shard_map/ppermute | solution.py:136
  193.4 0.8 copy-start.8
  200.0 22.3 %copy-start.1 = (bf16[1,2,192,4096]{3,2,1,0:T(8,128)(2,1)S(1)}, bf16[1,2,192,4096]{3,2,1,0:T(8,128)(2,1)}, u32[]{:S(2)}) copy-start(bf16[1,2,192,4096]{3,2,1,0:T(8,128)(2,1)} %gu_a.3) | copy-start | bytes 9437188
  200.0 59.1 %all-to-all-start.2 = ((bf16[32,24,2048]{2,1,0:T(8,128)(2,1)}), bf16[32,24,2048]{2,1,0:T(8,128)(2,1)}, u32[]{:S(2)}, u32[]{:S(2)}) async-start(bf16[32,24,2048]{2,1,0:T(8,128)(2,1)} %bitcast.30), calls=%async_computation.2 | async-start | bytes 6291456 | tf_op jit(solution)/shard_map/all_to_all | solution.py:189
  219.3 72.9 %collective-permute-start.16 = (bf16[1,192,4096]{2,1,0:T(8,128)(2,1)}, bf16[1,192,4096]{2,1,0:T(8,128)(2,1)}, u32[]{:S(2)}, u32[]{:S(2)}) collective-permute-start(bf16[1,192,4096]{2,1,0:T(8,128)(2,1)} %param.10), channel_id=1, source_target_pairs={{0,32},{16,48},{32,0},{48,16},{1,33},{17,49},{33,1},{49,17},{2,34}... | collective-permute-start | bytes 4718600 | tf_op jit(solution)/shard_map/ppermute | solution.py:223
  223.2 4.5 %copy-start.7 = (s32[8,2]{0,1:T(2,128)S(1)}, s32[8,2]{0,1:T(2,128)}, u32[]{:S(2)}) copy-start(s32[8,2]{0,1:T(2,128)} %param.11) | copy-start | bytes 196
  223.2 142.1 %collective-permute-start.14 = (bf16[96,4096]{1,0:T(8,128)(2,1)}, bf16[96,4096]{1,0:T(8,128)(2,1)}, u32[]{:S(2)}, u32[]{:S(2)}) collective-permute-start(bf16[96,4096]{1,0:T(8,128)(2,1)} %slice.96), channel_id=1, source_target_pairs={{0,32},{16,48},{32,0},{48,16},{1,33},{17,49},{33,1},{49,17},{2,34}... | collective-permute-start | bytes 2359304 | tf_op jit(solution)/shard_map/ppermute | solution.py:246
  224.8 134.6 %collective-permute-start.15 = (bf16[288,4096]{1,0:T(8,128)(2,1)}, bf16[288,4096]{1,0:T(8,128)(2,1)S(1)}, u32[]{:S(2)}, u32[]{:S(2)}) collective-permute-start(bf16[288,4096]{1,0:T(8,128)(2,1)} %slice.97), channel_id=1, source_target_pairs={{0,32},{16,48},{32,0},{48,16},{1,33},{17,49},{33,1},{49,17},{2,34}... | collective-permute-start | bytes 7077896 | tf_op jit(solution)/shard_map/ppermute | solution.py:245
  261.9 31.4 %copy-start.2 = (bf16[1,192,4096]{2,1,0:T(8,128)(2,1)S(1)}, bf16[1,192,4096]{2,1,0:T(8,128)(2,1)}, u32[]{:S(2)}) copy-start(bf16[1,192,4096]{2,1,0:T(8,128)(2,1)} %param.10) | copy-start | bytes 4718596
  262.8 104.7 %collective-permute-start.13 = (bf16[32,2048]{1,0:T(8,128)(2,1)}, bf16[32,2048]{1,0:T(8,128)(2,1)S(1)}, u32[]{:S(2)}, u32[]{:S(2)}) collective-permute-start(bf16[32,2048]{1,0:T(8,128)(2,1)} %get-tuple-element.14), channel_id=1, source_target_pairs={{0,130},{2,128},{128,2},{130,0},{1,131},{3,129},{129,3},{131,1},{4... | collective-permute-start | bytes 393224 | tf_op jit(solution)/shard_map/ppermute | solution.py:136
  264.9 102.6 %collective-permute-start.12 = (bf16[32,2048]{1,0:T(8,128)(2,1)}, bf16[32,2048]{1,0:T(8,128)(2,1)}, u32[]{:S(2)}, u32[]{:S(2)}) collective-permute-start(bf16[32,2048]{1,0:T(8,128)(2,1)} %get-tuple-element.15), channel_id=1, source_target_pairs={{0,128},{128,0},{1,129},{129,1},{2,130},{130,2},{3,131},{131,3},{4... | collective-permute-start | bytes 393224 | tf_op jit(solution)/shard_map/ppermute | solution.py:136
  292.1 75.4 %collective-permute-start.11 = (bf16[32,2048]{1,0:T(8,128)(2,1)}, bf16[32,2048]{1,0:T(8,128)(2,1)}, u32[]{:S(2)}, u32[]{:S(2)}) collective-permute-start(bf16[32,2048]{1,0:T(8,128)(2,1)} %get-tuple-element.13), channel_id=1, source_target_pairs={{0,2},{2,0},{1,3},{3,1},{4,6},{6,4},{5,7},{7,5},{8,10},{10,8},{9,1... | collective-permute-start | bytes 393224 | tf_op jit(solution)/shard_map/ppermute | solution.py:136
  359.4 1.4 copy-start.5

commit v4 on v3

--- a/solution.py
+++ b/solution.py
@@ -11,83 +11,86 @@
 CAP = 3
 CHUNK = 1024
 META = 128
-HEAD = 288
+HEAD = 336
 PLANE = ("x", "y", "c")
 
 
-def project(x, gu_a, gu_b):
-    weights = jnp.concatenate([gu_a[0, 0], gu_b[0, 0], gu_a[0, 1], gu_b[0, 1]], axis=0)
-    return lax.dot_general(x[...], weights, (((1,), (1,)), ((), ())), preferred_element_type=F32)
-
-
-def up_first_kernel(x_ref, gu_a, gu_b, out):
-    out[...] = project(x_ref, gu_a, gu_b)
-
-
-def up_last_kernel(x_ref, gu_a, gu_b, start, hid):
-    units = hid.shape[1]
-    value = start[...] + project(x_ref, gu_a, gu_b)
-    gate = value[:, :units]
-    hid[...] = (gate / (1.0 + jnp.exp(-gate)) * value[:, units:]).astype(BF16)
-
-
-def up(x, gu_a, gu_b, at, start=None):
-    rows, depth = x.shape
-    units = gu_a.shape[2]
+def project(x, table):
+    return [
+        lax.dot_general(x[...], table[0, k], (((1,), (1,)), ((), ())), preferred_element_type=F32)
+        for k in range(2)
+    ]
+
+
+def activate(gate, upper):
+    return (gate / (1.0 + jnp.exp(-gate)) * upper).astype(BF16)
+
+
+def own_first_kernel(x, table, gate, upper):
+    gate[...], upper[...] = project(x, table)
+
+
+def own_last_kernel(x, table, gate, upper, hid):
+    more = project(x, table)
+    hid[...] = activate(gate[...] + more[0], upper[...] + more[1])
+
+
+def other_kernel(x, x_late, table, table_late, hid):
+    one, two = project(x, table), project(x_late, table_late)
+    hid[...] = activate(one[0] + two[0], one[1] + two[1])
+
+
+def row_call(kernel, rows, units, blocks, args, outs):
     tile = rows // 2
-    gu_spec = pl.BlockSpec((1, 2, units, depth), lambda i: (0, 0, 0, at // depth))
-    wide = pl.BlockSpec((tile, 4 * units), lambda i: (i, 0))
-    specs = [pl.BlockSpec((tile, depth), lambda i: (i, 0)), gu_spec, gu_spec]
-    cost = pl.CostEstimate(
-        flops=2 * rows * depth * units * 4,
-        bytes_accessed=2 * rows * depth + 8 * units * depth + 16 * rows * units,
-        transcendentals=0,
-    )
-    if start is None:
-        return pl.pallas_call(
-            up_first_kernel,
-            grid=(2,),
-            in_specs=specs,
-            out_specs=wide,
-            out_shape=jax.ShapeDtypeStruct((rows, 4 * units), F32),
-            cost_estimate=cost,
-            name="up_first",
-        )(x, gu_a, gu_b)
+    whole = [pl.BlockSpec((tile, units), lambda i: (i, 0)) for _ in outs]
+    depth = sum(a.shape[1] for a in args if a.ndim == 2 and a.shape[1] > units)
     return pl.pallas_call(
-        up_last_kernel,
+        kernel,
         grid=(2,),
-        in_specs=specs + [wide],
-        out_specs=pl.BlockSpec((tile, 2 * units), lambda i: (i, 0)),
-        out_shape=jax.ShapeDtypeStruct((rows, 2 * units), BF16),
-        cost_estimate=cost,
-        name="up_last",
-    )(x, gu_a, gu_b, start)
-
-
-def down_kernel(hid_a, hid_b, w0, w1, w2, w3, out_ref):
-    hidden = jnp.concatenate([hid_a[...], hid_b[...]], axis=1)
-    weights = jnp.concatenate([w0[...], w1[...], w2[...], w3[...]], axis=0)
-    out_ref[...] = jnp.dot(hidden, weights, preferred_element_type=F32).astype(BF16)
-
-
-def down(hid_a, hid_b, pieces):
-    rows, units = hid_a.shape
-    shard, depth = pieces[0].shape
-    hid_spec = pl.BlockSpec((rows, units), lambda i: (0, 0))
-    w_spec = pl.BlockSpec((shard, CHUNK), lambda i: (0, i))
+        in_specs=[
+            pl.BlockSpec((1, 2, units, width), lambda i, at=at: (0, 0, 0, at))
+            if arg.ndim == 4
+            else pl.BlockSpec((tile, arg.shape[1]), lambda i: (i, 0))
+            for arg, (width, at) in zip(args, blocks)
+        ],
+        out_specs=whole,
+        out_shape=[jax.ShapeDtypeStruct((rows, units), kind) for kind in outs],
+        cost_estimate=pl.CostEstimate(
+            flops=4 * rows * depth * units,
+            bytes_accessed=2 * rows * depth + 4 * units * depth + 8 * rows * units,
+            transcendentals=0,
+        ),
+    )(*args)
+
+
+def down_kernel(*refs):
+    out_ref = refs[-1]
+    hiddens, weights = refs[:4], refs[4:8]
+    value = jnp.dot(hiddens[0][...], weights[0][...], preferred_element_type=F32)
+    for hidden, weight in zip(hiddens[1:], weights[1:]):
+        value += jnp.dot(hidden[...], weight[...], preferred_element_type=F32)
+    out_ref[...] = value.astype(BF16)
+
+
+def down(hiddens, pieces):
+    rows, units = hiddens[0].shape
+    depth = pieces[0].shape[1]
+    width = depth // 4
+    hid_spec = pl.BlockSpec(memory_space=pltpu.VMEM)
+    w_spec = pl.BlockSpec((units, width), lambda i: (0, i))
     return pl.pallas_call(
         down_kernel,
-        grid=(depth // CHUNK,),
-        in_specs=[hid_spec, hid_spec] + [w_spec] * 4,
-        out_specs=pl.BlockSpec((rows, CHUNK), lambda i: (0, i)),
+        grid=(depth // width,),
+        in_specs=[hid_spec] * 4 + [w_spec] * 4,
+        out_specs=pl.BlockSpec((rows, width), lambda i: (0, i)),
         out_shape=jax.ShapeDtypeStruct((rows, depth), BF16),
         cost_estimate=pl.CostEstimate(
-            flops=2 * rows * depth * units * 2,
-            bytes_accessed=2 * rows * depth + 8 * shard * depth + 4 * rows * units,
+            flops=8 * rows * depth * units,
+            bytes_accessed=2 * rows * depth + 8 * units * depth + 8 * rows * units,
             transcendentals=0,
         ),
         name="down",
-    )(hid_a, hid_b, *pieces)
+    )(*hiddens, *pieces)
 
 
 def put_kernel(moving, got, own, *refs):
@@ -103,7 +106,7 @@
 
 
 def put(moving, got, own, first, base=None):
-    block = 96
+    block = 48
     depth = own.shape[1]
     start = first // block
     here = pl.BlockSpec((block, depth), lambda i, m: (start + i, 0))
@@ -238,13 +241,32 @@
     x0 = across(packed0, experts)
     packed1 = pack(pick, held1)
     x1 = across(packed1, experts)
-    start = up(x0, gate_up, gu_b, late)
-    hidden = up(x1, gate_up, gu_b, 0, start)
-    hidden_b = swap(hidden, ("qh",))
+    units = gate_up.shape[2]
+    partial = row_call(
+        own_first_kernel, slots, units, ((0, 0), (CHUNK, late // CHUNK)), (x0, gate_up), (F32, F32)
+    )
+    (hidden_a,) = row_call(
+        own_last_kernel,
+        slots,
+        units,
+        ((0, 0), (late, 0), (0, 0), (0, 0)),
+        (x1, gate_up, *partial),
+        (BF16,),
+    )
+    got_a = swap(hidden_a, ("qh",))
+    (hidden_b,) = row_call(
+        other_kernel,
+        slots,
+        units,
+        ((0, 0), (0, 0), (CHUNK, late // CHUNK), (late, 0)),
+        (x0, x1, gu_b, gu_b),
+        (BF16,),
+    )
+    got_b = swap(hidden_b, ("qh",))
     table = gate_up.reshape(-1, depth)
     got_gu0 = lax.ppermute(table[:HEAD], ("x",), across_x)
     got_gu1 = lax.ppermute(table[HEAD:], ("x",), across_x)
-    made = down(hidden, hidden_b, pieces)
+    made = down((hidden_a, hidden_b, got_a, got_b), pieces)
     back = across(made, experts)
     both = jnp.dot(mix, back, preferred_element_type=F32)
     mixed = both[: 4 * own] + both[4 * own :]
@@ -257,7 +279,7 @@
         [jnp.where(low_half, near, far), jnp.where(low_half, far, near)], axis=1
     )
     moving = jnp.any(pairs == slot)
-    flag = moving.astype(jnp.int32).reshape(1)
+    flag = jnp.sum((pairs == slot).astype(jnp.int32)).reshape(1)
     new_gu = put(flag, got_gu0, table, 0)
     new_gu = put(flag, got_gu1, table, HEAD, new_gu)
     new_dn = jnp.where(moving, got_dn, down_proj)

time: 374 us -> 367 us (0.981)
  starting transfers between devices: 71.6 us -> 55.3 us
  Pallas kernels: 25.1 us -> 33.4 us
  waiting for transfers between devices: 243 us -> 247 us
    ppermute x14 -> x15, waiting for transfers between devices: 122 us -> 134 us  [swap(): return lax.ppermute(value, axes, [(i, i ^ count - 1) for i in range(count)])]
    all_to_all x3, starting transfers between devices: 37.2 us -> 26.1 us  [across(): lax.all_to_all(value.reshape(experts, slots // experts, depth), PLANE, 0,...]
    ppermute x1, waiting for transfers between devices: 64.2 us -> 55.8 us  [local(): got_gu0 = lax.ppermute(table[:HEAD], ('x',), across_x)]
    pallas_call x3 -> x4, Pallas kernels: 18.3 us -> 24.1 us  [the longest x3 17 us: row_call(): pl.pallas_call(kernel, grid=(2,), in_specs=[pl.BlockSpec((1, 2, units, wi...]
    ppermute x14 -> x15, starting transfers between devices: 28.4 us -> 23.3 us  [swap(): return lax.ppermute(value, axes, [(i, i ^ count - 1) for i in range(count)])]
  transfers between devices with their start and end apart: 20 -> 21, of which waited for: 11 -> 13; matrix products, arithmetic and copies ran while one was open for 4% -> 4% of each run, Pallas kernels for 5% -> 7%
where the time goes in v4:
time: 367 us; the launch traced here: 363 us
  waiting for transfers between devices  247 us (67%)
  starting transfers between devices  55.3 us (15%)
  Pallas kernels  33.4 us (9%)
  local copies, waits for them, and re-layouts  11.3 us (3%)
  matrix products  8.83 us (2%)
  other arithmetic  6.42 us (2%)
    ppermute x15, waiting for transfers between devices, swap(): return lax.ppermute(value, axes, [(i, i ^ count - 1) for i in range(count)])  134 us
    ppermute x1, waiting for transfers between devices, local(): got_gu0 = lax.ppermute(table[:HEAD], ('x',), across_x)  55.8 us
    all_to_all x3, waiting for transfers between devices, across(): lax.all_to_all(value.reshape(experts, slots // experts, depth), PLANE, 0,...  29 us
    ppermute x1, waiting for transfers between devices, local(): got_dn = lax.ppermute(down_proj, ('x',), across_x)  26.6 us
    all_to_all x3, starting transfers between devices, across(): lax.all_to_all(value.reshape(experts, slots // experts, depth), PLANE, 0,...  26.1 us
    ppermute x15, starting transfers between devices, swap(): return lax.ppermute(value, axes, [(i, i ^ count - 1) for i in range(count)])  23.3 us
    pallas_call x3, Pallas kernels, row_call(): pl.pallas_call(kernel, grid=(2,), in_specs=[pl.BlockSpec((1, 2, units, wi...  17 us
    pallas_call x2, Pallas kernels, put(): pl.pallas_call(put_kernel, grid_spec=pltpu.PrefetchScalarGridSpec(num_sca...  9.26 us
  transfers between devices with their start and end apart: 21, of which 13 were waited for; matrix products, arithmetic and copies ran while one was open for 4% of the time, Pallas kernels for 7%

profile of v4, /device:TPU:65, one launch (start us, length us, event | category | flops | bytes accessed | tf_op | source)
XLA Modules:
  0.0 363.4 jit_solution(90090168928063815)
XLA Ops:
  3.3 5.2 %collective-permute-start = (bf16[32,1152]{1,0:T(8,128)(2,1)S(1)}, bf16[32,1152]{1,0:T(8,128)(2,1)S(1)}, u32[]{:S(2)}, u32[]{:S(2)}) collective-permute-start(bf16[32,1152]{1,0:T(8,128)(2,1)S(1)} %concatenate.25), channel_id=1, source_target_pairs={{0,2},{2,0},{1,3},{3,1},{4,6},{6,4},{5,7},{7,5},{8,10},{10,8},{9,1... | collective-permute-start | bytes 221192 | tf_op jit(solution)/shard_map/ppermute | solution.py:139
  9.8 1.9 collective-permute-done
  11.7 3.0 collective-permute-done.1
  19.8 9.8 %all-to-all-start.1 = ((bf16[32,24,1024]{2,1,0:T(8,128)(2,1)}), bf16[32,24,1024]{2,1,0:T(8,128)(2,1)S(1)}, u32[]{:S(2)}, u32[]{:S(2)}) async-start(bf16[32,24,1024]{2,1,0:T(8,128)(2,1)} %bitcast.4), calls=%async_computation.1 | async-start | bytes 3145728 | tf_op jit(solution)/shard_map/all_to_all | solution.py:192
  29.7 2.7 collective-permute-start.3
  33.1 2.3 collective-permute-start.5
  35.4 9.5 %collective-permute-done.3 = bf16[32,3072]{1,0:T(8,128)(2,1)S(1)} collective-permute-done((bf16[32,3072]{1,0:T(8,128)(2,1)S(1)}, bf16[32,3072]{1,0:T(8,128)(2,1)S(1)}, u32[]{:S(2)}, u32[]{:S(2)}) %collective-permute-start.3) | collective-permute-done | bytes 196640 | tf_op jit(solution)/shard_map/ppermute | solution.py:139
  44.9 5.4 %collective-permute-done.4 = bf16[32,3072]{1,0:T(8,128)(2,1)S(1)} collective-permute-done((bf16[32,3072]{1,0:T(8,128)(2,1)S(1)}, bf16[32,3072]{1,0:T(8,128)(2,1)S(1)}, u32[]{:S(2)}, u32[]{:S(2)}) %collective-permute-start.4) | collective-permute-done | bytes 196640 | tf_op jit(solution)/shard_map/ppermute | solution.py:139
  50.4 2.4 collective-permute-done.5
  52.8 3.6 convolution_convert_fusion
  57.5 7.8 %all-to-all-start = ((bf16[32,24,3072]{2,1,0:T(8,128)(2,1)}), bf16[32,24,3072]{2,1,0:T(8,128)(2,1)}, u32[]{:S(2)}, u32[]{:S(2)}) async-start(bf16[32,24,3072]{2,1,0:T(8,128)(2,1)} %bitcast.27), calls=%async_computation | async-start | bytes 9437184 | tf_op jit(solution)/shard_map/all_to_all | solution.py:192
  65.4 2.7 dynamic-slice_bitcast_fusion
  68.2 1.9 collective-permute-start.10
  71.7 3.4 shard_map.85
  75.2 74.6 %collective-permute-done.6.table.table_late = bf16[1,2,192,4096]{3,2,1,0:T(8,128)(2,1)} collective-permute-done((bf16[1,2,192,4096]{3,2,1,0:T(8,128)(2,1)S(1)}, bf16[1,2,192,4096]{3,2,1,0:T(8,128)(2,1)}, u32[]{:S(2)}, u32[]{:S(2)}) %collective-permute-start.6) | collective-permute-done | bytes 3145760 | tf_op jit(solution)/shard_map/ppermute | solution.py:139
  149.7 7.2 %shard_map.87.refs_1_ = bf16[768,192]{1,0:T(8,128)(2,1)} custom-call(bf16[768,1024]{1,0:T(8,128)(2,1)} %bitcast.29, bf16[768,3072]{1,0:T(8,128)(2,1)} %bitcast.3.x.x_late, bf16[1,2,192,4096]{3,2,1,0:T(8,128)(2,1)} %collective-permute-done.6.table.table_late, bf16[1,2,192,4096]{3,2,1,0:T(8,128)(2,1)} %collective-permute-done.6.table.table_late), custom_call_target="tpu_custom_call" | custom-call | flops 2415919104 | bytes 10616832 | tf_op jit(solution)/shard_map/pallas_call | solution.py:47
  157.0 2.8 collective-permute-start.8
  159.8 6.3 %shard_map.86.refs_0_ = bf16[768,192]{1,0:T(8,128)(2,1)} custom-call(bf16[768,3072]{1,0:T(8,128)(2,1)} %bitcast.3.x.x_late, bf16[1,2,192,4096]{3,2,1,0:T(8,128)(2,1)} %table.3, f32[768,192]{1,0:T(8,128)} %get-tuple-element.5.gate, f32[768,192]{1,0:T(8,128)} %get-tuple-element.6.upper), custom_call_target="tpu_custom_call" | custom-call | flops 1811939328 | bytes 8257536 | tf_op jit(solution)/shard_map/pallas_call | solution.py:47
  166.1 34.2 %collective-permute-done.9.refs_5_ = bf16[192,2048]{1,0:T(8,128)(2,1)} collective-permute-done((bf16[192,2048]{1,0:T(8,128)(2,1)}, bf16[192,2048]{1,0:T(8,128)(2,1)}, u32[]{:S(2)}, u32[]{:S(2)}) %collective-permute-start.9) | collective-permute-done | bytes 786464 | tf_op jit(solution)/shard_map/ppermute | solution.py:139
  200.4 2.4 collective-permute-done.7.refs_2_
  203.5 7.1 %down.1 = bf16[768,2048]{1,0:T(8,128)(2,1)} custom-call(bf16[768,192]{1,0:T(8,128)(2,1)} %shard_map.86.refs_0_, bf16[768,192]{1,0:T(8,128)(2,1)} %shard_map.87.refs_1_, bf16[768,192]{1,0:T(8,128)(2,1)} %copy-done.9, bf16[768,192]{1,0:T(8,128)(2,1)} %copy-done.8, bf16[192,2048]{1,0:T(8,128)(2,1)} %get-tuple-element.14.refs_4_, ...), custom_call_target="tpu_custom_call" | custom-call | flops 2415919104 | bytes 7471104 | tf_op jit(solution)/shard_map/down/pallas_call | solution.py:81
  210.7 8.5 %all-to-all-start.2 = ((bf16[32,24,2048]{2,1,0:T(8,128)(2,1)}), bf16[32,24,2048]{2,1,0:T(8,128)(2,1)}, u32[]{:S(2)}, u32[]{:S(2)}) async-start(bf16[32,24,2048]{2,1,0:T(8,128)(2,1)} %bitcast.31), calls=%async_computation.2 | async-start | bytes 6291456 | tf_op jit(solution)/shard_map/all_to_all | solution.py:192
  219.1 3.0 collective-permute-start.17
  224.7 2.9 collective-permute-start.15
  229.9 29.0 %all-to-all-done.2 = bf16[32,24,2048]{2,1,0:T(8,128)(2,1)} async-done(((bf16[32,24,2048]{2,1,0:T(8,128)(2,1)}), bf16[32,24,2048]{2,1,0:T(8,128)(2,1)}, u32[]{:S(2)}, u32[]{:S(2)}) %all-to-all-start.2) | async-done | bytes 3145760 | tf_op jit(solution)/shard_map/all_to_all | solution.py:192
  258.9 2.9 fusion.18
  262.0 2.6 collective-permute-start.12
  265.4 26.6 %collective-permute-done.17 = bf16[1,192,4096]{2,1,0:T(8,128)(2,1)} collective-permute-done((bf16[1,192,4096]{2,1,0:T(8,128)(2,1)}, bf16[1,192,4096]{2,1,0:T(8,128)(2,1)}, u32[]{:S(2)}, u32[]{:S(2)}) %collective-permute-start.17) | collective-permute-done | bytes 1572896 | tf_op jit(solution)/shard_map/ppermute | solution.py:226
  293.3 2.0 broadcast_select_fusion
  295.2 55.8 %collective-permute-done.16.got = bf16[336,4096]{1,0:T(8,128)(2,1)} collective-permute-done((bf16[336,4096]{1,0:T(8,128)(2,1)}, bf16[336,4096]{1,0:T(8,128)(2,1)}, u32[]{:S(2)}, u32[]{:S(2)}) %collective-permute-start.16) | collective-permute-done | bytes 2752544 | tf_op jit(solution)/shard_map/ppermute | solution.py:267
  351.0 6.7 %put.2.refs_0_ = bf16[384,4096]{1,0:T(8,128)(2,1)} custom-call(s32[1]{0:T(128)} %bitcast.12.moving, bf16[336,4096]{1,0:T(8,128)(2,1)} %collective-permute-done.16.got, bf16[384,4096]{1,0:T(8,128)(2,1)} %bitcast.23), custom_call_target="tpu_custom_call" | custom-call | bytes 8257536 | tf_op jit(solution)/shard_map/put/pallas_call | solution.py:120
  360.1 2.5 put.3
  (78 shorter events, 23.7 us)
Async XLA Ops:
  3.3 8.3 %collective-permute-start = (bf16[32,1152]{1,0:T(8,128)(2,1)S(1)}, bf16[32,1152]{1,0:T(8,128)(2,1)S(1)}, u32[]{:S(2)}, u32[]{:S(2)}) collective-permute-start(bf16[32,1152]{1,0:T(8,128)(2,1)S(1)} %concatenate.25), channel_id=1, source_target_pairs={{0,2},{2,0},{1,3},{3,1},{4,6},{6,4},{5,7},{7,5},{8,10},{10,8},{9,1... | collective-permute-start | bytes 221192 | tf_op jit(solution)/shard_map/ppermute | solution.py:139
  8.5 6.1 %collective-permute-start.1 = (bf16[32,1152]{1,0:T(8,128)(2,1)S(1)}, bf16[32,1152]{1,0:T(8,128)(2,1)S(1)}, u32[]{:S(2)}, u32[]{:S(2)}) collective-permute-start(bf16[32,1152]{1,0:T(8,128)(2,1)S(1)} %concatenate.25), channel_id=1, source_target_pairs={{0,128},{128,0},{1,129},{129,1},{2,130},{130,2},{3,131},{131,3},{4... | collective-permute-start | bytes 221192 | tf_op jit(solution)/shard_map/ppermute | solution.py:139
  9.7 6.0 %collective-permute-start.2 = (bf16[32,1152]{1,0:T(8,128)(2,1)S(1)}, bf16[32,1152]{1,0:T(8,128)(2,1)S(1)}, u32[]{:S(2)}, u32[]{:S(2)}) collective-permute-start(bf16[32,1152]{1,0:T(8,128)(2,1)S(1)} %concatenate.25), channel_id=1, source_target_pairs={{0,130},{2,128},{128,2},{130,0},{1,131},{3,129},{129,3},{131,1},{4... | collective-permute-start | bytes 221192 | tf_op jit(solution)/shard_map/ppermute | solution.py:139
  16.8 1.0 copy-start.4
  19.8 9.9 %copy-start.6 = (bf16[2,16,4096]{2,1,0:T(8,128)(2,1)S(1)}, bf16[2,16,4096]{2,1,0:T(8,128)(2,1)}, u32[]{:S(2)}) copy-start(bf16[2,16,4096]{2,1,0:T(8,128)(2,1)} %param.6) | copy-start | bytes 786436
  19.8 36.5 %all-to-all-start.1 = ((bf16[32,24,1024]{2,1,0:T(8,128)(2,1)}), bf16[32,24,1024]{2,1,0:T(8,128)(2,1)S(1)}, u32[]{:S(2)}, u32[]{:S(2)}) async-start(bf16[32,24,1024]{2,1,0:T(8,128)(2,1)} %bitcast.4), calls=%async_computation.1 | async-start | bytes 3145728 | tf_op jit(solution)/shard_map/all_to_all | solution.py:192
  29.7 15.2 %collective-permute-start.3 = (bf16[32,3072]{1,0:T(8,128)(2,1)S(1)}, bf16[32,3072]{1,0:T(8,128)(2,1)S(1)}, u32[]{:S(2)}, u32[]{:S(2)}) collective-permute-start(bf16[32,3072]{1,0:T(8,128)(2,1)S(1)} %slice.89), channel_id=1, source_target_pairs={{0,2},{2,0},{1,3},{3,1},{4,6},{6,4},{5,7},{7,5},{8,10},{10,8},{9,1... | collective-permute-start | bytes 589832 | tf_op jit(solution)/shard_map/ppermute | solution.py:139
  32.5 17.9 %collective-permute-start.4 = (bf16[32,3072]{1,0:T(8,128)(2,1)S(1)}, bf16[32,3072]{1,0:T(8,128)(2,1)S(1)}, u32[]{:S(2)}, u32[]{:S(2)}) collective-permute-start(bf16[32,3072]{1,0:T(8,128)(2,1)S(1)} %slice.89), channel_id=1, source_target_pairs={{0,128},{128,0},{1,129},{129,1},{2,130},{130,2},{3,131},{131,3},{4... | collective-permute-start | bytes 589832 | tf_op jit(solution)/shard_map/ppermute | solution.py:139
  33.1 19.6 %collective-permute-start.5 = (bf16[32,3072]{1,0:T(8,128)(2,1)S(1)}, bf16[32,3072]{1,0:T(8,128)(2,1)S(1)}, u32[]{:S(2)}, u32[]{:S(2)}) collective-permute-start(bf16[32,3072]{1,0:T(8,128)(2,1)S(1)} %slice.89), channel_id=1, source_target_pairs={{0,130},{2,128},{128,2},{130,0},{1,131},{3,129},{129,3},{131,1},{4... | collective-permute-start | bytes 589832 | tf_op jit(solution)/shard_map/ppermute | solution.py:139
  56.4 1.1 copy-start.2
  57.5 7.8 %copy-start = (bf16[1,2,192,4096]{3,2,1,0:T(8,128)(2,1)S(1)}, bf16[1,2,192,4096]{3,2,1,0:T(8,128)(2,1)}, u32[]{:S(2)}) copy-start(bf16[1,2,192,4096]{3,2,1,0:T(8,128)(2,1)} %table.3) | copy-start | bytes 9437188
  57.5 92.2 %all-to-all-start = ((bf16[32,24,3072]{2,1,0:T(8,128)(2,1)}), bf16[32,24,3072]{2,1,0:T(8,128)(2,1)}, u32[]{:S(2)}, u32[]{:S(2)}) async-start(bf16[32,24,3072]{2,1,0:T(8,128)(2,1)} %bitcast.27), calls=%async_computation | async-start | bytes 9437184 | tf_op jit(solution)/shard_map/all_to_all | solution.py:192
  65.3 84.4 %collective-permute-start.6 = (bf16[1,2,192,4096]{3,2,1,0:T(8,128)(2,1)S(1)}, bf16[1,2,192,4096]{3,2,1,0:T(8,128)(2,1)}, u32[]{:S(2)}, u32[]{:S(2)}) collective-permute-start(bf16[1,2,192,4096]{3,2,1,0:T(8,128)(2,1)S(1)} %copy-done), channel_id=1, source_target_pairs={{0,64},{64,0},{1,65},{65,1},{2,66},{66,2},{3,67},{67,3},{4,68},{68... | collective-permute-start | bytes 9437192 | tf_op jit(solution)/shard_map/ppermute | solution.py:139
  68.2 98.0 %collective-permute-start.10 = (bf16[192,2048]{1,0:T(8,128)(2,1)}, bf16[192,2048]{1,0:T(8,128)(2,1)}, u32[]{:S(2)}, u32[]{:S(2)}) collective-permute-start(bf16[192,2048]{1,0:T(8,128)(2,1)} %get-tuple-element.13), channel_id=1, source_target_pairs={{0,128},{128,0},{1,129},{129,1},{2,130},{130,2},{3,131},{131,3},{4... | collective-permute-start | bytes 2359304 | tf_op jit(solution)/shard_map/ppermute | solution.py:139
  70.1 96.0 %collective-permute-start.11 = (bf16[192,2048]{1,0:T(8,128)(2,1)}, bf16[192,2048]{1,0:T(8,128)(2,1)}, u32[]{:S(2)}, u32[]{:S(2)}) collective-permute-start(bf16[192,2048]{1,0:T(8,128)(2,1)} %get-tuple-element.13), channel_id=1, source_target_pairs={{0,192},{64,128},{128,64},{192,0},{1,193},{65,129},{129,65},{193,1... | collective-permute-start | bytes 2359304 | tf_op jit(solution)/shard_map/ppermute | solution.py:139
  70.8 129.6 %collective-permute-start.9 = (bf16[192,2048]{1,0:T(8,128)(2,1)}, bf16[192,2048]{1,0:T(8,128)(2,1)}, u32[]{:S(2)}, u32[]{:S(2)}) collective-permute-start(bf16[192,2048]{1,0:T(8,128)(2,1)} %get-tuple-element.14.refs_4_), channel_id=1, source_target_pairs={{0,64},{64,0},{1,65},{65,1},{2,66},{66,2},{3,67},{67,3},{4,68},{68... | collective-permute-start | bytes 2359304 | tf_op jit(solution)/shard_map/ppermute | solution.py:139
  157.0 43.4 %collective-permute-start.8 = (bf16[768,192]{1,0:T(8,128)(2,1)}, bf16[768,192]{1,0:T(8,128)(2,1)S(1)}, u32[]{:S(2)}, u32[]{:S(2)}) collective-permute-start(bf16[768,192]{1,0:T(8,128)(2,1)} %shard_map.87.refs_1_), channel_id=1, source_target_pairs={{0,128},{128,0},{1,129},{129,1},{2,130},{130,2},{3,131},{131,3},{4... | collective-permute-start | bytes 884744 | tf_op jit(solution)/shard_map/ppermute | solution.py:139
  166.1 36.7 %collective-permute-start.7 = (bf16[768,192]{1,0:T(8,128)(2,1)}, bf16[768,192]{1,0:T(8,128)(2,1)S(1)}, u32[]{:S(2)}, u32[]{:S(2)}) collective-permute-start(bf16[768,192]{1,0:T(8,128)(2,1)} %shard_map.86.refs_0_), channel_id=1, source_target_pairs={{0,128},{128,0},{1,129},{129,1},{2,130},{130,2},{3,131},{131,3},{4... | collective-permute-start | bytes 884744 | tf_op jit(solution)/shard_map/ppermute | solution.py:139
  200.4 2.4 copy-start.8
  202.8 0.8 copy-start.9
  210.7 11.4 %copy-start.1 = (bf16[1,2,192,4096]{3,2,1,0:T(8,128)(2,1)S(1)}, bf16[1,2,192,4096]{3,2,1,0:T(8,128)(2,1)}, u32[]{:S(2)}) copy-start(bf16[1,2,192,4096]{3,2,1,0:T(8,128)(2,1)} %table.3) | copy-start | bytes 9437188
  210.7 48.3 %all-to-all-start.2 = ((bf16[32,24,2048]{2,1,0:T(8,128)(2,1)}), bf16[32,24,2048]{2,1,0:T(8,128)(2,1)}, u32[]{:S(2)}, u32[]{:S(2)}) async-start(bf16[32,24,2048]{2,1,0:T(8,128)(2,1)} %bitcast.31), calls=%async_computation.2 | async-start | bytes 6291456 | tf_op jit(solution)/shard_map/all_to_all | solution.py:192
  219.1 72.9 %collective-permute-start.17 = (bf16[1,192,4096]{2,1,0:T(8,128)(2,1)}, bf16[1,192,4096]{2,1,0:T(8,128)(2,1)}, u32[]{:S(2)}, u32[]{:S(2)}) collective-permute-start(bf16[1,192,4096]{2,1,0:T(8,128)(2,1)} %param.10), channel_id=1, source_target_pairs={{0,32},{16,48},{32,0},{48,16},{1,33},{17,49},{33,1},{49,17},{2,34}... | collective-permute-start | bytes 4718600 | tf_op jit(solution)/shard_map/ppermute | solution.py:226
  222.1 5.5 %copy-start.7 = (s32[8,2]{0,1:T(2,128)S(1)}, s32[8,2]{0,1:T(2,128)}, u32[]{:S(2)}) copy-start(s32[8,2]{0,1:T(2,128)} %param.11) | copy-start | bytes 196
  223.8 127.2 %collective-permute-start.16 = (bf16[336,4096]{1,0:T(8,128)(2,1)}, bf16[336,4096]{1,0:T(8,128)(2,1)}, u32[]{:S(2)}, u32[]{:S(2)}) collective-permute-start(bf16[336,4096]{1,0:T(8,128)(2,1)} %slice.97), channel_id=1, source_target_pairs={{0,32},{16,48},{32,0},{48,16},{1,33},{17,49},{33,1},{49,17},{2,34}... | collective-permute-start | bytes 8257544 | tf_op jit(solution)/shard_map/ppermute | solution.py:267
  224.7 134.6 %collective-permute-start.15 = (bf16[48,4096]{1,0:T(8,128)(2,1)}, bf16[48,4096]{1,0:T(8,128)(2,1)S(1)}, u32[]{:S(2)}, u32[]{:S(2)}) collective-permute-start(bf16[48,4096]{1,0:T(8,128)(2,1)} %slice.96), channel_id=1, source_target_pairs={{0,32},{16,48},{32,0},{48,16},{1,33},{17,49},{33,1},{49,17},{2,34}... | collective-permute-start | bytes 1179656 | tf_op jit(solution)/shard_map/ppermute | solution.py:268
  261.8 31.5 %copy-start.3 = (bf16[1,192,4096]{2,1,0:T(8,128)(2,1)S(1)}, bf16[1,192,4096]{2,1,0:T(8,128)(2,1)}, u32[]{:S(2)}) copy-start(bf16[1,192,4096]{2,1,0:T(8,128)(2,1)} %param.10) | copy-start | bytes 4718596
  262.0 100.6 %collective-permute-start.12 = (bf16[32,2048]{1,0:T(8,128)(2,1)S(1)}, bf16[32,2048]{1,0:T(8,128)(2,1)S(1)}, u32[]{:S(2)}, u32[]{:S(2)}) collective-permute-start(bf16[32,2048]{1,0:T(8,128)(2,1)S(1)} %get-tuple-element.17), channel_id=1, source_target_pairs={{0,2},{2,0},{1,3},{3,1},{4,6},{6,4},{5,7},{7,5},{8,10},{10,8},{9,1... | collective-permute-start | bytes 393224 | tf_op jit(solution)/shard_map/ppermute | solution.py:139
  264.6 98.0 %collective-permute-start.13 = (bf16[32,2048]{1,0:T(8,128)(2,1)S(1)}, bf16[32,2048]{1,0:T(8,128)(2,1)S(1)}, u32[]{:S(2)}, u32[]{:S(2)}) collective-permute-start(bf16[32,2048]{1,0:T(8,128)(2,1)S(1)} %get-tuple-element.19), channel_id=1, source_target_pairs={{0,128},{128,0},{1,129},{129,1},{2,130},{130,2},{3,131},{131,3},{4... | collective-permute-start | bytes 393224 | tf_op jit(solution)/shard_map/ppermute | solution.py:139
  292.0 70.6 %collective-permute-start.14 = (bf16[32,2048]{1,0:T(8,128)(2,1)S(1)}, bf16[32,2048]{1,0:T(8,128)(2,1)S(1)}, u32[]{:S(2)}, u32[]{:S(2)}) collective-permute-start(bf16[32,2048]{1,0:T(8,128)(2,1)S(1)} %get-tuple-element.18), channel_id=1, source_target_pairs={{0,130},{2,128},{128,2},{130,0},{1,131},{3,129},{129,3},{131,1},{4... | collective-permute-start | bytes 393224 | tf_op jit(solution)/shard_map/ppermute | solution.py:139
  359.3 0.8 copy-start.5

commit v5 on v4

--- a/solution.py
+++ b/solution.py
@@ -1,3 +1,5 @@
+import functools
+
 import jax
 import jax.numpy as jnp
 from jax import lax
@@ -13,11 +15,18 @@
 META = 128
 HEAD = 336
 PLANE = ("x", "y", "c")
-
-
-def project(x, table):
+CROSS = ("ql", "h")
+
+
+def project(x, table, at):
+    width = x.shape[1]
     return [
-        lax.dot_general(x[...], table[0, k], (((1,), (1,)), ((), ())), preferred_element_type=F32)
+        lax.dot_general(
+            x[...],
+            table[0, k, :, at : at + width],
+            (((1,), (1,)), ((), ())),
+            preferred_element_type=F32,
+        )
         for k in range(2)
     ]
 
@@ -26,64 +35,72 @@
     return (gate / (1.0 + jnp.exp(-gate)) * upper).astype(BF16)
 
 
-def own_first_kernel(x, table, gate, upper):
-    gate[...], upper[...] = project(x, table)
-
-
-def own_last_kernel(x, table, gate, upper, hid):
-    more = project(x, table)
-    hid[...] = activate(gate[...] + more[0], upper[...] + more[1])
-
-
-def other_kernel(x, x_late, table, table_late, hid):
-    one, two = project(x, table), project(x_late, table_late)
-    hid[...] = activate(one[0] + two[0], one[1] + two[1])
-
-
-def row_call(kernel, rows, units, blocks, args, outs):
-    tile = rows // 2
-    whole = [pl.BlockSpec((tile, units), lambda i: (i, 0)) for _ in outs]
-    depth = sum(a.shape[1] for a in args if a.ndim == 2 and a.shape[1] > units)
+def up_kernel(at, x_far, x_late, table, hid, x, sem):
+    fetch = pltpu.make_async_copy(x_far, x, sem)
+    fetch.start()
+    tile = 384
+    for m in range(x.shape[0] // tile):
+        rows = pl.ds(m * tile, tile)
+        two = project(x_late.at[rows], table, 0)
+        if m == 0:
+            fetch.wait()
+        one = project(x.at[rows], table, at)
+        hid[rows, :] = activate(one[0] + two[0], one[1] + two[1])
+
+
+RESIDENT = pl.BlockSpec(memory_space=pltpu.VMEM)
+FAR = pl.BlockSpec(memory_space=pltpu.HBM)
+ROOM = pltpu.CompilerParams(vmem_limit_bytes=20 * 2**20)
+
+
+def up(x, x_late, table, at):
+    rows, units = x.shape[0], table.shape[2]
+    depth = table.shape[3]
     return pl.pallas_call(
-        kernel,
-        grid=(2,),
-        in_specs=[
-            pl.BlockSpec((1, 2, units, width), lambda i, at=at: (0, 0, 0, at))
-            if arg.ndim == 4
-            else pl.BlockSpec((tile, arg.shape[1]), lambda i: (i, 0))
-            for arg, (width, at) in zip(args, blocks)
-        ],
-        out_specs=whole,
-        out_shape=[jax.ShapeDtypeStruct((rows, units), kind) for kind in outs],
+        functools.partial(up_kernel, at),
+        in_specs=[FAR, RESIDENT, RESIDENT],
+        out_specs=RESIDENT,
+        out_shape=jax.ShapeDtypeStruct((rows, units), BF16),
+        scratch_shapes=[pltpu.VMEM(x.shape, BF16), pltpu.SemaphoreType.DMA],
+        compiler_params=ROOM,
         cost_estimate=pl.CostEstimate(
-            flops=4 * rows * depth * units,
-            bytes_accessed=2 * rows * depth + 4 * units * depth + 8 * rows * units,
+            flops=4 * rows * units * depth,
+            bytes_accessed=2 * rows * depth + 4 * units * depth,
             transcendentals=0,
         ),
-    )(*args)
+    )(x, x_late, table)
 
 
 def down_kernel(*refs):
-    out_ref = refs[-1]
-    hiddens, weights = refs[:4], refs[4:8]
-    value = jnp.dot(hiddens[0][...], weights[0][...], preferred_element_type=F32)
-    for hidden, weight in zip(hiddens[1:], weights[1:]):
-        value += jnp.dot(hidden[...], weight[...], preferred_element_type=F32)
-    out_ref[...] = value.astype(BF16)
+    hiddens, weights, (out, held, sems) = refs[:4], refs[4:8], refs[8:]
+    width = held.shape[2]
+    copies = []
+    for c in range(held.shape[0]):
+        at = pl.ds(c * width, width)
+        value = jnp.dot(hiddens[0][...], weights[0][:, at], preferred_element_type=F32)
+        for hidden, weight in zip(hiddens[1:], weights[1:]):
+            value += jnp.dot(hidden[...], weight[:, at], preferred_element_type=F32)
+        held[c] = value.astype(BF16)
+        copies.append(pltpu.make_async_copy(held.at[c], out.at[:, at], sems.at[c]))
+        copies[-1].start()
+    for copy in copies:
+        copy.wait()
 
 
 def down(hiddens, pieces):
     rows, units = hiddens[0].shape
     depth = pieces[0].shape[1]
-    width = depth // 4
-    hid_spec = pl.BlockSpec(memory_space=pltpu.VMEM)
-    w_spec = pl.BlockSpec((units, width), lambda i: (0, i))
+    parts = 4
     return pl.pallas_call(
         down_kernel,
-        grid=(depth // width,),
-        in_specs=[hid_spec] * 4 + [w_spec] * 4,
-        out_specs=pl.BlockSpec((rows, width), lambda i: (0, i)),
+        in_specs=[RESIDENT] * 8,
+        out_specs=FAR,
         out_shape=jax.ShapeDtypeStruct((rows, depth), BF16),
+        scratch_shapes=[
+            pltpu.VMEM((parts, rows, depth // parts), BF16),
+            pltpu.SemaphoreType.DMA((parts,)),
+        ],
+        compiler_params=ROOM,
         cost_estimate=pl.CostEstimate(
             flops=8 * rows * depth * units,
             bytes_accessed=2 * rows * depth + 8 * units * depth + 8 * rows * units,
@@ -141,7 +158,7 @@
 
 def column(own):
     return jnp.concatenate(
-        [own, swap(own, ("h",)), swap(own, ("qh",)), swap(own, ("qh", "h"))], axis=0
+        [own, swap(own, CROSS), swap(own, ("qh",)), swap(own, ("qh",) + CROSS)], axis=0
     )
 
 
@@ -241,27 +258,9 @@
     x0 = across(packed0, experts)
     packed1 = pack(pick, held1)
     x1 = across(packed1, experts)
-    units = gate_up.shape[2]
-    partial = row_call(
-        own_first_kernel, slots, units, ((0, 0), (CHUNK, late // CHUNK)), (x0, gate_up), (F32, F32)
-    )
-    (hidden_a,) = row_call(
-        own_last_kernel,
-        slots,
-        units,
-        ((0, 0), (late, 0), (0, 0), (0, 0)),
-        (x1, gate_up, *partial),
-        (BF16,),
-    )
+    hidden_a = up(x0, x1, gate_up, late)
     got_a = swap(hidden_a, ("qh",))
-    (hidden_b,) = row_call(
-        other_kernel,
-        slots,
-        units,
-        ((0, 0), (0, 0), (CHUNK, late // CHUNK), (late, 0)),
-        (x0, x1, gu_b, gu_b),
-        (BF16,),
-    )
+    hidden_b = up(x0, x1, gu_b, late)
     got_b = swap(hidden_b, ("qh",))
     table = gate_up.reshape(-1, depth)
     got_gu0 = lax.ppermute(table[:HEAD], ("x",), across_x)
@@ -272,8 +271,8 @@
     mixed = both[: 4 * own] + both[4 * own :]
     parts = mixed.reshape(4, own, half)
     sent = parts[1:].astype(BF16)
-    near = parts[0] + swap(sent[0], ("h",)).astype(F32)
-    far = swap(sent[1], ("qh",)).astype(F32) + swap(sent[2], ("qh", "h")).astype(F32)
+    near = parts[0] + swap(sent[0], CROSS).astype(F32)
+    far = swap(sent[1], ("qh",)).astype(F32) + swap(sent[2], ("qh",) + CROSS).astype(F32)
     low_half = q_high == 0
     out = jnp.concatenate(
         [jnp.where(low_half, near, far), jnp.where(low_half, far, near)], axis=1

time: 367 us -> 373 us (1.016)
  starting transfers between devices: 55.3 us -> 66.3 us
  Pallas kernels: 33.4 us -> 28.4 us
  waiting for transfers between devices: 247 us -> 243 us
    ppermute x15, waiting for transfers between devices: 134 us -> 81.8 us  [swap(): return lax.ppermute(value, axes, [(i, i ^ count - 1) for i in range(count)])]
    all_to_all x3, waiting for transfers between devices: 29 us -> 78.8 us  [across(): lax.all_to_all(value.reshape(experts, slots // experts, depth), PLANE, 0,...]
    all_to_all x3, starting transfers between devices: 26.1 us -> 33 us  [across(): lax.all_to_all(value.reshape(experts, slots // experts, depth), PLANE, 0,...]
    pallas_call x4 -> x3, Pallas kernels: 24.1 us -> 19.1 us  [the longest x2 12.9 us: up(): pl.pallas_call(functools.partial(up_kernel, at), in_specs=[FAR, RESIDENT,...]
    ppermute x15, starting transfers between devices: 23.3 us -> 27.4 us  [swap(): return lax.ppermute(value, axes, [(i, i ^ count - 1) for i in range(count)])]
  transfers between devices with their start and end apart: 21 -> 21, of which waited for: 13 -> 14; matrix products, arithmetic and copies ran while one was open for 4% -> 4% of each run, Pallas kernels for 7% -> 6%
where the time goes in v5:
time: 373 us; the launch traced here: 367 us
  waiting for transfers between devices  243 us (65%)
  starting transfers between devices  66.3 us (18%)
  Pallas kernels  28.4 us (8%)
  local copies, waits for them, and re-layouts  13.6 us (4%)
  matrix products  8.84 us (2%)
  other arithmetic  6.35 us (2%)
    ppermute x15, waiting for transfers between devices, swap(): return lax.ppermute(value, axes, [(i, i ^ count - 1) for i in range(count)])  81.8 us
    all_to_all x3, waiting for transfers between devices, across(): lax.all_to_all(value.reshape(experts, slots // experts, depth), PLANE, 0,...  78.8 us
    ppermute x1, waiting for transfers between devices, local(): got_gu0 = lax.ppermute(table[:HEAD], ('x',), across_x)  54.9 us
    all_to_all x3, starting transfers between devices, across(): lax.all_to_all(value.reshape(experts, slots // experts, depth), PLANE, 0,...  33 us
    ppermute x15, starting transfers between devices, swap(): return lax.ppermute(value, axes, [(i, i ^ count - 1) for i in range(count)])  27.4 us
    ppermute x1, waiting for transfers between devices, local(): got_dn = lax.ppermute(down_proj, ('x',), across_x)  25.8 us
    pallas_call x2, Pallas kernels, up(): pl.pallas_call(functools.partial(up_kernel, at), in_specs=[FAR, RESIDENT,...  12.9 us
    pallas_call x2, Pallas kernels, put(): pl.pallas_call(put_kernel, grid_spec=pltpu.PrefetchScalarGridSpec(num_sca...  9.26 us
  transfers between devices with their start and end apart: 21, of which 14 were waited for; matrix products, arithmetic and copies ran while one was open for 4% of the time, Pallas kernels for 6%

profile of v5, /device:TPU:65, one launch (start us, length us, event | category | flops | bytes accessed | tf_op | source)
XLA Modules:
  0.0 367.2 jit_solution(13656058214806788736)
XLA Ops:
  3.3 4.7 %collective-permute-start = (bf16[32,1152]{1,0:T(8,128)(2,1)S(1)}, bf16[32,1152]{1,0:T(8,128)(2,1)S(1)}, u32[]{:S(2)}, u32[]{:S(2)}) collective-permute-start(bf16[32,1152]{1,0:T(8,128)(2,1)S(1)} %concatenate.25), channel_id=1, source_target_pairs={{0,66},{2,64},{64,2},{66,0},{1,67},{3,65},{65,3},{67,1},{4,70},{6,... | collective-permute-start | bytes 221192 | tf_op jit(solution)/shard_map/ppermute | solution.py:156
  9.5 1.9 collective-permute-done
  11.4 2.5 collective-permute-done.1
  13.9 3.4 collective-permute-done.2
  21.5 8.1 %all-to-all-start = ((bf16[32,24,1024]{2,1,0:T(8,128)(2,1)}), bf16[32,24,1024]{2,1,0:T(8,128)(2,1)S(1)}, u32[]{:S(2)}, u32[]{:S(2)}) async-start(bf16[32,24,1024]{2,1,0:T(8,128)(2,1)} %bitcast.2), calls=%async_computation | async-start | bytes 3145728 | tf_op jit(solution)/shard_map/all_to_all | solution.py:209
  32.6 2.7 collective-permute-start.5
  35.3 11.7 %collective-permute-done.3 = bf16[32,3072]{1,0:T(8,128)(2,1)S(1)} collective-permute-done((bf16[32,3072]{1,0:T(8,128)(2,1)S(1)}, bf16[32,3072]{1,0:T(8,128)(2,1)S(1)}, u32[]{:S(2)}, u32[]{:S(2)}) %collective-permute-start.3) | collective-permute-done | bytes 196640 | tf_op jit(solution)/shard_map/ppermute | solution.py:156
  48.1 3.6 convolution_convert_fusion
  53.4 7.9 %all-to-all-start.1 = ((bf16[32,24,3072]{2,1,0:T(8,128)(2,1)}), bf16[32,24,3072]{2,1,0:T(8,128)(2,1)}, u32[]{:S(2)}, u32[]{:S(2)}) async-start(bf16[32,24,3072]{2,1,0:T(8,128)(2,1)} %bitcast.30), calls=%async_computation.1 | async-start | bytes 9437184 | tf_op jit(solution)/shard_map/all_to_all | solution.py:209
  61.3 2.8 collective-permute-start.6
  64.1 2.7 dynamic-slice_bitcast_fusion
  68.0 2.3 collective-permute-start.9
  70.3 49.2 %all-to-all-done.1 = bf16[32,24,3072]{2,1,0:T(8,128)(2,1)} async-done(((bf16[32,24,3072]{2,1,0:T(8,128)(2,1)}), bf16[32,24,3072]{2,1,0:T(8,128)(2,1)}, u32[]{:S(2)}, u32[]{:S(2)}) %all-to-all-start.1) | async-done | bytes 4718624 | tf_op jit(solution)/shard_map/all_to_all | solution.py:209
  121.0 6.0 %shard_map.85.refs_0_ = bf16[768,192]{1,0:T(8,128)(2,1)S(1)} custom-call(bf16[768,1024]{1,0:T(8,128)(2,1)S(1)} %bitcast.27, bf16[768,3072]{1,0:T(8,128)(2,1)} %bitcast.5.x_late, bf16[1,2,192,4096]{3,2,1,0:T(8,128)(2,1)S(1)} %copy-done), custom_call_target="tpu_custom_call" | custom-call | flops 2415919104 | bytes 9437184 | tf_op jit(solution)/shard_map/pallas_call | solution.py:59
  126.9 21.1 %collective-permute-done.6.table = bf16[1,2,192,4096]{3,2,1,0:T(8,128)(2,1)} collective-permute-done((bf16[1,2,192,4096]{3,2,1,0:T(8,128)(2,1)S(1)}, bf16[1,2,192,4096]{3,2,1,0:T(8,128)(2,1)}, u32[]{:S(2)}, u32[]{:S(2)}) %collective-permute-start.6) | collective-permute-done | bytes 3145760 | tf_op jit(solution)/shard_map/ppermute | solution.py:156
  148.1 6.9 %shard_map.86.refs_1_ = bf16[768,192]{1,0:T(8,128)(2,1)S(1)} custom-call(bf16[768,1024]{1,0:T(8,128)(2,1)S(1)} %bitcast.28, bf16[768,3072]{1,0:T(8,128)(2,1)} %bitcast.5.x_late, bf16[1,2,192,4096]{3,2,1,0:T(8,128)(2,1)} %collective-permute-done.6.table), custom_call_target="tpu_custom_call" | custom-call | flops 2415919104 | bytes 9437184 | tf_op jit(solution)/shard_map/pallas_call | solution.py:59
  155.0 2.8 collective-permute-start.8
  157.9 32.5 %collective-permute-done.9.refs_5_ = bf16[192,2048]{1,0:T(8,128)(2,1)} collective-permute-done((bf16[192,2048]{1,0:T(8,128)(2,1)}, bf16[192,2048]{1,0:T(8,128)(2,1)}, u32[]{:S(2)}, u32[]{:S(2)}) %collective-permute-start.9) | collective-permute-done | bytes 786464 | tf_op jit(solution)/shard_map/ppermute | solution.py:156
  190.4 7.6 %collective-permute-done.7.refs_2_ = bf16[768,192]{1,0:T(8,128)(2,1)S(1)} collective-permute-done((bf16[768,192]{1,0:T(8,128)(2,1)S(1)}, bf16[768,192]{1,0:T(8,128)(2,1)S(1)}, u32[]{:S(2)}, u32[]{:S(2)}) %collective-permute-start.7) | collective-permute-done | bytes 294944 | tf_op jit(solution)/shard_map/ppermute | solution.py:156
  198.0 6.2 %down.1 = bf16[768,2048]{1,0:T(8,128)(2,1)S(1)} custom-call(bf16[768,192]{1,0:T(8,128)(2,1)S(1)} %shard_map.85.refs_0_, bf16[768,192]{1,0:T(8,128)(2,1)S(1)} %shard_map.86.refs_1_, bf16[768,192]{1,0:T(8,128)(2,1)S(1)} %collective-permute-done.7.refs_2_, bf16[768,192]{1,0:T(8,128)(2,1)S(1)} %collective-permute-done.8.refs_3_, ...), custom_call_target="tpu_custom_call" | custom-call | flops 2415919104 | bytes 7471104 | tf_op jit(solution)/shard_map/down/pallas_call | solution.py:94
  205.9 17.1 %all-to-all-start.2 = ((bf16[32,24,2048]{2,1,0:T(8,128)(2,1)}), bf16[32,24,2048]{2,1,0:T(8,128)(2,1)}, u32[]{:S(2)}, u32[]{:S(2)}) async-start(bf16[32,24,2048]{2,1,0:T(8,128)(2,1)} %bitcast.29), calls=%async_computation.2 | async-start | bytes 6291456 | tf_op jit(solution)/shard_map/all_to_all | solution.py:209
  223.0 3.0 collective-permute-start.17
  228.5 2.9 collective-permute-start.15
  233.7 29.0 %all-to-all-done.2 = bf16[32,24,2048]{2,1,0:T(8,128)(2,1)} async-done(((bf16[32,24,2048]{2,1,0:T(8,128)(2,1)}), bf16[32,24,2048]{2,1,0:T(8,128)(2,1)}, u32[]{:S(2)}, u32[]{:S(2)}) %all-to-all-start.2) | async-done | bytes 3145760 | tf_op jit(solution)/shard_map/all_to_all | solution.py:209
  262.8 2.9 fusion.18
  265.8 4.2 %collective-permute-start.12 = (bf16[32,2048]{1,0:T(8,128)(2,1)S(1)}, bf16[32,2048]{1,0:T(8,128)(2,1)S(1)}, u32[]{:S(2)}, u32[]{:S(2)}) collective-permute-start(bf16[32,2048]{1,0:T(8,128)(2,1)S(1)} %get-tuple-element.13), channel_id=1, source_target_pairs={{0,66},{2,64},{64,2},{66,0},{1,67},{3,65},{65,3},{67,1},{4,70},{6,... | collective-permute-start | bytes 393224 | tf_op jit(solution)/shard_map/ppermute | solution.py:156
  270.0 25.8 %collective-permute-done.17 = bf16[1,192,4096]{2,1,0:T(8,128)(2,1)} collective-permute-done((bf16[1,192,4096]{2,1,0:T(8,128)(2,1)}, bf16[1,192,4096]{2,1,0:T(8,128)(2,1)}, u32[]{:S(2)}, u32[]{:S(2)}) %collective-permute-start.17) | collective-permute-done | bytes 1572896 | tf_op jit(solution)/shard_map/ppermute | solution.py:243
  295.8 2.2 collective-permute-start.14
  298.0 1.9 broadcast_select_fusion
  299.9 54.9 %collective-permute-done.16.got = bf16[336,4096]{1,0:T(8,128)(2,1)} collective-permute-done((bf16[336,4096]{1,0:T(8,128)(2,1)}, bf16[336,4096]{1,0:T(8,128)(2,1)}, u32[]{:S(2)}, u32[]{:S(2)}) %collective-permute-start.16) | collective-permute-done | bytes 2752544 | tf_op jit(solution)/shard_map/ppermute | solution.py:266
  354.8 6.7 %put.2.refs_0_ = bf16[384,4096]{1,0:T(8,128)(2,1)} custom-call(s32[1]{0:T(128)} %bitcast.12.moving, bf16[336,4096]{1,0:T(8,128)(2,1)} %collective-permute-done.16.got, bf16[384,4096]{1,0:T(8,128)(2,1)} %bitcast.23), custom_call_target="tpu_custom_call" | custom-call | bytes 8257536 | tf_op jit(solution)/shard_map/put/pallas_call | solution.py:137
  363.9 2.5 put.3
  (75 shorter events, 26.5 us)
Async XLA Ops:
  3.3 8.0 %collective-permute-start = (bf16[32,1152]{1,0:T(8,128)(2,1)S(1)}, bf16[32,1152]{1,0:T(8,128)(2,1)S(1)}, u32[]{:S(2)}, u32[]{:S(2)}) collective-permute-start(bf16[32,1152]{1,0:T(8,128)(2,1)S(1)} %concatenate.25), channel_id=1, source_target_pairs={{0,66},{2,64},{64,2},{66,0},{1,67},{3,65},{65,3},{67,1},{4,70},{6,... | collective-permute-start | bytes 221192 | tf_op jit(solution)/shard_map/ppermute | solution.py:156
  8.1 5.8 %collective-permute-start.1 = (bf16[32,1152]{1,0:T(8,128)(2,1)S(1)}, bf16[32,1152]{1,0:T(8,128)(2,1)S(1)}, u32[]{:S(2)}, u32[]{:S(2)}) collective-permute-start(bf16[32,1152]{1,0:T(8,128)(2,1)S(1)} %concatenate.25), channel_id=1, source_target_pairs={{0,128},{128,0},{1,129},{129,1},{2,130},{130,2},{3,131},{131,3},{4... | collective-permute-start | bytes 221192 | tf_op jit(solution)/shard_map/ppermute | solution.py:156
  9.3 8.1 %collective-permute-start.2 = (bf16[32,1152]{1,0:T(8,128)(2,1)S(1)}, bf16[32,1152]{1,0:T(8,128)(2,1)S(1)}, u32[]{:S(2)}, u32[]{:S(2)}) collective-permute-start(bf16[32,1152]{1,0:T(8,128)(2,1)S(1)} %concatenate.25), channel_id=1, source_target_pairs={{0,194},{2,192},{64,130},{66,128},{128,66},{130,64},{192,2},{194,0... | collective-permute-start | bytes 221192 | tf_op jit(solution)/shard_map/ppermute | solution.py:156
  18.4 1.1 copy-start.5
  21.5 8.1 %copy-start.7 = (bf16[2,16,4096]{2,1,0:T(8,128)(2,1)S(1)}, bf16[2,16,4096]{2,1,0:T(8,128)(2,1)}, u32[]{:S(2)}) copy-start(bf16[2,16,4096]{2,1,0:T(8,128)(2,1)} %param.6) | copy-start | bytes 786436
  21.5 30.8 %all-to-all-start = ((bf16[32,24,1024]{2,1,0:T(8,128)(2,1)}), bf16[32,24,1024]{2,1,0:T(8,128)(2,1)S(1)}, u32[]{:S(2)}, u32[]{:S(2)}) async-start(bf16[32,24,1024]{2,1,0:T(8,128)(2,1)} %bitcast.2), calls=%async_computation | async-start | bytes 3145728 | tf_op jit(solution)/shard_map/all_to_all | solution.py:209
  29.6 17.4 %collective-permute-start.3 = (bf16[32,3072]{1,0:T(8,128)(2,1)S(1)}, bf16[32,3072]{1,0:T(8,128)(2,1)S(1)}, u32[]{:S(2)}, u32[]{:S(2)}) collective-permute-start(bf16[32,3072]{1,0:T(8,128)(2,1)S(1)} %slice.89), channel_id=1, source_target_pairs={{0,66},{2,64},{64,2},{66,0},{1,67},{3,65},{65,3},{67,1},{4,70},{6,... | collective-permute-start | bytes 589832 | tf_op jit(solution)/shard_map/ppermute | solution.py:156
  31.4 16.7 %collective-permute-start.4 = (bf16[32,3072]{1,0:T(8,128)(2,1)S(1)}, bf16[32,3072]{1,0:T(8,128)(2,1)S(1)}, u32[]{:S(2)}, u32[]{:S(2)}) collective-permute-start(bf16[32,3072]{1,0:T(8,128)(2,1)S(1)} %slice.89), channel_id=1, source_target_pairs={{0,128},{128,0},{1,129},{129,1},{2,130},{130,2},{3,131},{131,3},{4... | collective-permute-start | bytes 589832 | tf_op jit(solution)/shard_map/ppermute | solution.py:156
  32.6 15.5 %collective-permute-start.5 = (bf16[32,3072]{1,0:T(8,128)(2,1)S(1)}, bf16[32,3072]{1,0:T(8,128)(2,1)S(1)}, u32[]{:S(2)}, u32[]{:S(2)}) collective-permute-start(bf16[32,3072]{1,0:T(8,128)(2,1)S(1)} %slice.89), channel_id=1, source_target_pairs={{0,194},{2,192},{64,130},{66,128},{128,66},{130,64},{192,2},{194,0... | collective-permute-start | bytes 589832 | tf_op jit(solution)/shard_map/ppermute | solution.py:156
  52.2 1.1 copy-start.1
  53.4 7.9 %copy-start = (bf16[1,2,192,4096]{3,2,1,0:T(8,128)(2,1)S(1)}, bf16[1,2,192,4096]{3,2,1,0:T(8,128)(2,1)}, u32[]{:S(2)}) copy-start(bf16[1,2,192,4096]{3,2,1,0:T(8,128)(2,1)} %table.1) | copy-start | bytes 9437188
  53.4 66.2 %all-to-all-start.1 = ((bf16[32,24,3072]{2,1,0:T(8,128)(2,1)}), bf16[32,24,3072]{2,1,0:T(8,128)(2,1)}, u32[]{:S(2)}, u32[]{:S(2)}) async-start(bf16[32,24,3072]{2,1,0:T(8,128)(2,1)} %bitcast.30), calls=%async_computation.1 | async-start | bytes 9437184 | tf_op jit(solution)/shard_map/all_to_all | solution.py:209
  61.3 86.8 %collective-permute-start.6 = (bf16[1,2,192,4096]{3,2,1,0:T(8,128)(2,1)S(1)}, bf16[1,2,192,4096]{3,2,1,0:T(8,128)(2,1)}, u32[]{:S(2)}, u32[]{:S(2)}) collective-permute-start(bf16[1,2,192,4096]{3,2,1,0:T(8,128)(2,1)S(1)} %copy-done), channel_id=1, source_target_pairs={{0,64},{64,0},{1,65},{65,1},{2,66},{66,2},{3,67},{67,3},{4,68},{68... | collective-permute-start | bytes 9437192 | tf_op jit(solution)/shard_map/ppermute | solution.py:156
  66.8 91.2 %collective-permute-start.10 = (bf16[192,2048]{1,0:T(8,128)(2,1)}, bf16[192,2048]{1,0:T(8,128)(2,1)}, u32[]{:S(2)}, u32[]{:S(2)}) collective-permute-start(bf16[192,2048]{1,0:T(8,128)(2,1)} %get-tuple-element.9), channel_id=1, source_target_pairs={{0,128},{128,0},{1,129},{129,1},{2,130},{130,2},{3,131},{131,3},{4... | collective-permute-start | bytes 2359304 | tf_op jit(solution)/shard_map/ppermute | solution.py:156
  67.2 90.7 %collective-permute-start.11 = (bf16[192,2048]{1,0:T(8,128)(2,1)}, bf16[192,2048]{1,0:T(8,128)(2,1)}, u32[]{:S(2)}, u32[]{:S(2)}) collective-permute-start(bf16[192,2048]{1,0:T(8,128)(2,1)} %get-tuple-element.9), channel_id=1, source_target_pairs={{0,192},{64,128},{128,64},{192,0},{1,193},{65,129},{129,65},{193,1... | collective-permute-start | bytes 2359304 | tf_op jit(solution)/shard_map/ppermute | solution.py:156
  68.0 122.4 %collective-permute-start.9 = (bf16[192,2048]{1,0:T(8,128)(2,1)}, bf16[192,2048]{1,0:T(8,128)(2,1)}, u32[]{:S(2)}, u32[]{:S(2)}) collective-permute-start(bf16[192,2048]{1,0:T(8,128)(2,1)} %get-tuple-element.10.refs_4_), channel_id=1, source_target_pairs={{0,64},{64,0},{1,65},{65,1},{2,66},{66,2},{3,67},{67,3},{4,68},{68... | collective-permute-start | bytes 2359304 | tf_op jit(solution)/shard_map/ppermute | solution.py:156
  119.5 1.4 copy-start.2
  155.0 35.4 %collective-permute-start.8 = (bf16[768,192]{1,0:T(8,128)(2,1)S(1)}, bf16[768,192]{1,0:T(8,128)(2,1)S(1)}, u32[]{:S(2)}, u32[]{:S(2)}) collective-permute-start(bf16[768,192]{1,0:T(8,128)(2,1)S(1)} %shard_map.86.refs_1_), channel_id=1, source_target_pairs={{0,128},{128,0},{1,129},{129,1},{2,130},{130,2},{3,131},{131,3},{4... | collective-permute-start | bytes 884744 | tf_op jit(solution)/shard_map/ppermute | solution.py:156
  157.8 40.2 %collective-permute-start.7 = (bf16[768,192]{1,0:T(8,128)(2,1)S(1)}, bf16[768,192]{1,0:T(8,128)(2,1)S(1)}, u32[]{:S(2)}, u32[]{:S(2)}) collective-permute-start(bf16[768,192]{1,0:T(8,128)(2,1)S(1)} %shard_map.85.refs_0_), channel_id=1, source_target_pairs={{0,128},{128,0},{1,129},{129,1},{2,130},{130,2},{3,131},{131,3},{4... | collective-permute-start | bytes 884744 | tf_op jit(solution)/shard_map/ppermute | solution.py:156
  204.2 1.7 copy-start.3
  205.9 56.9 %all-to-all-start.2 = ((bf16[32,24,2048]{2,1,0:T(8,128)(2,1)}), bf16[32,24,2048]{2,1,0:T(8,128)(2,1)}, u32[]{:S(2)}, u32[]{:S(2)}) async-start(bf16[32,24,2048]{2,1,0:T(8,128)(2,1)} %bitcast.29), calls=%async_computation.2 | async-start | bytes 6291456 | tf_op jit(solution)/shard_map/all_to_all | solution.py:209
  223.0 72.9 %collective-permute-start.17 = (bf16[1,192,4096]{2,1,0:T(8,128)(2,1)}, bf16[1,192,4096]{2,1,0:T(8,128)(2,1)}, u32[]{:S(2)}, u32[]{:S(2)}) collective-permute-start(bf16[1,192,4096]{2,1,0:T(8,128)(2,1)} %param.10), channel_id=1, source_target_pairs={{0,32},{16,48},{32,0},{48,16},{1,33},{17,49},{33,1},{49,17},{2,34}... | collective-permute-start | bytes 4718600 | tf_op jit(solution)/shard_map/ppermute | solution.py:243
  225.9 5.5 %copy-start.8 = (s32[8,2]{0,1:T(2,128)S(1)}, s32[8,2]{0,1:T(2,128)}, u32[]{:S(2)}) copy-start(s32[8,2]{0,1:T(2,128)} %param.11) | copy-start | bytes 196
  227.6 127.2 %collective-permute-start.16 = (bf16[336,4096]{1,0:T(8,128)(2,1)}, bf16[336,4096]{1,0:T(8,128)(2,1)}, u32[]{:S(2)}, u32[]{:S(2)}) collective-permute-start(bf16[336,4096]{1,0:T(8,128)(2,1)} %slice.97), channel_id=1, source_target_pairs={{0,32},{16,48},{32,0},{48,16},{1,33},{17,49},{33,1},{49,17},{2,34}... | collective-permute-start | bytes 8257544 | tf_op jit(solution)/shard_map/ppermute | solution.py:266
  228.5 134.6 %collective-permute-start.15 = (bf16[48,4096]{1,0:T(8,128)(2,1)}, bf16[48,4096]{1,0:T(8,128)(2,1)S(1)}, u32[]{:S(2)}, u32[]{:S(2)}) collective-permute-start(bf16[48,4096]{1,0:T(8,128)(2,1)} %slice.96), channel_id=1, source_target_pairs={{0,32},{16,48},{32,0},{48,16},{1,33},{17,49},{33,1},{49,17},{2,34}... | collective-permute-start | bytes 1179656 | tf_op jit(solution)/shard_map/ppermute | solution.py:267
  265.6 32.4 %copy-start.4 = (bf16[1,192,4096]{2,1,0:T(8,128)(2,1)S(1)}, bf16[1,192,4096]{2,1,0:T(8,128)(2,1)}, u32[]{:S(2)}) copy-start(bf16[1,192,4096]{2,1,0:T(8,128)(2,1)} %param.10) | copy-start | bytes 4718596
  265.8 100.6 %collective-permute-start.12 = (bf16[32,2048]{1,0:T(8,128)(2,1)S(1)}, bf16[32,2048]{1,0:T(8,128)(2,1)S(1)}, u32[]{:S(2)}, u32[]{:S(2)}) collective-permute-start(bf16[32,2048]{1,0:T(8,128)(2,1)S(1)} %get-tuple-element.13), channel_id=1, source_target_pairs={{0,66},{2,64},{64,2},{66,0},{1,67},{3,65},{65,3},{67,1},{4,70},{6,... | collective-permute-start | bytes 393224 | tf_op jit(solution)/shard_map/ppermute | solution.py:156
  270.0 96.4 %collective-permute-start.13 = (bf16[32,2048]{1,0:T(8,128)(2,1)S(1)}, bf16[32,2048]{1,0:T(8,128)(2,1)S(1)}, u32[]{:S(2)}, u32[]{:S(2)}) collective-permute-start(bf16[32,2048]{1,0:T(8,128)(2,1)S(1)} %get-tuple-element.15), channel_id=1, source_target_pairs={{0,128},{128,0},{1,129},{129,1},{2,130},{130,2},{3,131},{131,3},{4... | collective-permute-start | bytes 393224 | tf_op jit(solution)/shard_map/ppermute | solution.py:156
  295.8 70.6 %collective-permute-start.14 = (bf16[32,2048]{1,0:T(8,128)(2,1)S(1)}, bf16[32,2048]{1,0:T(8,128)(2,1)S(1)}, u32[]{:S(2)}, u32[]{:S(2)}) collective-permute-start(bf16[32,2048]{1,0:T(8,128)(2,1)S(1)} %get-tuple-element.14), channel_id=1, source_target_pairs={{0,194},{2,192},{64,130},{66,128},{128,66},{130,64},{192,2},{194,0... | collective-permute-start | bytes 393224 | tf_op jit(solution)/shard_map/ppermute | solution.py:156
  363.1 0.8 copy-start.6

commit v6 on v5

--- a/solution.py
+++ b/solution.py
@@ -13,7 +13,6 @@
 CAP = 3
 CHUNK = 1024
 META = 128
-HEAD = 336
 PLANE = ("x", "y", "c")
 CROSS = ("ql", "h")
 
@@ -38,14 +37,16 @@
 def up_kernel(at, x_far, x_late, table, hid, x, sem):
     fetch = pltpu.make_async_copy(x_far, x, sem)
     fetch.start()
-    tile = 384
+    tile = hid.shape[0]
+    sides = []
     for m in range(x.shape[0] // tile):
         rows = pl.ds(m * tile, tile)
         two = project(x_late.at[rows], table, 0)
         if m == 0:
             fetch.wait()
         one = project(x.at[rows], table, at)
-        hid[rows, :] = activate(one[0] + two[0], one[1] + two[1])
+        sides.append(activate(one[0] + two[0], one[1] + two[1]))
+    hid[...] = jnp.concatenate(sides, axis=1)
 
 
 RESIDENT = pl.BlockSpec(memory_space=pltpu.VMEM)
@@ -60,7 +61,7 @@
         functools.partial(up_kernel, at),
         in_specs=[FAR, RESIDENT, RESIDENT],
         out_specs=RESIDENT,
-        out_shape=jax.ShapeDtypeStruct((rows, units), BF16),
+        out_shape=jax.ShapeDtypeStruct((rows // 2, 2 * units), BF16),
         scratch_shapes=[pltpu.VMEM(x.shape, BF16), pltpu.SemaphoreType.DMA],
         compiler_params=ROOM,
         cost_estimate=pl.CostEstimate(
@@ -73,14 +74,19 @@
 
 def down_kernel(*refs):
     hiddens, weights, (out, held, sems) = refs[:4], refs[4:8], refs[8:]
-    width = held.shape[2]
+    count, rows, width = held.shape
+    tile, units = rows // 2, weights[0].shape[0]
+    sides = [
+        jnp.concatenate([h[:, m * units : (m + 1) * units] for h in hiddens], axis=1)
+        for m in range(2)
+    ]
     copies = []
-    for c in range(held.shape[0]):
+    for c in range(count):
         at = pl.ds(c * width, width)
-        value = jnp.dot(hiddens[0][...], weights[0][:, at], preferred_element_type=F32)
-        for hidden, weight in zip(hiddens[1:], weights[1:]):
-            value += jnp.dot(hidden[...], weight[:, at], preferred_element_type=F32)
-        held[c] = value.astype(BF16)
+        table = jnp.concatenate([w[:, at] for w in weights], axis=0)
+        for m in range(2):
+            value = jnp.dot(sides[m], table, preferred_element_type=F32)
+            held[c, m * tile : (m + 1) * tile] = value.astype(BF16)
         copies.append(pltpu.make_async_copy(held.at[c], out.at[:, at], sems.at[c]))
         copies[-1].start()
     for copy in copies:
@@ -88,8 +94,8 @@
 
 
 def down(hiddens, pieces):
-    rows, units = hiddens[0].shape
-    depth = pieces[0].shape[1]
+    rows = 2 * hiddens[0].shape[0]
+    units, depth = pieces[0].shape
     parts = 4
     return pl.pallas_call(
         down_kernel,
@@ -110,9 +116,7 @@
     )(*hiddens, *pieces)
 
 
-def put_kernel(moving, got, own, *refs):
-    out = refs[-1]
-
+def put_kernel(moving, got, own, out):
     @pl.when(moving[0] != 0)
     def _():
         out[...] = got[...]
@@ -122,33 +126,24 @@
         out[...] = own[...]
 
 
-def put(moving, got, own, first, base=None):
-    block = 48
+def put(moving, got, own):
+    block = 64
     depth = own.shape[1]
-    start = first // block
-    here = pl.BlockSpec((block, depth), lambda i, m: (start + i, 0))
-    specs = [pl.BlockSpec((block, depth), lambda i, m: (i, 0)), here]
-    args = [moving, got, own]
-    aliases = {}
-    if base is not None:
-        specs.append(pl.BlockSpec(memory_space=pl.ANY))
-        args.append(base)
-        aliases = {3: 0}
+    spec = pl.BlockSpec((block, depth), lambda i, m: (i, 0))
     return pl.pallas_call(
         put_kernel,
         grid_spec=pltpu.PrefetchScalarGridSpec(
             num_scalar_prefetch=1,
             grid=(got.shape[0] // block,),
-            in_specs=specs,
-            out_specs=here,
+            in_specs=[spec, spec],
+            out_specs=spec,
         ),
         out_shape=jax.ShapeDtypeStruct(own.shape, own.dtype),
-        input_output_aliases=aliases,
         cost_estimate=pl.CostEstimate(
             flops=0, bytes_accessed=6 * got.shape[0] * depth, transcendentals=0
         ),
         name="put",
-    )(*args)
+    )(moving, got, own)
 
 
 def swap(value, axes):
@@ -263,8 +258,7 @@
     hidden_b = up(x0, x1, gu_b, late)
     got_b = swap(hidden_b, ("qh",))
     table = gate_up.reshape(-1, depth)
-    got_gu0 = lax.ppermute(table[:HEAD], ("x",), across_x)
-    got_gu1 = lax.ppermute(table[HEAD:], ("x",), across_x)
+    got_gu = lax.ppermute(table, ("x",), across_x)
     made = down((hidden_a, hidden_b, got_a, got_b), pieces)
     back = across(made, experts)
     both = jnp.dot(mix, back, preferred_element_type=F32)
@@ -279,8 +273,7 @@
     )
     moving = jnp.any(pairs == slot)
     flag = jnp.sum((pairs == slot).astype(jnp.int32)).reshape(1)
-    new_gu = put(flag, got_gu0, table, 0)
-    new_gu = put(flag, got_gu1, table, HEAD, new_gu)
+    new_gu = put(flag, got_gu, table)
     new_dn = jnp.where(moving, got_dn, down_proj)
     return (
         out.astype(BF16).reshape(steps, rows, depth),

time: 373 us -> 370 us (level)
  waiting for transfers between devices: 243 us -> 252 us
  starting transfers between devices: 66.3 us -> 59.3 us
  Pallas kernels: 28.4 us -> 24.6 us
    ppermute x1, waiting for transfers between devices: 25.8 us -> 89.2 us  [local(): got_dn = lax.ppermute(down_proj, ('x',), across_x)]
    ppermute x2 -> x1, waiting for transfers between devices: 56.5 us -> 0.01 us  [local(): got_gu = lax.ppermute(table, ('x',), across_x)]
    all_to_all x3, waiting for transfers between devices: 78.8 us -> 83.8 us  [across(): lax.all_to_all(value.reshape(experts, slots // experts, depth), PLANE, 0,...]
    all_to_all x3, starting transfers between devices: 33 us -> 28.9 us  [across(): lax.all_to_all(value.reshape(experts, slots // experts, depth), PLANE, 0,...]
    pallas_call x2 -> x1, Pallas kernels: 9.26 us -> 6.46 us  [put(): pl.pallas_call(put_kernel, grid_spec=pltpu.PrefetchScalarGridSpec(num_sca...]
  transfers between devices with their start and end apart: 21 -> 20, of which waited for: 14 -> 13; matrix products, arithmetic and copies ran while one was open for 4% -> 4% of each run, Pallas kernels for 6% -> 5%
where the time goes in v6:
time: 370 us; the launch traced here: 365 us
  waiting for transfers between devices  252 us (68%)
  starting transfers between devices  59.3 us (16%)
  Pallas kernels  24.6 us (7%)
  local copies, waits for them, and re-layouts  10.1 us (3%)
  other arithmetic  9.01 us (2%)
  matrix products  8.98 us (2%)
    ppermute x1, waiting for transfers between devices, local(): got_dn = lax.ppermute(down_proj, ('x',), across_x)  89.2 us
    all_to_all x3, waiting for transfers between devices, across(): lax.all_to_all(value.reshape(experts, slots // experts, depth), PLANE, 0,...  83.8 us
    ppermute x15, waiting for transfers between devices, swap(): return lax.ppermute(value, axes, [(i, i ^ count - 1) for i in range(count)])  79.3 us
    all_to_all x3, starting transfers between devices, across(): lax.all_to_all(value.reshape(experts, slots // experts, depth), PLANE, 0,...  28.9 us
    ppermute x15, starting transfers between devices, swap(): return lax.ppermute(value, axes, [(i, i ^ count - 1) for i in range(count)])  27.3 us
    pallas_call x2, Pallas kernels, up(): pl.pallas_call(functools.partial(up_kernel, at), in_specs=[FAR, RESIDENT,...  13.1 us
  transfers between devices with their start and end apart: 20, of which 13 were waited for; matrix products, arithmetic and copies ran while one was open for 4% of the time, Pallas kernels for 5%

profile of v6, /device:TPU:65, one launch (start us, length us, event | category | flops | bytes accessed | tf_op | source)
XLA Modules:
  0.0 365.0 jit_solution(7162222374497478932)
XLA Ops:
  3.3 4.7 %collective-permute-start = (bf16[32,1152]{1,0:T(8,128)(2,1)S(1)}, bf16[32,1152]{1,0:T(8,128)(2,1)S(1)}, u32[]{:S(2)}, u32[]{:S(2)}) collective-permute-start(bf16[32,1152]{1,0:T(8,128)(2,1)S(1)} %concatenate.25), channel_id=1, source_target_pairs={{0,66},{2,64},{64,2},{66,0},{1,67},{3,65},{65,3},{67,1},{4,70},{6,... | collective-permute-start | bytes 221192 | tf_op jit(solution)/shard_map/ppermute | solution.py:151
  9.5 1.9 collective-permute-done
  11.4 2.5 collective-permute-done.1
  13.9 3.4 collective-permute-done.2
  19.7 1.8 convolution_convert_fusion.1
  21.5 8.1 %all-to-all-start = ((bf16[32,24,1024]{2,1,0:T(8,128)(2,1)}), bf16[32,24,1024]{2,1,0:T(8,128)(2,1)S(1)}, u32[]{:S(2)}, u32[]{:S(2)}) async-start(bf16[32,24,1024]{2,1,0:T(8,128)(2,1)} %bitcast.2), calls=%async_computation | async-start | bytes 3145728 | tf_op jit(solution)/shard_map/all_to_all | solution.py:204
  29.6 1.8 collective-permute-start.3
  32.6 2.7 collective-permute-start.5
  35.3 11.7 %collective-permute-done.3 = bf16[32,3072]{1,0:T(8,128)(2,1)S(1)} collective-permute-done((bf16[32,3072]{1,0:T(8,128)(2,1)S(1)}, bf16[32,3072]{1,0:T(8,128)(2,1)S(1)}, u32[]{:S(2)}, u32[]{:S(2)}) %collective-permute-start.3) | collective-permute-done | bytes 196640 | tf_op jit(solution)/shard_map/ppermute | solution.py:151
  48.1 3.6 convolution_convert_fusion
  52.2 7.6 %all-to-all-start.1 = ((bf16[32,24,3072]{2,1,0:T(8,128)(2,1)}), bf16[32,24,3072]{2,1,0:T(8,128)(2,1)}, u32[]{:S(2)}, u32[]{:S(2)}) async-start(bf16[32,24,3072]{2,1,0:T(8,128)(2,1)} %bitcast.28), calls=%async_computation.1 | async-start | bytes 9437184 | tf_op jit(solution)/shard_map/all_to_all | solution.py:204
  59.9 2.8 collective-permute-start.6
  62.7 2.4 dynamic-slice_bitcast_fusion
  66.3 2.3 collective-permute-start.9
  68.6 49.6 %all-to-all-done.1 = bf16[32,24,3072]{2,1,0:T(8,128)(2,1)} async-done(((bf16[32,24,3072]{2,1,0:T(8,128)(2,1)}), bf16[32,24,3072]{2,1,0:T(8,128)(2,1)}, u32[]{:S(2)}, u32[]{:S(2)}) %all-to-all-start.1) | async-done | bytes 4718624 | tf_op jit(solution)/shard_map/all_to_all | solution.py:204
  118.2 1.9 copy-done
  120.1 6.0 %shard_map.85.refs_0_ = bf16[384,384]{1,0:T(8,128)(2,1)S(1)} custom-call(bf16[768,1024]{1,0:T(8,128)(2,1)S(1)} %bitcast.23, bf16[768,3072]{1,0:T(8,128)(2,1)} %bitcast.5.x_late, bf16[1,2,192,4096]{3,2,1,0:T(8,128)(2,1)S(1)} %copy-done), custom_call_target="tpu_custom_call" | custom-call | flops 2415919104 | bytes 9437184 | tf_op jit(solution)/shard_map/pallas_call | solution.py:60
  126.1 20.9 %collective-permute-done.6.table = bf16[1,2,192,4096]{3,2,1,0:T(8,128)(2,1)} collective-permute-done((bf16[1,2,192,4096]{3,2,1,0:T(8,128)(2,1)}, bf16[1,2,192,4096]{3,2,1,0:T(8,128)(2,1)}, u32[]{:S(2)}, u32[]{:S(2)}) %collective-permute-start.6) | collective-permute-done | bytes 3145760 | tf_op jit(solution)/shard_map/ppermute | solution.py:151
  147.0 7.0 %shard_map.86.refs_1_ = bf16[384,384]{1,0:T(8,128)(2,1)S(1)} custom-call(bf16[768,1024]{1,0:T(8,128)(2,1)S(1)} %bitcast.24, bf16[768,3072]{1,0:T(8,128)(2,1)} %bitcast.5.x_late, bf16[1,2,192,4096]{3,2,1,0:T(8,128)(2,1)} %collective-permute-done.6.table), custom_call_target="tpu_custom_call" | custom-call | flops 2415919104 | bytes 9437184 | tf_op jit(solution)/shard_map/pallas_call | solution.py:60
  154.0 2.7 collective-permute-start.8
  156.8 30.2 %collective-permute-done.9.refs_5_ = bf16[192,2048]{1,0:T(8,128)(2,1)} collective-permute-done((bf16[192,2048]{1,0:T(8,128)(2,1)S(1)}, bf16[192,2048]{1,0:T(8,128)(2,1)}, u32[]{:S(2)}, u32[]{:S(2)}) %collective-permute-start.9) | collective-permute-done | bytes 786464 | tf_op jit(solution)/shard_map/ppermute | solution.py:151
  188.3 6.3 %collective-permute-done.7.refs_2_ = bf16[384,384]{1,0:T(8,128)(2,1)S(1)} collective-permute-done((bf16[384,384]{1,0:T(8,128)(2,1)S(1)}, bf16[384,384]{1,0:T(8,128)(2,1)S(1)}, u32[]{:S(2)}, u32[]{:S(2)}) %collective-permute-start.7) | collective-permute-done | bytes 294944 | tf_op jit(solution)/shard_map/ppermute | solution.py:151
  194.6 5.0 %down.1 = bf16[768,2048]{1,0:T(8,128)(2,1)S(1)} custom-call(bf16[384,384]{1,0:T(8,128)(2,1)S(1)} %shard_map.85.refs_0_, bf16[384,384]{1,0:T(8,128)(2,1)S(1)} %shard_map.86.refs_1_, bf16[384,384]{1,0:T(8,128)(2,1)S(1)} %collective-permute-done.7.refs_2_, bf16[384,384]{1,0:T(8,128)(2,1)S(1)} %collective-permute-done.8.refs_3_, ...), custom_call_target="tpu_custom_call" | custom-call | flops 2415919104 | bytes 7471104 | tf_op jit(solution)/shard_map/down/pallas_call | solution.py:100
  201.3 13.2 %all-to-all-start.2 = ((bf16[32,24,2048]{2,1,0:T(8,128)(2,1)}), bf16[32,24,2048]{2,1,0:T(8,128)(2,1)}, u32[]{:S(2)}, u32[]{:S(2)}) async-start(bf16[32,24,2048]{2,1,0:T(8,128)(2,1)} %bitcast.27), calls=%async_computation.2 | async-start | bytes 6291456 | tf_op jit(solution)/shard_map/all_to_all | solution.py:204
  214.6 3.0 collective-permute-start.15
  220.6 33.7 %all-to-all-done.2 = bf16[32,24,2048]{2,1,0:T(8,128)(2,1)} async-done(((bf16[32,24,2048]{2,1,0:T(8,128)(2,1)}), bf16[32,24,2048]{2,1,0:T(8,128)(2,1)}, u32[]{:S(2)}, u32[]{:S(2)}) %all-to-all-start.2) | async-done | bytes 3145760 | tf_op jit(solution)/shard_map/all_to_all | solution.py:204
  254.4 3.0 fusion.18
  259.2 4.1 %collective-permute-start.12 = (bf16[32,2048]{1,0:T(8,128)(2,1)}, bf16[32,2048]{1,0:T(8,128)(2,1)S(1)}, u32[]{:S(2)}, u32[]{:S(2)}) collective-permute-start(bf16[32,2048]{1,0:T(8,128)(2,1)} %get-tuple-element.13), channel_id=1, source_target_pairs={{0,66},{2,64},{64,2},{66,0},{1,67},{3,65},{65,3},{67,1},{4,70},{6,... | collective-permute-start | bytes 393224 | tf_op jit(solution)/shard_map/ppermute | solution.py:151
  263.4 2.3 collective-permute-start.14
  265.6 89.2 %collective-permute-done.16 = bf16[1,192,4096]{2,1,0:T(8,128)(2,1)} collective-permute-done((bf16[1,192,4096]{2,1,0:T(8,128)(2,1)}, bf16[1,192,4096]{2,1,0:T(8,128)(2,1)}, u32[]{:S(2)}, u32[]{:S(2)}) %collective-permute-start.16) | collective-permute-done | bytes 1572896 | tf_op jit(solution)/shard_map/ppermute | solution.py:238
  354.8 1.9 broadcast_select_fusion
  356.8 6.5 %put.1 = bf16[384,4096]{1,0:T(8,128)(2,1)} custom-call(s32[1]{0:T(128)} %bitcast.12.moving, bf16[384,4096]{1,0:T(8,128)(2,1)} %collective-permute-done.15.got, bf16[384,4096]{1,0:T(8,128)(2,1)} %bitcast.25), custom_call_target="tpu_custom_call" | custom-call | bytes 9437184 | tf_op jit(solution)/shard_map/put/pallas_call | solution.py:133
  (66 shorter events, 20.2 us)
Async XLA Ops:
  3.3 8.0 %collective-permute-start = (bf16[32,1152]{1,0:T(8,128)(2,1)S(1)}, bf16[32,1152]{1,0:T(8,128)(2,1)S(1)}, u32[]{:S(2)}, u32[]{:S(2)}) collective-permute-start(bf16[32,1152]{1,0:T(8,128)(2,1)S(1)} %concatenate.25), channel_id=1, source_target_pairs={{0,66},{2,64},{64,2},{66,0},{1,67},{3,65},{65,3},{67,1},{4,70},{6,... | collective-permute-start | bytes 221192 | tf_op jit(solution)/shard_map/ppermute | solution.py:151
  8.1 5.8 %collective-permute-start.1 = (bf16[32,1152]{1,0:T(8,128)(2,1)S(1)}, bf16[32,1152]{1,0:T(8,128)(2,1)S(1)}, u32[]{:S(2)}, u32[]{:S(2)}) collective-permute-start(bf16[32,1152]{1,0:T(8,128)(2,1)S(1)} %concatenate.25), channel_id=1, source_target_pairs={{0,128},{128,0},{1,129},{129,1},{2,130},{130,2},{3,131},{131,3},{4... | collective-permute-start | bytes 221192 | tf_op jit(solution)/shard_map/ppermute | solution.py:151
  9.3 8.1 %collective-permute-start.2 = (bf16[32,1152]{1,0:T(8,128)(2,1)S(1)}, bf16[32,1152]{1,0:T(8,128)(2,1)S(1)}, u32[]{:S(2)}, u32[]{:S(2)}) collective-permute-start(bf16[32,1152]{1,0:T(8,128)(2,1)S(1)} %concatenate.25), channel_id=1, source_target_pairs={{0,194},{2,192},{64,130},{66,128},{128,66},{130,64},{192,2},{194,0... | collective-permute-start | bytes 221192 | tf_op jit(solution)/shard_map/ppermute | solution.py:151
  18.4 1.1 copy-start.4
  21.5 8.1 %copy-start.5 = (bf16[2,16,4096]{2,1,0:T(8,128)(2,1)S(1)}, bf16[2,16,4096]{2,1,0:T(8,128)(2,1)}, u32[]{:S(2)}) copy-start(bf16[2,16,4096]{2,1,0:T(8,128)(2,1)} %param.6) | copy-start | bytes 786436
  21.5 30.8 %all-to-all-start = ((bf16[32,24,1024]{2,1,0:T(8,128)(2,1)}), bf16[32,24,1024]{2,1,0:T(8,128)(2,1)S(1)}, u32[]{:S(2)}, u32[]{:S(2)}) async-start(bf16[32,24,1024]{2,1,0:T(8,128)(2,1)} %bitcast.2), calls=%async_computation | async-start | bytes 3145728 | tf_op jit(solution)/shard_map/all_to_all | solution.py:204
  29.6 17.5 %collective-permute-start.3 = (bf16[32,3072]{1,0:T(8,128)(2,1)S(1)}, bf16[32,3072]{1,0:T(8,128)(2,1)S(1)}, u32[]{:S(2)}, u32[]{:S(2)}) collective-permute-start(bf16[32,3072]{1,0:T(8,128)(2,1)S(1)} %slice.81), channel_id=1, source_target_pairs={{0,66},{2,64},{64,2},{66,0},{1,67},{3,65},{65,3},{67,1},{4,70},{6,... | collective-permute-start | bytes 589832 | tf_op jit(solution)/shard_map/ppermute | solution.py:151
  31.4 16.7 %collective-permute-start.4 = (bf16[32,3072]{1,0:T(8,128)(2,1)S(1)}, bf16[32,3072]{1,0:T(8,128)(2,1)S(1)}, u32[]{:S(2)}, u32[]{:S(2)}) collective-permute-start(bf16[32,3072]{1,0:T(8,128)(2,1)S(1)} %slice.81), channel_id=1, source_target_pairs={{0,128},{128,0},{1,129},{129,1},{2,130},{130,2},{3,131},{131,3},{4... | collective-permute-start | bytes 589832 | tf_op jit(solution)/shard_map/ppermute | solution.py:151
  32.6 15.5 %collective-permute-start.5 = (bf16[32,3072]{1,0:T(8,128)(2,1)S(1)}, bf16[32,3072]{1,0:T(8,128)(2,1)S(1)}, u32[]{:S(2)}, u32[]{:S(2)}) collective-permute-start(bf16[32,3072]{1,0:T(8,128)(2,1)S(1)} %slice.81), channel_id=1, source_target_pairs={{0,194},{2,192},{64,130},{66,128},{128,66},{130,64},{192,2},{194,0... | collective-permute-start | bytes 589832 | tf_op jit(solution)/shard_map/ppermute | solution.py:151
  52.2 65.9 %all-to-all-start.1 = ((bf16[32,24,3072]{2,1,0:T(8,128)(2,1)}), bf16[32,24,3072]{2,1,0:T(8,128)(2,1)}, u32[]{:S(2)}, u32[]{:S(2)}) async-start(bf16[32,24,3072]{2,1,0:T(8,128)(2,1)} %bitcast.28), calls=%async_computation.1 | async-start | bytes 9437184 | tf_op jit(solution)/shard_map/all_to_all | solution.py:204
  59.9 87.1 %collective-permute-start.6 = (bf16[1,2,192,4096]{3,2,1,0:T(8,128)(2,1)}, bf16[1,2,192,4096]{3,2,1,0:T(8,128)(2,1)}, u32[]{:S(2)}, u32[]{:S(2)}) collective-permute-start(bf16[1,2,192,4096]{3,2,1,0:T(8,128)(2,1)} %table.1), channel_id=1, source_target_pairs={{0,64},{64,0},{1,65},{65,1},{2,66},{66,2},{3,67},{67,3},{4,68},{68... | collective-permute-start | bytes 9437192 | tf_op jit(solution)/shard_map/ppermute | solution.py:151
  65.1 91.8 %collective-permute-start.10 = (bf16[192,2048]{1,0:T(8,128)(2,1)}, bf16[192,2048]{1,0:T(8,128)(2,1)S(1)}, u32[]{:S(2)}, u32[]{:S(2)}) collective-permute-start(bf16[192,2048]{1,0:T(8,128)(2,1)} %get-tuple-element.9), channel_id=1, source_target_pairs={{0,128},{128,0},{1,129},{129,1},{2,130},{130,2},{3,131},{131,3},{4... | collective-permute-start | bytes 2359304 | tf_op jit(solution)/shard_map/ppermute | solution.py:151
  65.5 91.3 %collective-permute-start.11 = (bf16[192,2048]{1,0:T(8,128)(2,1)}, bf16[192,2048]{1,0:T(8,128)(2,1)}, u32[]{:S(2)}, u32[]{:S(2)}) collective-permute-start(bf16[192,2048]{1,0:T(8,128)(2,1)} %get-tuple-element.9), channel_id=1, source_target_pairs={{0,192},{64,128},{128,64},{192,0},{1,193},{65,129},{129,65},{193,1... | collective-permute-start | bytes 2359304 | tf_op jit(solution)/shard_map/ppermute | solution.py:151
  66.3 120.7 %collective-permute-start.9 = (bf16[192,2048]{1,0:T(8,128)(2,1)S(1)}, bf16[192,2048]{1,0:T(8,128)(2,1)}, u32[]{:S(2)}, u32[]{:S(2)}) collective-permute-start(bf16[192,2048]{1,0:T(8,128)(2,1)S(1)} %get-tuple-element.10.refs_4_), channel_id=1, source_target_pairs={{0,64},{64,0},{1,65},{65,1},{2,66},{66,2},{3,67},{67,3},{4,68},{68... | collective-permute-start | bytes 2359304 | tf_op jit(solution)/shard_map/ppermute | solution.py:151
  118.2 1.9 copy-start
  154.0 34.3 %collective-permute-start.8 = (bf16[384,384]{1,0:T(8,128)(2,1)S(1)}, bf16[384,384]{1,0:T(8,128)(2,1)S(1)}, u32[]{:S(2)}, u32[]{:S(2)}) collective-permute-start(bf16[384,384]{1,0:T(8,128)(2,1)S(1)} %shard_map.86.refs_1_), channel_id=1, source_target_pairs={{0,128},{128,0},{1,129},{129,1},{2,130},{130,2},{3,131},{131,3},{4... | collective-permute-start | bytes 884744 | tf_op jit(solution)/shard_map/ppermute | solution.py:151
  156.7 37.9 %collective-permute-start.7 = (bf16[384,384]{1,0:T(8,128)(2,1)S(1)}, bf16[384,384]{1,0:T(8,128)(2,1)S(1)}, u32[]{:S(2)}, u32[]{:S(2)}) collective-permute-start(bf16[384,384]{1,0:T(8,128)(2,1)S(1)} %shard_map.85.refs_0_), channel_id=1, source_target_pairs={{0,128},{128,0},{1,129},{129,1},{2,130},{130,2},{3,131},{131,3},{4... | collective-permute-start | bytes 884744 | tf_op jit(solution)/shard_map/ppermute | solution.py:151
  199.7 1.7 copy-start.2
  201.3 13.2 %copy-start.1 = (bf16[1,2,192,4096]{3,2,1,0:T(8,128)(2,1)S(1)}, bf16[1,2,192,4096]{3,2,1,0:T(8,128)(2,1)}, u32[]{:S(2)}) copy-start(bf16[1,2,192,4096]{3,2,1,0:T(8,128)(2,1)} %table.1) | copy-start | bytes 9437188
  201.3 16.3 %copy-start.6 = (s32[8,2]{0,1:T(2,128)S(1)}, s32[8,2]{0,1:T(2,128)}, u32[]{:S(2)}) copy-start(s32[8,2]{0,1:T(2,128)} %param.11) | copy-start | bytes 196
  201.3 53.0 %all-to-all-start.2 = ((bf16[32,24,2048]{2,1,0:T(8,128)(2,1)}), bf16[32,24,2048]{2,1,0:T(8,128)(2,1)}, u32[]{:S(2)}, u32[]{:S(2)}) async-start(bf16[32,24,2048]{2,1,0:T(8,128)(2,1)} %bitcast.27), calls=%async_computation.2 | async-start | bytes 6291456 | tf_op jit(solution)/shard_map/all_to_all | solution.py:204
  214.6 142.2 %collective-permute-start.15 = (bf16[384,4096]{1,0:T(8,128)(2,1)S(1)}, bf16[384,4096]{1,0:T(8,128)(2,1)}, u32[]{:S(2)}, u32[]{:S(2)}) collective-permute-start(bf16[384,4096]{1,0:T(8,128)(2,1)S(1)} %bitcast.26), channel_id=1, source_target_pairs={{0,32},{16,48},{32,0},{48,16},{1,33},{17,49},{33,1},{49,17},{2,34}... | collective-permute-start | bytes 9437192 | tf_op jit(solution)/shard_map/ppermute | solution.py:261
  217.5 137.3 %collective-permute-start.16 = (bf16[1,192,4096]{2,1,0:T(8,128)(2,1)}, bf16[1,192,4096]{2,1,0:T(8,128)(2,1)}, u32[]{:S(2)}, u32[]{:S(2)}) collective-permute-start(bf16[1,192,4096]{2,1,0:T(8,128)(2,1)} %param.10), channel_id=1, source_target_pairs={{0,32},{16,48},{32,0},{48,16},{1,33},{17,49},{33,1},{49,17},{2,34}... | collective-permute-start | bytes 4718600 | tf_op jit(solution)/shard_map/ppermute | solution.py:238
  257.4 97.5 %copy-start.3 = (bf16[1,192,4096]{2,1,0:T(8,128)(2,1)S(1)}, bf16[1,192,4096]{2,1,0:T(8,128)(2,1)}, u32[]{:S(2)}) copy-start(bf16[1,192,4096]{2,1,0:T(8,128)(2,1)} %param.10) | copy-start | bytes 4718596
  259.2 104.0 %collective-permute-start.12 = (bf16[32,2048]{1,0:T(8,128)(2,1)}, bf16[32,2048]{1,0:T(8,128)(2,1)S(1)}, u32[]{:S(2)}, u32[]{:S(2)}) collective-permute-start(bf16[32,2048]{1,0:T(8,128)(2,1)} %get-tuple-element.13), channel_id=1, source_target_pairs={{0,66},{2,64},{64,2},{66,0},{1,67},{3,65},{65,3},{67,1},{4,70},{6,... | collective-permute-start | bytes 393224 | tf_op jit(solution)/shard_map/ppermute | solution.py:151
  263.4 99.9 %collective-permute-start.13 = (bf16[32,2048]{1,0:T(8,128)(2,1)}, bf16[32,2048]{1,0:T(8,128)(2,1)S(1)}, u32[]{:S(2)}, u32[]{:S(2)}) collective-permute-start(bf16[32,2048]{1,0:T(8,128)(2,1)} %get-tuple-element.15), channel_id=1, source_target_pairs={{0,128},{128,0},{1,129},{129,1},{2,130},{130,2},{3,131},{131,3},{4... | collective-permute-start | bytes 393224 | tf_op jit(solution)/shard_map/ppermute | solution.py:151
  263.4 99.9 %collective-permute-start.14 = (bf16[32,2048]{1,0:T(8,128)(2,1)}, bf16[32,2048]{1,0:T(8,128)(2,1)S(1)}, u32[]{:S(2)}, u32[]{:S(2)}) collective-permute-start(bf16[32,2048]{1,0:T(8,128)(2,1)} %get-tuple-element.14), channel_id=1, source_target_pairs={{0,194},{2,192},{64,130},{66,128},{128,66},{130,64},{192,2},{194,0... | collective-permute-start | bytes 393224 | tf_op jit(solution)/shard_map/ppermute | solution.py:151

commit v7 on v6

--- a/solution.py
+++ b/solution.py
@@ -13,6 +13,7 @@
 CAP = 3
 CHUNK = 1024
 META = 128
+HEAD = 320
 PLANE = ("x", "y", "c")
 CROSS = ("ql", "h")
 
@@ -116,7 +117,9 @@
     )(*hiddens, *pieces)
 
 
-def put_kernel(moving, got, own, out):
+def put_kernel(moving, got, own, *refs):
+    out = refs[-1]
+
     @pl.when(moving[0] != 0)
     def _():
         out[...] = got[...]
@@ -126,24 +129,33 @@
         out[...] = own[...]
 
 
-def put(moving, got, own):
+def put(moving, got, own, first, base=None):
     block = 64
     depth = own.shape[1]
-    spec = pl.BlockSpec((block, depth), lambda i, m: (i, 0))
+    start = first // block
+    here = pl.BlockSpec((block, depth), lambda i, m: (start + i, 0))
+    specs = [pl.BlockSpec((block, depth), lambda i, m: (i, 0)), here]
+    args = [moving, got, own]
+    aliases = {}
+    if base is not None:
+        specs.append(pl.BlockSpec(memory_space=pl.ANY))
+        args.append(base)
+        aliases = {3: 0}
     return pl.pallas_call(
         put_kernel,
         grid_spec=pltpu.PrefetchScalarGridSpec(
             num_scalar_prefetch=1,
             grid=(got.shape[0] // block,),
-            in_specs=[spec, spec],
-            out_specs=spec,
+            in_specs=specs,
+            out_specs=here,
         ),
         out_shape=jax.ShapeDtypeStruct(own.shape, own.dtype),
+        input_output_aliases=aliases,
         cost_estimate=pl.CostEstimate(
             flops=0, bytes_accessed=6 * got.shape[0] * depth, transcendentals=0
         ),
         name="put",
-    )(moving, got, own)
+    )(*args)
 
 
 def swap(value, axes):
@@ -258,7 +270,9 @@
     hidden_b = up(x0, x1, gu_b, late)
     got_b = swap(hidden_b, ("qh",))
     table = gate_up.reshape(-1, depth)
-    got_gu = lax.ppermute(table, ("x",), across_x)
+    top, rest = table[:HEAD], table[HEAD:]
+    got_gu0 = lax.ppermute(top, ("x",), across_x)
+    got_gu1 = lax.ppermute(rest, ("x",), across_x)
     made = down((hidden_a, hidden_b, got_a, got_b), pieces)
     back = across(made, experts)
     both = jnp.dot(mix, back, preferred_element_type=F32)
@@ -273,7 +287,8 @@
     )
     moving = jnp.any(pairs == slot)
     flag = jnp.sum((pairs == slot).astype(jnp.int32)).reshape(1)
-    new_gu = put(flag, got_gu, table)
+    new_gu = put(flag, got_gu0, table, 0)
+    new_gu = put(flag, got_gu1, table, HEAD, new_gu)
     new_dn = jnp.where(moving, got_dn, down_proj)
     return (
         out.astype(BF16).reshape(steps, rows, depth),

time: 370 us -> 366 us (0.989)
  waiting for transfers between devices: 252 us -> 241 us
    ppermute x1, waiting for transfers between devices: 89.2 us -> 25.8 us  [local(): got_dn = lax.ppermute(down_proj, ('x',), across_x)]
    ppermute x1 -> x2, waiting for transfers between devices: 0.01 us -> 57 us  [the longest x1 52 us: local(): got_gu0 = lax.ppermute(top, ('x',), across_x)]
    all_to_all x3, waiting for transfers between devices: 83.8 us -> 78.7 us  [across(): lax.all_to_all(value.reshape(experts, slots // experts, depth), PLANE, 0,...]
    pallas_call x1 -> x2, Pallas kernels: 6.46 us -> 8.75 us  [put(): pl.pallas_call(put_kernel, grid_spec=pltpu.PrefetchScalarGridSpec(num_sca...]
  transfers between devices with their start and end apart: 20 -> 21, of which waited for: 13 -> 15; matrix products, arithmetic and copies ran while one was open for 4% -> 5% of each run, Pallas kernels for 5% -> 6%
where the time goes in v7:
time: 366 us; the launch traced here: 360 us
  waiting for transfers between devices  241 us (66%)
  starting transfers between devices  62.2 us (17%)
  Pallas kernels  27.3 us (7%)
  local copies, waits for them, and re-layouts  13.6 us (4%)
  matrix products  8.84 us (2%)
  other arithmetic  6.45 us (2%)
    ppermute x15, waiting for transfers between devices, swap(): return lax.ppermute(value, axes, [(i, i ^ count - 1) for i in range(count)])  79.5 us
    all_to_all x3, waiting for transfers between devices, across(): lax.all_to_all(value.reshape(experts, slots // experts, depth), PLANE, 0,...  78.7 us
    ppermute x1, waiting for transfers between devices, local(): got_gu0 = lax.ppermute(top, ('x',), across_x)  52 us
    all_to_all x3, starting transfers between devices, across(): lax.all_to_all(value.reshape(experts, slots // experts, depth), PLANE, 0,...  28.9 us
    ppermute x15, starting transfers between devices, swap(): return lax.ppermute(value, axes, [(i, i ^ count - 1) for i in range(count)])  27.4 us
    ppermute x1, waiting for transfers between devices, local(): got_dn = lax.ppermute(down_proj, ('x',), across_x)  25.8 us
    pallas_call x2, Pallas kernels, up(): pl.pallas_call(functools.partial(up_kernel, at), in_specs=[FAR, RESIDENT,...  13.1 us
    pallas_call x2, Pallas kernels, put(): pl.pallas_call(put_kernel, grid_spec=pltpu.PrefetchScalarGridSpec(num_sca...  8.75 us
  transfers between devices with their start and end apart: 21, of which 15 were waited for; matrix products, arithmetic and copies ran while one was open for 5% of the time, Pallas kernels for 6%

profile of v7, /device:TPU:65, one launch (start us, length us, event | category | flops | bytes accessed | tf_op | source)
XLA Modules:
  0.0 360.4 jit_solution(1516485246363508753)
XLA Ops:
  3.3 4.7 %collective-permute-start = (bf16[32,1152]{1,0:T(8,128)(2,1)S(1)}, bf16[32,1152]{1,0:T(8,128)(2,1)S(1)}, u32[]{:S(2)}, u32[]{:S(2)}) collective-permute-start(bf16[32,1152]{1,0:T(8,128)(2,1)S(1)} %concatenate.25), channel_id=1, source_target_pairs={{0,66},{2,64},{64,2},{66,0},{1,67},{3,65},{65,3},{67,1},{4,70},{6,... | collective-permute-start | bytes 221192 | tf_op jit(solution)/shard_map/ppermute | solution.py:163
  11.4 2.5 collective-permute-done.1
  13.9 3.4 collective-permute-done.2
  21.5 8.1 %all-to-all-start = ((bf16[32,24,1024]{2,1,0:T(8,128)(2,1)}), bf16[32,24,1024]{2,1,0:T(8,128)(2,1)S(1)}, u32[]{:S(2)}, u32[]{:S(2)}) async-start(bf16[32,24,1024]{2,1,0:T(8,128)(2,1)} %bitcast.2), calls=%async_computation | async-start | bytes 3145728 | tf_op jit(solution)/shard_map/all_to_all | solution.py:216
  32.6 2.7 collective-permute-start.5
  35.3 11.7 %collective-permute-done.3 = bf16[32,3072]{1,0:T(8,128)(2,1)S(1)} collective-permute-done((bf16[32,3072]{1,0:T(8,128)(2,1)S(1)}, bf16[32,3072]{1,0:T(8,128)(2,1)S(1)}, u32[]{:S(2)}, u32[]{:S(2)}) %collective-permute-start.3) | collective-permute-done | bytes 196640 | tf_op jit(solution)/shard_map/ppermute | solution.py:163
  48.1 3.6 %convolution_convert_fusion = bf16[768,3072]{1,0:T(8,128)(2,1)} fusion(pred[128,768]{1,0:T(32,128)(4,1)S(1)} %get-tuple-element.8, bf16[32,3072]{1,0:T(8,128)(2,1)S(1)} %collective-permute-done.5, bf16[32,3072]{1,0:T(8,128)(2,1)S(1)} %collective-permute-done.4, bf16[32,3072]{1,0:T(8,128)(2,1)S(1)} %collective-permute-done.3, bf16[32,3072]{1,0:T(8,128)(2,1)S(1)} %slice.89), kind=kOutput, calls=%fused_computation | convolution fusion | flops 609484800 | bytes 5603328 | tf_op jit(solution)/shard_map/dot_general | solution.py:209
  53.4 7.9 %all-to-all-start.1 = ((bf16[32,24,3072]{2,1,0:T(8,128)(2,1)}), bf16[32,24,3072]{2,1,0:T(8,128)(2,1)}, u32[]{:S(2)}, u32[]{:S(2)}) async-start(bf16[32,24,3072]{2,1,0:T(8,128)(2,1)} %bitcast.30), calls=%async_computation.1 | async-start | bytes 9437184 | tf_op jit(solution)/shard_map/all_to_all | solution.py:216
  61.3 2.8 collective-permute-start.6
  64.1 2.7 dynamic-slice_bitcast_fusion
  68.0 2.3 collective-permute-start.9
  70.3 49.2 %all-to-all-done.1 = bf16[32,24,3072]{2,1,0:T(8,128)(2,1)} async-done(((bf16[32,24,3072]{2,1,0:T(8,128)(2,1)}), bf16[32,24,3072]{2,1,0:T(8,128)(2,1)}, u32[]{:S(2)}, u32[]{:S(2)}) %all-to-all-start.1) | async-done | bytes 4718624 | tf_op jit(solution)/shard_map/all_to_all | solution.py:216
  121.0 6.0 %shard_map.85.refs_0_ = bf16[384,384]{1,0:T(8,128)(2,1)S(1)} custom-call(bf16[768,1024]{1,0:T(8,128)(2,1)S(1)} %bitcast.27, bf16[768,3072]{1,0:T(8,128)(2,1)} %bitcast.5.x_late, bf16[1,2,192,4096]{3,2,1,0:T(8,128)(2,1)S(1)} %copy-done), custom_call_target="tpu_custom_call" | custom-call | flops 2415919104 | bytes 9437184 | tf_op jit(solution)/shard_map/pallas_call | solution.py:61
  127.0 21.1 %collective-permute-done.6.table = bf16[1,2,192,4096]{3,2,1,0:T(8,128)(2,1)} collective-permute-done((bf16[1,2,192,4096]{3,2,1,0:T(8,128)(2,1)S(1)}, bf16[1,2,192,4096]{3,2,1,0:T(8,128)(2,1)}, u32[]{:S(2)}, u32[]{:S(2)}) %collective-permute-start.6) | collective-permute-done | bytes 3145760 | tf_op jit(solution)/shard_map/ppermute | solution.py:163
  148.1 7.0 %shard_map.86.refs_1_ = bf16[384,384]{1,0:T(8,128)(2,1)S(1)} custom-call(bf16[768,1024]{1,0:T(8,128)(2,1)S(1)} %bitcast.28, bf16[768,3072]{1,0:T(8,128)(2,1)} %bitcast.5.x_late, bf16[1,2,192,4096]{3,2,1,0:T(8,128)(2,1)} %collective-permute-done.6.table), custom_call_target="tpu_custom_call" | custom-call | flops 2415919104 | bytes 9437184 | tf_op jit(solution)/shard_map/pallas_call | solution.py:61
  155.1 2.8 collective-permute-start.8
  158.0 30.3 %collective-permute-done.9.refs_5_ = bf16[192,2048]{1,0:T(8,128)(2,1)} collective-permute-done((bf16[192,2048]{1,0:T(8,128)(2,1)}, bf16[192,2048]{1,0:T(8,128)(2,1)}, u32[]{:S(2)}, u32[]{:S(2)}) %collective-permute-start.9) | collective-permute-done | bytes 786464 | tf_op jit(solution)/shard_map/ppermute | solution.py:163
  189.5 6.3 %collective-permute-done.7.refs_2_ = bf16[384,384]{1,0:T(8,128)(2,1)S(1)} collective-permute-done((bf16[384,384]{1,0:T(8,128)(2,1)S(1)}, bf16[384,384]{1,0:T(8,128)(2,1)S(1)}, u32[]{:S(2)}, u32[]{:S(2)}) %collective-permute-start.7) | collective-permute-done | bytes 294944 | tf_op jit(solution)/shard_map/ppermute | solution.py:163
  195.8 5.5 %down.1 = bf16[768,2048]{1,0:T(8,128)(2,1)S(1)} custom-call(bf16[384,384]{1,0:T(8,128)(2,1)S(1)} %shard_map.85.refs_0_, bf16[384,384]{1,0:T(8,128)(2,1)S(1)} %shard_map.86.refs_1_, bf16[384,384]{1,0:T(8,128)(2,1)S(1)} %collective-permute-done.7.refs_2_, bf16[384,384]{1,0:T(8,128)(2,1)S(1)} %collective-permute-done.8.refs_3_, ...), custom_call_target="tpu_custom_call" | custom-call | flops 2415919104 | bytes 7471104 | tf_op jit(solution)/shard_map/down/pallas_call | solution.py:101
  203.0 12.9 %all-to-all-start.2 = ((bf16[32,24,2048]{2,1,0:T(8,128)(2,1)}), bf16[32,24,2048]{2,1,0:T(8,128)(2,1)}, u32[]{:S(2)}, u32[]{:S(2)}) async-start(bf16[32,24,2048]{2,1,0:T(8,128)(2,1)} %bitcast.29), calls=%async_computation.2 | async-start | bytes 6291456 | tf_op jit(solution)/shard_map/all_to_all | solution.py:216
  215.9 3.0 collective-permute-start.17
  221.5 2.9 collective-permute-start.15
  226.7 29.0 %all-to-all-done.2 = bf16[32,24,2048]{2,1,0:T(8,128)(2,1)} async-done(((bf16[32,24,2048]{2,1,0:T(8,128)(2,1)}), bf16[32,24,2048]{2,1,0:T(8,128)(2,1)}, u32[]{:S(2)}, u32[]{:S(2)}) %all-to-all-start.2) | async-done | bytes 3145760 | tf_op jit(solution)/shard_map/all_to_all | solution.py:216
  255.7 2.9 fusion.18
  258.8 4.2 %collective-permute-start.12 = (bf16[32,2048]{1,0:T(8,128)(2,1)S(1)}, bf16[32,2048]{1,0:T(8,128)(2,1)S(1)}, u32[]{:S(2)}, u32[]{:S(2)}) collective-permute-start(bf16[32,2048]{1,0:T(8,128)(2,1)S(1)} %get-tuple-element.13), channel_id=1, source_target_pairs={{0,66},{2,64},{64,2},{66,0},{1,67},{3,65},{65,3},{67,1},{4,70},{6,... | collective-permute-start | bytes 393224 | tf_op jit(solution)/shard_map/ppermute | solution.py:163
  263.0 25.8 %collective-permute-done.17 = bf16[1,192,4096]{2,1,0:T(8,128)(2,1)} collective-permute-done((bf16[1,192,4096]{2,1,0:T(8,128)(2,1)}, bf16[1,192,4096]{2,1,0:T(8,128)(2,1)}, u32[]{:S(2)}, u32[]{:S(2)}) %collective-permute-start.17) | collective-permute-done | bytes 1572896 | tf_op jit(solution)/shard_map/ppermute | solution.py:250
  288.8 2.2 collective-permute-start.14
  291.0 2.0 broadcast_select_fusion
  293.0 52.0 %collective-permute-done.16.got = bf16[320,4096]{1,0:T(8,128)(2,1)} collective-permute-done((bf16[320,4096]{1,0:T(8,128)(2,1)}, bf16[320,4096]{1,0:T(8,128)(2,1)}, u32[]{:S(2)}, u32[]{:S(2)}) %collective-permute-start.16) | collective-permute-done | bytes 2621472 | tf_op jit(solution)/shard_map/ppermute | solution.py:274
  345.0 6.1 %put.2.refs_0_ = bf16[384,4096]{1,0:T(8,128)(2,1)} custom-call(s32[1]{0:T(128)} %bitcast.12.moving, bf16[320,4096]{1,0:T(8,128)(2,1)} %collective-permute-done.16.got, bf16[384,4096]{1,0:T(8,128)(2,1)} %bitcast.23), custom_call_target="tpu_custom_call" | custom-call | bytes 7864320 | tf_op jit(solution)/shard_map/put/pallas_call | solution.py:144
  351.1 5.1 %collective-permute-done.15.got = bf16[64,4096]{1,0:T(8,128)(2,1)S(1)} collective-permute-done((bf16[64,4096]{1,0:T(8,128)(2,1)}, bf16[64,4096]{1,0:T(8,128)(2,1)S(1)}, u32[]{:S(2)}, u32[]{:S(2)}) %collective-permute-start.15) | collective-permute-done | bytes 524320 | tf_op jit(solution)/shard_map/ppermute | solution.py:275
  356.9 2.7 put.3
  (75 shorter events, 28.1 us)
Async XLA Ops:
  3.3 8.0 %collective-permute-start = (bf16[32,1152]{1,0:T(8,128)(2,1)S(1)}, bf16[32,1152]{1,0:T(8,128)(2,1)S(1)}, u32[]{:S(2)}, u32[]{:S(2)}) collective-permute-start(bf16[32,1152]{1,0:T(8,128)(2,1)S(1)} %concatenate.25), channel_id=1, source_target_pairs={{0,66},{2,64},{64,2},{66,0},{1,67},{3,65},{65,3},{67,1},{4,70},{6,... | collective-permute-start | bytes 221192 | tf_op jit(solution)/shard_map/ppermute | solution.py:163
  8.1 5.8 %collective-permute-start.1 = (bf16[32,1152]{1,0:T(8,128)(2,1)S(1)}, bf16[32,1152]{1,0:T(8,128)(2,1)S(1)}, u32[]{:S(2)}, u32[]{:S(2)}) collective-permute-start(bf16[32,1152]{1,0:T(8,128)(2,1)S(1)} %concatenate.25), channel_id=1, source_target_pairs={{0,128},{128,0},{1,129},{129,1},{2,130},{130,2},{3,131},{131,3},{4... | collective-permute-start | bytes 221192 | tf_op jit(solution)/shard_map/ppermute | solution.py:163
  9.3 8.1 %collective-permute-start.2 = (bf16[32,1152]{1,0:T(8,128)(2,1)S(1)}, bf16[32,1152]{1,0:T(8,128)(2,1)S(1)}, u32[]{:S(2)}, u32[]{:S(2)}) collective-permute-start(bf16[32,1152]{1,0:T(8,128)(2,1)S(1)} %concatenate.25), channel_id=1, source_target_pairs={{0,194},{2,192},{64,130},{66,128},{128,66},{130,64},{192,2},{194,0... | collective-permute-start | bytes 221192 | tf_op jit(solution)/shard_map/ppermute | solution.py:163
  18.4 1.1 copy-start.5
  21.5 8.1 %copy-start.7 = (bf16[2,16,4096]{2,1,0:T(8,128)(2,1)S(1)}, bf16[2,16,4096]{2,1,0:T(8,128)(2,1)}, u32[]{:S(2)}) copy-start(bf16[2,16,4096]{2,1,0:T(8,128)(2,1)} %param.6) | copy-start | bytes 786436
  21.5 30.8 %all-to-all-start = ((bf16[32,24,1024]{2,1,0:T(8,128)(2,1)}), bf16[32,24,1024]{2,1,0:T(8,128)(2,1)S(1)}, u32[]{:S(2)}, u32[]{:S(2)}) async-start(bf16[32,24,1024]{2,1,0:T(8,128)(2,1)} %bitcast.2), calls=%async_computation | async-start | bytes 3145728 | tf_op jit(solution)/shard_map/all_to_all | solution.py:216
  29.6 17.4 %collective-permute-start.3 = (bf16[32,3072]{1,0:T(8,128)(2,1)S(1)}, bf16[32,3072]{1,0:T(8,128)(2,1)S(1)}, u32[]{:S(2)}, u32[]{:S(2)}) collective-permute-start(bf16[32,3072]{1,0:T(8,128)(2,1)S(1)} %slice.89), channel_id=1, source_target_pairs={{0,66},{2,64},{64,2},{66,0},{1,67},{3,65},{65,3},{67,1},{4,70},{6,... | collective-permute-start | bytes 589832 | tf_op jit(solution)/shard_map/ppermute | solution.py:163
  31.4 16.7 %collective-permute-start.4 = (bf16[32,3072]{1,0:T(8,128)(2,1)S(1)}, bf16[32,3072]{1,0:T(8,128)(2,1)S(1)}, u32[]{:S(2)}, u32[]{:S(2)}) collective-permute-start(bf16[32,3072]{1,0:T(8,128)(2,1)S(1)} %slice.89), channel_id=1, source_target_pairs={{0,128},{128,0},{1,129},{129,1},{2,130},{130,2},{3,131},{131,3},{4... | collective-permute-start | bytes 589832 | tf_op jit(solution)/shard_map/ppermute | solution.py:163
  32.6 15.5 %collective-permute-start.5 = (bf16[32,3072]{1,0:T(8,128)(2,1)S(1)}, bf16[32,3072]{1,0:T(8,128)(2,1)S(1)}, u32[]{:S(2)}, u32[]{:S(2)}) collective-permute-start(bf16[32,3072]{1,0:T(8,128)(2,1)S(1)} %slice.89), channel_id=1, source_target_pairs={{0,194},{2,192},{64,130},{66,128},{128,66},{130,64},{192,2},{194,0... | collective-permute-start | bytes 589832 | tf_op jit(solution)/shard_map/ppermute | solution.py:163
  52.2 1.1 copy-start.1
  53.4 7.9 %copy-start = (bf16[1,2,192,4096]{3,2,1,0:T(8,128)(2,1)S(1)}, bf16[1,2,192,4096]{3,2,1,0:T(8,128)(2,1)}, u32[]{:S(2)}) copy-start(bf16[1,2,192,4096]{3,2,1,0:T(8,128)(2,1)} %table.1) | copy-start | bytes 9437188
  53.4 66.2 %all-to-all-start.1 = ((bf16[32,24,3072]{2,1,0:T(8,128)(2,1)}), bf16[32,24,3072]{2,1,0:T(8,128)(2,1)}, u32[]{:S(2)}, u32[]{:S(2)}) async-start(bf16[32,24,3072]{2,1,0:T(8,128)(2,1)} %bitcast.30), calls=%async_computation.1 | async-start | bytes 9437184 | tf_op jit(solution)/shard_map/all_to_all | solution.py:216
  61.3 86.8 %collective-permute-start.6 = (bf16[1,2,192,4096]{3,2,1,0:T(8,128)(2,1)S(1)}, bf16[1,2,192,4096]{3,2,1,0:T(8,128)(2,1)}, u32[]{:S(2)}, u32[]{:S(2)}) collective-permute-start(bf16[1,2,192,4096]{3,2,1,0:T(8,128)(2,1)S(1)} %copy-done), channel_id=1, source_target_pairs={{0,64},{64,0},{1,65},{65,1},{2,66},{66,2},{3,67},{67,3},{4,68},{68... | collective-permute-start | bytes 9437192 | tf_op jit(solution)/shard_map/ppermute | solution.py:163
  66.8 91.2 %collective-permute-start.10 = (bf16[192,2048]{1,0:T(8,128)(2,1)}, bf16[192,2048]{1,0:T(8,128)(2,1)}, u32[]{:S(2)}, u32[]{:S(2)}) collective-permute-start(bf16[192,2048]{1,0:T(8,128)(2,1)} %get-tuple-element.9), channel_id=1, source_target_pairs={{0,128},{128,0},{1,129},{129,1},{2,130},{130,2},{3,131},{131,3},{4... | collective-permute-start | bytes 2359304 | tf_op jit(solution)/shard_map/ppermute | solution.py:163
  67.2 90.8 %collective-permute-start.11 = (bf16[192,2048]{1,0:T(8,128)(2,1)}, bf16[192,2048]{1,0:T(8,128)(2,1)}, u32[]{:S(2)}, u32[]{:S(2)}) collective-permute-start(bf16[192,2048]{1,0:T(8,128)(2,1)} %get-tuple-element.9), channel_id=1, source_target_pairs={{0,192},{64,128},{128,64},{192,0},{1,193},{65,129},{129,65},{193,1... | collective-permute-start | bytes 2359304 | tf_op jit(solution)/shard_map/ppermute | solution.py:163
  68.0 120.3 %collective-permute-start.9 = (bf16[192,2048]{1,0:T(8,128)(2,1)}, bf16[192,2048]{1,0:T(8,128)(2,1)}, u32[]{:S(2)}, u32[]{:S(2)}) collective-permute-start(bf16[192,2048]{1,0:T(8,128)(2,1)} %get-tuple-element.10.refs_4_), channel_id=1, source_target_pairs={{0,64},{64,0},{1,65},{65,1},{2,66},{66,2},{3,67},{67,3},{4,68},{68... | collective-permute-start | bytes 2359304 | tf_op jit(solution)/shard_map/ppermute | solution.py:163
  119.5 1.4 copy-start.2
  155.1 34.4 %collective-permute-start.8 = (bf16[384,384]{1,0:T(8,128)(2,1)S(1)}, bf16[384,384]{1,0:T(8,128)(2,1)S(1)}, u32[]{:S(2)}, u32[]{:S(2)}) collective-permute-start(bf16[384,384]{1,0:T(8,128)(2,1)S(1)} %shard_map.86.refs_1_), channel_id=1, source_target_pairs={{0,128},{128,0},{1,129},{129,1},{2,130},{130,2},{3,131},{131,3},{4... | collective-permute-start | bytes 884744 | tf_op jit(solution)/shard_map/ppermute | solution.py:163
  157.9 37.9 %collective-permute-start.7 = (bf16[384,384]{1,0:T(8,128)(2,1)S(1)}, bf16[384,384]{1,0:T(8,128)(2,1)S(1)}, u32[]{:S(2)}, u32[]{:S(2)}) collective-permute-start(bf16[384,384]{1,0:T(8,128)(2,1)S(1)} %shard_map.85.refs_0_), channel_id=1, source_target_pairs={{0,128},{128,0},{1,129},{129,1},{2,130},{130,2},{3,131},{131,3},{4... | collective-permute-start | bytes 884744 | tf_op jit(solution)/shard_map/ppermute | solution.py:163
  201.3 1.7 copy-start.3
  203.0 52.7 %all-to-all-start.2 = ((bf16[32,24,2048]{2,1,0:T(8,128)(2,1)}), bf16[32,24,2048]{2,1,0:T(8,128)(2,1)}, u32[]{:S(2)}, u32[]{:S(2)}) async-start(bf16[32,24,2048]{2,1,0:T(8,128)(2,1)} %bitcast.29), calls=%async_computation.2 | async-start | bytes 6291456 | tf_op jit(solution)/shard_map/all_to_all | solution.py:216
  215.9 72.9 %collective-permute-start.17 = (bf16[1,192,4096]{2,1,0:T(8,128)(2,1)}, bf16[1,192,4096]{2,1,0:T(8,128)(2,1)}, u32[]{:S(2)}, u32[]{:S(2)}) collective-permute-start(bf16[1,192,4096]{2,1,0:T(8,128)(2,1)} %param.10), channel_id=1, source_target_pairs={{0,32},{16,48},{32,0},{48,16},{1,33},{17,49},{33,1},{49,17},{2,34}... | collective-permute-start | bytes 4718600 | tf_op jit(solution)/shard_map/ppermute | solution.py:250
  218.9 5.5 %copy-start.8 = (s32[8,2]{0,1:T(2,128)S(1)}, s32[8,2]{0,1:T(2,128)}, u32[]{:S(2)}) copy-start(s32[8,2]{0,1:T(2,128)} %param.11) | copy-start | bytes 196
  220.6 124.4 %collective-permute-start.16 = (bf16[320,4096]{1,0:T(8,128)(2,1)}, bf16[320,4096]{1,0:T(8,128)(2,1)}, u32[]{:S(2)}, u32[]{:S(2)}) collective-permute-start(bf16[320,4096]{1,0:T(8,128)(2,1)} %slice.97), channel_id=1, source_target_pairs={{0,32},{16,48},{32,0},{48,16},{1,33},{17,49},{33,1},{49,17},{2,34}... | collective-permute-start | bytes 7864328 | tf_op jit(solution)/shard_map/ppermute | solution.py:274
  221.5 134.6 %collective-permute-start.15 = (bf16[64,4096]{1,0:T(8,128)(2,1)}, bf16[64,4096]{1,0:T(8,128)(2,1)S(1)}, u32[]{:S(2)}, u32[]{:S(2)}) collective-permute-start(bf16[64,4096]{1,0:T(8,128)(2,1)} %slice.96), channel_id=1, source_target_pairs={{0,32},{16,48},{32,0},{48,16},{1,33},{17,49},{33,1},{49,17},{2,34}... | collective-permute-start | bytes 1572872 | tf_op jit(solution)/shard_map/ppermute | solution.py:275
  258.6 32.4 %copy-start.4 = (bf16[1,192,4096]{2,1,0:T(8,128)(2,1)S(1)}, bf16[1,192,4096]{2,1,0:T(8,128)(2,1)}, u32[]{:S(2)}) copy-start(bf16[1,192,4096]{2,1,0:T(8,128)(2,1)} %param.10) | copy-start | bytes 4718596
  258.8 100.8 %collective-permute-start.12 = (bf16[32,2048]{1,0:T(8,128)(2,1)S(1)}, bf16[32,2048]{1,0:T(8,128)(2,1)S(1)}, u32[]{:S(2)}, u32[]{:S(2)}) collective-permute-start(bf16[32,2048]{1,0:T(8,128)(2,1)S(1)} %get-tuple-element.13), channel_id=1, source_target_pairs={{0,66},{2,64},{64,2},{66,0},{1,67},{3,65},{65,3},{67,1},{4,70},{6,... | collective-permute-start | bytes 393224 | tf_op jit(solution)/shard_map/ppermute | solution.py:163
  263.0 96.6 %collective-permute-start.13 = (bf16[32,2048]{1,0:T(8,128)(2,1)S(1)}, bf16[32,2048]{1,0:T(8,128)(2,1)S(1)}, u32[]{:S(2)}, u32[]{:S(2)}) collective-permute-start(bf16[32,2048]{1,0:T(8,128)(2,1)S(1)} %get-tuple-element.15), channel_id=1, source_target_pairs={{0,128},{128,0},{1,129},{129,1},{2,130},{130,2},{3,131},{131,3},{4... | collective-permute-start | bytes 393224 | tf_op jit(solution)/shard_map/ppermute | solution.py:163
  288.8 70.8 %collective-permute-start.14 = (bf16[32,2048]{1,0:T(8,128)(2,1)S(1)}, bf16[32,2048]{1,0:T(8,128)(2,1)S(1)}, u32[]{:S(2)}, u32[]{:S(2)}) collective-permute-start(bf16[32,2048]{1,0:T(8,128)(2,1)S(1)} %get-tuple-element.14), channel_id=1, source_target_pairs={{0,194},{2,192},{64,130},{66,128},{128,66},{130,64},{192,2},{194,0... | collective-permute-start | bytes 393224 | tf_op jit(solution)/shard_map/ppermute | solution.py:163
  356.1 0.8 copy-start.6

commit v8 on v7

--- a/solution.py
+++ b/solution.py
@@ -1,5 +1,3 @@
-import functools
-
 import jax
 import jax.numpy as jnp
 from jax import lax
@@ -11,22 +9,15 @@
 F32 = jnp.float32
 BF16 = jnp.bfloat16
 CAP = 3
-CHUNK = 1024
 META = 128
 HEAD = 320
 PLANE = ("x", "y", "c")
 CROSS = ("ql", "h")
 
 
-def project(x, table, at):
-    width = x.shape[1]
+def project(x, table):
     return [
-        lax.dot_general(
-            x[...],
-            table[0, k, :, at : at + width],
-            (((1,), (1,)), ((), ())),
-            preferred_element_type=F32,
-        )
+        lax.dot_general(x, table[0, k], (((1,), (1,)), ((), ())), preferred_element_type=F32)
         for k in range(2)
     ]
 
@@ -35,18 +26,12 @@
     return (gate / (1.0 + jnp.exp(-gate)) * upper).astype(BF16)
 
 
-def up_kernel(at, x_far, x_late, table, hid, x, sem):
-    fetch = pltpu.make_async_copy(x_far, x, sem)
-    fetch.start()
+def up_kernel(x, table, hid):
     tile = hid.shape[0]
-    sides = []
-    for m in range(x.shape[0] // tile):
-        rows = pl.ds(m * tile, tile)
-        two = project(x_late.at[rows], table, 0)
-        if m == 0:
-            fetch.wait()
-        one = project(x.at[rows], table, at)
-        sides.append(activate(one[0] + two[0], one[1] + two[1]))
+    sides = [
+        activate(*project(x[m * tile : (m + 1) * tile], table))
+        for m in range(x.shape[0] // tile)
+    ]
     hid[...] = jnp.concatenate(sides, axis=1)
 
 
@@ -55,22 +40,21 @@
 ROOM = pltpu.CompilerParams(vmem_limit_bytes=20 * 2**20)
 
 
-def up(x, x_late, table, at):
+def up(x, table):
     rows, units = x.shape[0], table.shape[2]
     depth = table.shape[3]
     return pl.pallas_call(
-        functools.partial(up_kernel, at),
-        in_specs=[FAR, RESIDENT, RESIDENT],
+        up_kernel,
+        in_specs=[RESIDENT] * 2,
         out_specs=RESIDENT,
         out_shape=jax.ShapeDtypeStruct((rows // 2, 2 * units), BF16),
-        scratch_shapes=[pltpu.VMEM(x.shape, BF16), pltpu.SemaphoreType.DMA],
         compiler_params=ROOM,
         cost_estimate=pl.CostEstimate(
             flops=4 * rows * units * depth,
             bytes_accessed=2 * rows * depth + 4 * units * depth,
             transcendentals=0,
         ),
-    )(x, x_late, table)
+    )(x, table)
 
 
 def down_kernel(*refs):
@@ -222,7 +206,6 @@
     steps, rows, depth = tokens.shape
     tops = expert_ids.shape[2]
     half = depth // 2
-    late = depth - CHUNK
     plane = lax.axis_index("h")
     q_high = lax.axis_index("qh")
     slot = (
@@ -238,7 +221,7 @@
     low = gates - high
     first = jnp.concatenate(
         [
-            flat[:, late:],
+            flat,
             expert_ids.reshape(own, tops).astype(BF16),
             high.astype(BF16),
             low.astype(BF16),
@@ -249,7 +232,6 @@
     across_x = [(i, i ^ 2) for i in range(4)]
     got_dn = lax.ppermute(down_proj, ("x",), across_x)
     held0 = column(first)
-    held1 = column(flat[:, :late])
     gu_b = swap(gate_up, ("ql",))
     mine = lax.dynamic_slice_in_dim(down_proj[0], q_high * half, half, axis=1)
     theirs = lax.dynamic_slice_in_dim(down_proj[0], (1 - q_high) * half, half, axis=1)
@@ -259,15 +241,13 @@
     pieces = [mine, near_piece, far_piece, across_piece]
 
     pick, mix = tables(
-        held0[:, CHUNK:].astype(F32), rows, tops, plane, q_high, experts, slots
-    )
-    packed0 = pack(pick, held0[:, :CHUNK])
+        held0[:, depth:].astype(F32), rows, tops, plane, q_high, experts, slots
+    )
+    packed0 = pack(pick, held0[:, :depth])
     x0 = across(packed0, experts)
-    packed1 = pack(pick, held1)
-    x1 = across(packed1, experts)
-    hidden_a = up(x0, x1, gate_up, late)
+    hidden_a = up(x0, gate_up)
     got_a = swap(hidden_a, ("qh",))
-    hidden_b = up(x0, x1, gu_b, late)
+    hidden_b = up(x0, gu_b)
     got_b = swap(hidden_b, ("qh",))
     table = gate_up.reshape(-1, depth)
     top, rest = table[:HEAD], table[HEAD:]

time: 366 us -> 356 us (0.973)
  starting transfers between devices: 62.2 us -> 47.2 us
  waiting for transfers between devices: 241 us -> 250 us
    all_to_all x3 -> x2, waiting for transfers between devices: 78.7 us -> 98.1 us  [across(): lax.all_to_all(value.reshape(experts, slots // experts, depth), PLANE, 0,...]
    all_to_all x3 -> x2, starting transfers between devices: 28.9 us -> 15.5 us  [across(): lax.all_to_all(value.reshape(experts, slots // experts, depth), PLANE, 0,...]
    ppermute x15 -> x12, waiting for transfers between devices: 79.5 us -> 73.7 us  [swap(): return lax.ppermute(value, axes, [(i, i ^ count - 1) for i in range(count)])]
    ppermute x15 -> x12, starting transfers between devices: 27.4 us -> 25.8 us  [swap(): return lax.ppermute(value, axes, [(i, i ^ count - 1) for i in range(count)])]
  transfers between devices with their start and end apart: 21 -> 17, of which waited for: 15 -> 12; matrix products, arithmetic and copies ran while one was open for 5% -> 4% of each run, Pallas kernels for 6% -> 6%
where the time goes in v8:
time: 356 us; the launch traced here: 351 us
  waiting for transfers between devices  250 us (70%)
  starting transfers between devices  47.2 us (13%)
  Pallas kernels  27.8 us (8%)
  local copies, waits for them, and re-layouts  11.1 us (3%)
  matrix products  7.9 us (2%)
  other arithmetic  6.56 us (2%)
    all_to_all x2, waiting for transfers between devices, across(): lax.all_to_all(value.reshape(experts, slots // experts, depth), PLANE, 0,...  98.1 us
    ppermute x12, waiting for transfers between devices, swap(): return lax.ppermute(value, axes, [(i, i ^ count - 1) for i in range(count)])  73.7 us
    ppermute x1, waiting for transfers between devices, local(): got_gu0 = lax.ppermute(top, ('x',), across_x)  49.1 us
    ppermute x12, starting transfers between devices, swap(): return lax.ppermute(value, axes, [(i, i ^ count - 1) for i in range(count)])  25.8 us
    ppermute x1, waiting for transfers between devices, local(): got_dn = lax.ppermute(down_proj, ('x',), across_x)  23.7 us
    all_to_all x2, starting transfers between devices, across(): lax.all_to_all(value.reshape(experts, slots // experts, depth), PLANE, 0,...  15.5 us
    pallas_call x2, Pallas kernels, up(): pl.pallas_call(up_kernel, in_specs=[RESIDENT] * 2, out_specs=RESIDENT, ou...  13.5 us
    pallas_call x2, Pallas kernels, put(): pl.pallas_call(put_kernel, grid_spec=pltpu.PrefetchScalarGridSpec(num_sca...  8.75 us
  transfers between devices with their start and end apart: 17, of which 12 were waited for; matrix products, arithmetic and copies ran while one was open for 4% of the time, Pallas kernels for 6%

profile of v8, /device:TPU:65, one launch (start us, length us, event | category | flops | bytes accessed | tf_op | source)
XLA Modules:
  0.0 351.1 jit_solution(7305800385519235027)
XLA Ops:
  3.4 4.7 %collective-permute-start = (bf16[32,4224]{1,0:T(8,128)(2,1)S(1)}, bf16[32,4224]{1,0:T(8,128)(2,1)S(1)}, u32[]{:S(2)}, u32[]{:S(2)}) collective-permute-start(bf16[32,4224]{1,0:T(8,128)(2,1)S(1)} %concatenate.22), channel_id=1, source_target_pairs={{0,66},{2,64},{64,2},{66,0},{1,67},{3,65},{65,3},{67,1},{4,70},{6,... | collective-permute-start | bytes 811016 | tf_op jit(solution)/shard_map/ppermute | solution.py:147
  9.6 15.2 %collective-permute-done = bf16[32,4224]{1,0:T(8,128)(2,1)S(1)} collective-permute-done((bf16[32,4224]{1,0:T(8,128)(2,1)S(1)}, bf16[32,4224]{1,0:T(8,128)(2,1)S(1)}, u32[]{:S(2)}, u32[]{:S(2)}) %collective-permute-start) | collective-permute-done | bytes 270368 | tf_op jit(solution)/shard_map/ppermute | solution.py:147
  24.8 6.2 %collective-permute-done.1 = bf16[32,4224]{1,0:T(8,128)(2,1)S(1)} collective-permute-done((bf16[32,4224]{1,0:T(8,128)(2,1)S(1)}, bf16[32,4224]{1,0:T(8,128)(2,1)S(1)}, u32[]{:S(2)}, u32[]{:S(2)}) %collective-permute-start.1) | collective-permute-done | bytes 270368 | tf_op jit(solution)/shard_map/ppermute | solution.py:147
  33.3 4.4 %convolution_convert_fusion = bf16[768,4096]{1,0:T(8,128)(2,1)} fusion(pred[128,768]{1,0:T(32,128)(4,1)S(1)} %get-tuple-element.8, bf16[32,4224]{1,0:T(8,128)(2,1)S(1)} %collective-permute-done.2, bf16[32,4224]{1,0:T(8,128)(2,1)S(1)} %collective-permute-done.1, bf16[32,4224]{1,0:T(8,128)(2,1)S(1)} %collective-permute-done, bf16[32,4224]{1,0:T(8,128)(2,1)S(1)} %concatenate.22), kind=kOutput, calls=%fused_computation | convolution fusion | flops 812646400 | bytes 7471104 | tf_op jit(solution)/shard_map/dot_general | solution.py:193
  37.8 7.9 %all-to-all-start = ((bf16[32,24,4096]{2,1,0:T(8,128)(2,1)}), bf16[32,24,4096]{2,1,0:T(8,128)(2,1)}, u32[]{:S(2)}, u32[]{:S(2)}) async-start(bf16[32,24,4096]{2,1,0:T(8,128)(2,1)} %bitcast.25), calls=%async_computation | async-start | bytes 12582912 | tf_op jit(solution)/shard_map/all_to_all | solution.py:200
  45.7 2.8 collective-permute-start.3
  48.5 2.7 dynamic-slice_bitcast_fusion
  51.2 1.8 collective-permute-start.7
  53.9 69.1 %all-to-all-done = bf16[32,24,4096]{2,1,0:T(8,128)(2,1)} async-done(((bf16[32,24,4096]{2,1,0:T(8,128)(2,1)}), bf16[32,24,4096]{2,1,0:T(8,128)(2,1)}, u32[]{:S(2)}, u32[]{:S(2)}) %all-to-all-start) | async-done | bytes 6291488 | tf_op jit(solution)/shard_map/all_to_all | solution.py:200
  123.0 6.3 %shard_map.85.refs_0_ = bf16[384,384]{1,0:T(8,128)(2,1)S(1)} custom-call(bf16[768,4096]{1,0:T(8,128)(2,1)} %bitcast.3.x, bf16[1,2,192,4096]{3,2,1,0:T(8,128)(2,1)S(1)} %copy-done), custom_call_target="tpu_custom_call" | custom-call | flops 2415919104 | bytes 9437184 | tf_op jit(solution)/shard_map/pallas_call | solution.py:46
  129.3 3.2 collective-permute-done.3.table
  132.5 7.2 %shard_map.86.refs_1_ = bf16[384,384]{1,0:T(8,128)(2,1)S(1)} custom-call(bf16[768,4096]{1,0:T(8,128)(2,1)} %bitcast.3.x, bf16[1,2,192,4096]{3,2,1,0:T(8,128)(2,1)} %collective-permute-done.3.table), custom_call_target="tpu_custom_call" | custom-call | flops 2415919104 | bytes 9437184 | tf_op jit(solution)/shard_map/pallas_call | solution.py:46
  139.8 3.0 collective-permute-start.5
  142.8 6.8 %collective-permute-done.6.refs_5_ = bf16[192,2048]{1,0:T(8,128)(2,1)} collective-permute-done((bf16[192,2048]{1,0:T(8,128)(2,1)}, bf16[192,2048]{1,0:T(8,128)(2,1)}, u32[]{:S(2)}, u32[]{:S(2)}) %collective-permute-start.6) | collective-permute-done | bytes 786464 | tf_op jit(solution)/shard_map/ppermute | solution.py:147
  151.0 34.6 %collective-permute-done.5.refs_3_ = bf16[384,384]{1,0:T(8,128)(2,1)S(1)} collective-permute-done((bf16[384,384]{1,0:T(8,128)(2,1)S(1)}, bf16[384,384]{1,0:T(8,128)(2,1)S(1)}, u32[]{:S(2)}, u32[]{:S(2)}) %collective-permute-start.5) | collective-permute-done | bytes 294944 | tf_op jit(solution)/shard_map/ppermute | solution.py:147
  185.6 6.3 %collective-permute-done.4.refs_2_ = bf16[384,384]{1,0:T(8,128)(2,1)S(1)} collective-permute-done((bf16[384,384]{1,0:T(8,128)(2,1)S(1)}, bf16[384,384]{1,0:T(8,128)(2,1)S(1)}, u32[]{:S(2)}, u32[]{:S(2)}) %collective-permute-start.4) | collective-permute-done | bytes 294944 | tf_op jit(solution)/shard_map/ppermute | solution.py:147
  191.9 5.5 %down.1 = bf16[768,2048]{1,0:T(8,128)(2,1)S(1)} custom-call(bf16[384,384]{1,0:T(8,128)(2,1)S(1)} %shard_map.85.refs_0_, bf16[384,384]{1,0:T(8,128)(2,1)S(1)} %shard_map.86.refs_1_, bf16[384,384]{1,0:T(8,128)(2,1)S(1)} %collective-permute-done.4.refs_2_, bf16[384,384]{1,0:T(8,128)(2,1)S(1)} %collective-permute-done.5.refs_3_, ...), custom_call_target="tpu_custom_call" | custom-call | flops 2415919104 | bytes 7471104 | tf_op jit(solution)/shard_map/down/pallas_call | solution.py:85
  199.1 7.5 %all-to-all-start.1 = ((bf16[32,24,2048]{2,1,0:T(8,128)(2,1)}), bf16[32,24,2048]{2,1,0:T(8,128)(2,1)}, u32[]{:S(2)}, u32[]{:S(2)}) async-start(bf16[32,24,2048]{2,1,0:T(8,128)(2,1)} %bitcast.24), calls=%async_computation.1 | async-start | bytes 6291456 | tf_op jit(solution)/shard_map/all_to_all | solution.py:200
  206.6 3.0 collective-permute-start.14
  209.6 1.7 slice.87
  212.2 2.9 collective-permute-start.12
  217.5 28.9 %all-to-all-done.1 = bf16[32,24,2048]{2,1,0:T(8,128)(2,1)} async-done(((bf16[32,24,2048]{2,1,0:T(8,128)(2,1)}), bf16[32,24,2048]{2,1,0:T(8,128)(2,1)}, u32[]{:S(2)}, u32[]{:S(2)}) %all-to-all-start.1) | async-done | bytes 3145760 | tf_op jit(solution)/shard_map/all_to_all | solution.py:200
  246.4 2.9 fusion.12
  249.5 3.2 collective-permute-start.10
  252.7 3.1 collective-permute-start.11
  255.8 23.7 %collective-permute-done.14 = bf16[1,192,4096]{2,1,0:T(8,128)(2,1)} collective-permute-done((bf16[1,192,4096]{2,1,0:T(8,128)(2,1)}, bf16[1,192,4096]{2,1,0:T(8,128)(2,1)}, u32[]{:S(2)}, u32[]{:S(2)}) %collective-permute-start.14) | collective-permute-done | bytes 1572896 | tf_op jit(solution)/shard_map/ppermute | solution.py:233
  279.5 5.0 %collective-permute-start.9 = (bf16[32,2048]{1,0:T(8,128)(2,1)S(1)}, bf16[32,2048]{1,0:T(8,128)(2,1)S(1)}, u32[]{:S(2)}, u32[]{:S(2)}) collective-permute-start(bf16[32,2048]{1,0:T(8,128)(2,1)S(1)} %get-tuple-element.13), channel_id=1, source_target_pairs={{0,66},{2,64},{64,2},{66,0},{1,67},{3,65},{65,3},{67,1},{4,70},{6,... | collective-permute-start | bytes 393224 | tf_op jit(solution)/shard_map/ppermute | solution.py:147
  284.5 2.0 broadcast_select_fusion
  286.5 49.1 %collective-permute-done.13.got = bf16[320,4096]{1,0:T(8,128)(2,1)} collective-permute-done((bf16[320,4096]{1,0:T(8,128)(2,1)}, bf16[320,4096]{1,0:T(8,128)(2,1)}, u32[]{:S(2)}, u32[]{:S(2)}) %collective-permute-start.13) | collective-permute-done | bytes 2621472 | tf_op jit(solution)/shard_map/ppermute | solution.py:254
  335.7 6.1 %put.2.refs_0_ = bf16[384,4096]{1,0:T(8,128)(2,1)} custom-call(s32[1]{0:T(128)} %bitcast.10.moving, bf16[320,4096]{1,0:T(8,128)(2,1)} %collective-permute-done.13.got, bf16[384,4096]{1,0:T(8,128)(2,1)} %bitcast.20), custom_call_target="tpu_custom_call" | custom-call | bytes 7864320 | tf_op jit(solution)/shard_map/put/pallas_call | solution.py:128
  341.8 5.1 %collective-permute-done.12.got = bf16[64,4096]{1,0:T(8,128)(2,1)S(1)} collective-permute-done((bf16[64,4096]{1,0:T(8,128)(2,1)}, bf16[64,4096]{1,0:T(8,128)(2,1)S(1)}, u32[]{:S(2)}, u32[]{:S(2)}) %collective-permute-start.12) | collective-permute-done | bytes 524320 | tf_op jit(solution)/shard_map/ppermute | solution.py:255
  347.6 2.7 put.3
  (58 shorter events, 15.5 us)
Async XLA Ops:
  3.4 21.4 %collective-permute-start = (bf16[32,4224]{1,0:T(8,128)(2,1)S(1)}, bf16[32,4224]{1,0:T(8,128)(2,1)S(1)}, u32[]{:S(2)}, u32[]{:S(2)}) collective-permute-start(bf16[32,4224]{1,0:T(8,128)(2,1)S(1)} %concatenate.22), channel_id=1, source_target_pairs={{0,66},{2,64},{64,2},{66,0},{1,67},{3,65},{65,3},{67,1},{4,70},{6,... | collective-permute-start | bytes 811016 | tf_op jit(solution)/shard_map/ppermute | solution.py:147
  8.2 22.8 %collective-permute-start.1 = (bf16[32,4224]{1,0:T(8,128)(2,1)S(1)}, bf16[32,4224]{1,0:T(8,128)(2,1)S(1)}, u32[]{:S(2)}, u32[]{:S(2)}) collective-permute-start(bf16[32,4224]{1,0:T(8,128)(2,1)S(1)} %concatenate.22), channel_id=1, source_target_pairs={{0,128},{128,0},{1,129},{129,1},{2,130},{130,2},{3,131},{131,3},{4... | collective-permute-start | bytes 811016 | tf_op jit(solution)/shard_map/ppermute | solution.py:147
  9.4 21.6 %collective-permute-start.2 = (bf16[32,4224]{1,0:T(8,128)(2,1)S(1)}, bf16[32,4224]{1,0:T(8,128)(2,1)S(1)}, u32[]{:S(2)}, u32[]{:S(2)}) collective-permute-start(bf16[32,4224]{1,0:T(8,128)(2,1)S(1)} %concatenate.22), channel_id=1, source_target_pairs={{0,194},{2,192},{64,130},{66,128},{128,66},{130,64},{192,2},{194,0... | collective-permute-start | bytes 811016 | tf_op jit(solution)/shard_map/ppermute | solution.py:147
  32.1 1.0 copy-start.3
  37.8 8.0 %copy-start = (bf16[1,2,192,4096]{3,2,1,0:T(8,128)(2,1)S(1)}, bf16[1,2,192,4096]{3,2,1,0:T(8,128)(2,1)}, u32[]{:S(2)}) copy-start(bf16[1,2,192,4096]{3,2,1,0:T(8,128)(2,1)} %table.1) | copy-start | bytes 9437188
  37.8 85.3 %all-to-all-start = ((bf16[32,24,4096]{2,1,0:T(8,128)(2,1)}), bf16[32,24,4096]{2,1,0:T(8,128)(2,1)}, u32[]{:S(2)}, u32[]{:S(2)}) async-start(bf16[32,24,4096]{2,1,0:T(8,128)(2,1)} %bitcast.25), calls=%async_computation | async-start | bytes 12582912 | tf_op jit(solution)/shard_map/all_to_all | solution.py:200
  45.7 86.8 %collective-permute-start.3 = (bf16[1,2,192,4096]{3,2,1,0:T(8,128)(2,1)S(1)}, bf16[1,2,192,4096]{3,2,1,0:T(8,128)(2,1)}, u32[]{:S(2)}, u32[]{:S(2)}) collective-permute-start(bf16[1,2,192,4096]{3,2,1,0:T(8,128)(2,1)S(1)} %copy-done), channel_id=1, source_target_pairs={{0,64},{64,0},{1,65},{65,1},{2,66},{66,2},{3,67},{67,3},{4,68},{68... | collective-permute-start | bytes 9437192 | tf_op jit(solution)/shard_map/ppermute | solution.py:147
  51.2 98.4 %collective-permute-start.6 = (bf16[192,2048]{1,0:T(8,128)(2,1)}, bf16[192,2048]{1,0:T(8,128)(2,1)}, u32[]{:S(2)}, u32[]{:S(2)}) collective-permute-start(bf16[192,2048]{1,0:T(8,128)(2,1)} %get-tuple-element.10.refs_4_), channel_id=1, source_target_pairs={{0,64},{64,0},{1,65},{65,1},{2,66},{66,2},{3,67},{67,3},{4,68},{68... | collective-permute-start | bytes 2359304 | tf_op jit(solution)/shard_map/ppermute | solution.py:147
  51.2 99.7 %collective-permute-start.7 = (bf16[192,2048]{1,0:T(8,128)(2,1)}, bf16[192,2048]{1,0:T(8,128)(2,1)}, u32[]{:S(2)}, u32[]{:S(2)}) collective-permute-start(bf16[192,2048]{1,0:T(8,128)(2,1)} %get-tuple-element.9), channel_id=1, source_target_pairs={{0,128},{128,0},{1,129},{129,1},{2,130},{130,2},{3,131},{131,3},{4... | collective-permute-start | bytes 2359304 | tf_op jit(solution)/shard_map/ppermute | solution.py:147
  53.1 97.9 %collective-permute-start.8 = (bf16[192,2048]{1,0:T(8,128)(2,1)}, bf16[192,2048]{1,0:T(8,128)(2,1)}, u32[]{:S(2)}, u32[]{:S(2)}) collective-permute-start(bf16[192,2048]{1,0:T(8,128)(2,1)} %get-tuple-element.9), channel_id=1, source_target_pairs={{0,192},{64,128},{128,64},{192,0},{1,193},{65,129},{129,65},{193,1... | collective-permute-start | bytes 2359304 | tf_op jit(solution)/shard_map/ppermute | solution.py:147
  139.8 45.8 %collective-permute-start.5 = (bf16[384,384]{1,0:T(8,128)(2,1)S(1)}, bf16[384,384]{1,0:T(8,128)(2,1)S(1)}, u32[]{:S(2)}, u32[]{:S(2)}) collective-permute-start(bf16[384,384]{1,0:T(8,128)(2,1)S(1)} %shard_map.86.refs_1_), channel_id=1, source_target_pairs={{0,128},{128,0},{1,129},{129,1},{2,130},{130,2},{3,131},{131,3},{4... | collective-permute-start | bytes 884744 | tf_op jit(solution)/shard_map/ppermute | solution.py:147
  142.7 49.2 %collective-permute-start.4 = (bf16[384,384]{1,0:T(8,128)(2,1)S(1)}, bf16[384,384]{1,0:T(8,128)(2,1)S(1)}, u32[]{:S(2)}, u32[]{:S(2)}) collective-permute-start(bf16[384,384]{1,0:T(8,128)(2,1)S(1)} %shard_map.85.refs_0_), channel_id=1, source_target_pairs={{0,128},{128,0},{1,129},{129,1},{2,130},{130,2},{3,131},{131,3},{4... | collective-permute-start | bytes 884744 | tf_op jit(solution)/shard_map/ppermute | solution.py:147
  197.4 1.7 copy-start.1
  199.1 47.3 %all-to-all-start.1 = ((bf16[32,24,2048]{2,1,0:T(8,128)(2,1)}), bf16[32,24,2048]{2,1,0:T(8,128)(2,1)}, u32[]{:S(2)}, u32[]{:S(2)}) async-start(bf16[32,24,2048]{2,1,0:T(8,128)(2,1)} %bitcast.24), calls=%async_computation.1 | async-start | bytes 6291456 | tf_op jit(solution)/shard_map/all_to_all | solution.py:200
  206.6 72.9 %collective-permute-start.14 = (bf16[1,192,4096]{2,1,0:T(8,128)(2,1)}, bf16[1,192,4096]{2,1,0:T(8,128)(2,1)}, u32[]{:S(2)}, u32[]{:S(2)}) collective-permute-start(bf16[1,192,4096]{2,1,0:T(8,128)(2,1)} %param.10), channel_id=1, source_target_pairs={{0,32},{16,48},{32,0},{48,16},{1,33},{17,49},{33,1},{49,17},{2,34}... | collective-permute-start | bytes 4718600 | tf_op jit(solution)/shard_map/ppermute | solution.py:233
  209.6 5.5 %copy-start.5 = (s32[8,2]{0,1:T(2,128)S(1)}, s32[8,2]{0,1:T(2,128)}, u32[]{:S(2)}) copy-start(s32[8,2]{0,1:T(2,128)} %param.11) | copy-start | bytes 196
  211.3 124.4 %collective-permute-start.13 = (bf16[320,4096]{1,0:T(8,128)(2,1)}, bf16[320,4096]{1,0:T(8,128)(2,1)}, u32[]{:S(2)}, u32[]{:S(2)}) collective-permute-start(bf16[320,4096]{1,0:T(8,128)(2,1)} %slice.87), channel_id=1, source_target_pairs={{0,32},{16,48},{32,0},{48,16},{1,33},{17,49},{33,1},{49,17},{2,34}... | collective-permute-start | bytes 7864328 | tf_op jit(solution)/shard_map/ppermute | solution.py:254
  212.2 134.6 %collective-permute-start.12 = (bf16[64,4096]{1,0:T(8,128)(2,1)}, bf16[64,4096]{1,0:T(8,128)(2,1)S(1)}, u32[]{:S(2)}, u32[]{:S(2)}) collective-permute-start(bf16[64,4096]{1,0:T(8,128)(2,1)} %slice.86), channel_id=1, source_target_pairs={{0,32},{16,48},{32,0},{48,16},{1,33},{17,49},{33,1},{49,17},{2,34}... | collective-permute-start | bytes 1572872 | tf_op jit(solution)/shard_map/ppermute | solution.py:255
  249.3 35.2 %copy-start.2 = (bf16[1,192,4096]{2,1,0:T(8,128)(2,1)S(1)}, bf16[1,192,4096]{2,1,0:T(8,128)(2,1)}, u32[]{:S(2)}) copy-start(bf16[1,192,4096]{2,1,0:T(8,128)(2,1)} %param.10) | copy-start | bytes 4718596
  249.5 100.8 %collective-permute-start.10 = (bf16[32,2048]{1,0:T(8,128)(2,1)S(1)}, bf16[32,2048]{1,0:T(8,128)(2,1)S(1)}, u32[]{:S(2)}, u32[]{:S(2)}) collective-permute-start(bf16[32,2048]{1,0:T(8,128)(2,1)S(1)} %get-tuple-element.15), channel_id=1, source_target_pairs={{0,128},{128,0},{1,129},{129,1},{2,130},{130,2},{3,131},{131,3},{4... | collective-permute-start | bytes 393224 | tf_op jit(solution)/shard_map/ppermute | solution.py:147
  252.7 97.6 %collective-permute-start.11 = (bf16[32,2048]{1,0:T(8,128)(2,1)S(1)}, bf16[32,2048]{1,0:T(8,128)(2,1)S(1)}, u32[]{:S(2)}, u32[]{:S(2)}) collective-permute-start(bf16[32,2048]{1,0:T(8,128)(2,1)S(1)} %get-tuple-element.14), channel_id=1, source_target_pairs={{0,194},{2,192},{64,130},{66,128},{128,66},{130,64},{192,2},{194,0... | collective-permute-start | bytes 393224 | tf_op jit(solution)/shard_map/ppermute | solution.py:147
  279.5 70.8 %collective-permute-start.9 = (bf16[32,2048]{1,0:T(8,128)(2,1)S(1)}, bf16[32,2048]{1,0:T(8,128)(2,1)S(1)}, u32[]{:S(2)}, u32[]{:S(2)}) collective-permute-start(bf16[32,2048]{1,0:T(8,128)(2,1)S(1)} %get-tuple-element.13), channel_id=1, source_target_pairs={{0,66},{2,64},{64,2},{66,0},{1,67},{3,65},{65,3},{67,1},{4,70},{6,... | collective-permute-start | bytes 393224 | tf_op jit(solution)/shard_map/ppermute | solution.py:147
  346.8 0.8 copy-start.4
